TPU v7x, 256 devices: a whole 4x4x8 slice. The times are simulated.
256 devices in a mesh: ab: 16 (over y, x), cd: 8 (over z), ij: 2 (over core).
Axes of the slice: x: 4, y: 4, z: 8, core: 2. Of those that a mesh axis runs over, the one named last changes fastest.
Arguments:
- amplitudes: float32 [512, 65536], P('ij', ('cd', 'ab')), may hold values from -6 to 6
- integrals: float32 [5888, 256, 256], P(('ab', 'cd')), may hold values from -0.375 to 0.375
- tile_row: int32 [5888], P(('ab', 'cd')), may hold values from 0 to 15, as said below
- tile_col: int32 [5888], P(('ab', 'cd')), may hold values from 0 to 31
- tile_count: int32 [128], P(('ab', 'cd')), may hold values from 1 to 46, as said below
Outputs:
- residual: float32 [512, 16, 16, 256], P('ij', 'ab', 'cd')
Inputs may be any that keep to these rules, and one draw needn't show every extreme that they name: Within one slab the 46 slots name distinct (tile_row, tile_col) pairs. `tile_count`: in every draw some slab has all 46 slots live.
All inputs are finite; a program needn't handle non-finite values.
Results may differ from a plain program's by a relative error of at most 0.0003.
Values sent between devices are 32-bit elements; how exact they have to be, the bound alone decides.
No kernel may reach another device: no remote copies, remote signals or barrier semaphores. Data moves between devices by JAX's collectives and lax.ppermute only.
A program may use at most 128 MiB of HBM per device.

v0:
```python
import math

import jax
import jax.numpy as jnp
from jax import lax
from jax.sharding import PartitionSpec as P


def from_partner(block, axis, bit):
    count = lax.axis_size(axis)
    route = []
    for low in range(count):
        high = low | 1 << bit
        if high != low and high < count:
            route += [(low, high), (high, low)]
    return lax.ppermute(block, axis, route)


def place_rows(chosen, tile_rows, row_picks, block_size):
    terms = jnp.einsum("okf,kef->oke", chosen, tile_rows, precision=lax.Precision.HIGHEST)
    occ_dev, slots, width = terms.shape
    terms = terms.reshape(occ_dev, slots, width // block_size, block_size)
    placed = jnp.einsum("rk,okab->aorb", row_picks, terms, precision=lax.Precision.HIGHEST)
    return placed.reshape(width // block_size, occ_dev, row_picks.shape[0] * block_size)


def per_device(amplitudes, integrals, tile_row, tile_col, tile_count):
    occ_dev = amplitudes.shape[0]
    slots = integrals.shape[0]
    tile_size = integrals.shape[1]
    block_size = math.isqrt(tile_size)
    blocks = lax.axis_size("ab")
    cd_size = lax.axis_size("cd")
    group_size = block_size // cd_size
    live_count = tile_count[0]
    live = jnp.arange(slots, dtype=jnp.int32) < live_count
    row_picks = (
        (tile_row[None, :] == jnp.arange(blocks, dtype=jnp.int32)[:, None]) & live[None, :]
    ).astype(jnp.float32)
    gathered = lax.all_gather(amplitudes, "ab", axis=1, tiled=True)
    columns = gathered.reshape(occ_dev, -1, tile_size)
    chosen = jnp.take(columns, tile_col, axis=1)
    partial_value = place_rows(chosen, integrals, row_picks, block_size)
    summed = lax.psum_scatter(partial_value, "cd", scatter_dimension=0, tiled=True)
    direct = jnp.transpose(summed, (1, 0, 2))
    outgoing = summed.reshape(group_size, occ_dev, blocks, cd_size, group_size)
    outgoing = jnp.transpose(outgoing, (2, 3, 1, 0, 4))
    arrived = lax.all_to_all(
        outgoing.reshape(blocks * cd_size, occ_dev * group_size * group_size),
        ("ab", "cd"),
        split_axis=0,
        concat_axis=0,
        tiled=True,
    )
    arrived = arrived.reshape(blocks, cd_size, occ_dev, group_size, group_size)
    mirrored = jnp.transpose(arrived, (2, 4, 0, 1, 3)).reshape(
        occ_dev, group_size, blocks * block_size
    )
    partner = from_partner(mirrored, "ij", 0)
    return (direct + partner).reshape(occ_dev, 1, group_size, blocks * block_size)


def solution(mesh):
    in_specs = (
        P("ij", ("cd", "ab")),
        P(("ab", "cd"), None, None),
        P(("ab", "cd")),
        P(("ab", "cd")),
        P(("ab", "cd")),
    )
    out_specs = P("ij", "ab", "cd", None)
    return jax.shard_map(
        per_device, mesh=mesh, in_specs=in_specs, out_specs=out_specs, check_vma=False
    )
```

profile of v0, /device:TPU:1, one launch (start us, length us, event | category | flops | bytes accessed | tf_op | source)
XLA Modules:
  0.0 277.0 jit_solution(6151117193735669548)
XLA Ops:
  6.5 0.0 all-gather.2.cloned.1.call-start
  6.5 2.0 copy.23
  8.6 0.0 all-gather.2.cloned.1.call-update
  8.6 0.0 reduce-scatter.2.cloned.1.call-start
  9.3 0.7 compare_select_fusion
  10.0 0.7 compare_and_fusion
  10.6 78.7 %all-gather.2.cloned.1.call-done = f32[256,8192]{0,1:T(8,128)} async-done(((f32[256,512]{0,1:T(8,128)}), f32[256,8192]{0,1:T(8,128)}) %all-gather.2.cloned.1.call-update) | async-done | bytes 8388624 | tf_op jit(solution)/shard_map/all_gather | solution.py:40
  89.4 9.0 %copy.24 = f32[256,32,256]{2,0,1:T(8,128)} copy(f32[256,32,256]{0,2,1:T(8,128)} %bitcast.38) | data formatting | bytes 16777216 | tf_op jit(solution)/shard_map/reshape | solution.py:41
  98.4 10.9 %gather_fusion = f32[46,256,256]{2,1,0:T(8,128)} fusion(f32[256,32,256]{2,0,1:T(8,128)} %copy.24, s32[1024]{0:T(1024)S(1)} %pad_clamp_fusion), kind=kCustom, calls=%fused_computation | custom fusion | bytes 24117432 | tf_op jit(solution)/shard_map/jit(_take)/gather | solution.py:42
  109.2 0.0 copy-start.1
  109.2 20.0 %fusion.2 = f32[46,256,256]{1,2,0:T(8,128)} fusion(f32[46,256,256]{2,1,0:T(8,128)} %param.6, f32[46,256,256]{2,1,0:T(8,128)} %gather_fusion, pred[46]{0:T(512)(128)(4,1)S(1)} %compare_and_fusion), kind=kOutput, calls=%fused_computation.3 | convolution fusion | flops 9264037888 | bytes 36175920 | tf_op jit(solution)/shard_map/okf,kef->oke/dot_general | solution.py:20
  129.3 0.0 copy-done.1
  129.3 16.3 %fusion.7 = f32[16,256,16,16]{1,2,3,0:T(8,128)S(1)} fusion(f32[256,46,16,16]{0,3,2,1:T(8,128)} %bitcast.35, s32[46]{0:T(128)S(1)} %copy-done.1, pred[46]{0:T(512)(128)(4,1)S(1)} %iota_compare_fusion.1), kind=kOutput, calls=%fused_computation.8 | convolution fusion | flops 578815424 | bytes 16253158 | tf_op jit(solution)/shard_map/rk,okab->aorb/dot_general | solution.py:23
  145.6 5.2 %copy.26 = f32[16,256,16,16]{1,3,2,0:T(8,128)} copy(f32[16,256,16,16]{1,2,3,0:T(8,128)S(1)} %fusion.7) | data formatting | bytes 8388608 | tf_op jit(solution)/shard_map/rk,okab->aorb/transpose | solution.py:23
  150.8 0.0 reduce-scatter.2.cloned.1.call-update
  150.8 55.3 %reduce-scatter.2.cloned.1.call-done = f32[2,256,256]{1,2,0:T(8,128)} async-done(((f32[16,256,256]{1,2,0:T(8,128)}), f32[2,256,256]{1,2,0:T(8,128)}) %reduce-scatter.2.cloned.1.call-update) | async-done | bytes 524304 | tf_op jit(solution)/shard_map/reduce_scatter | solution.py:44
  206.1 1.4 copy.27
  207.5 7.6 %copy.28 = f32[16,8,256,2,2]{1,0,4,3,2:T(8,128)} copy(f32[16,8,256,2,2]{2,3,4,1,0:T(2,128)S(1)} %bitcast.40) | data formatting | bytes 1048576 | tf_op jit(solution)/shard_map/transpose | solution.py:47
  215.1 6.4 %all_to_all.6 = f32[128,1,1024]{0,2,1:T(8,128)S(1)} reshape(f32[16,8,256,2,2]{1,0,4,3,2:T(8,128)} %copy.28) | data formatting | bytes 1048576 | tf_op jit(solution)/shard_map/all_to_all | solution.py:48
  221.5 0.0 copy-start
  221.5 0.4 copy.29
  222.0 30.1 %all_to_all.9 = f32[128,1,1024]{2,1,0:T(1,128)S(1)} all-to-all(f32[128,1,1024]{2,1,0:T(1,128)S(1)} %copy.29), channel_id=1, replica_groups=mesh['ab'=16,'cd'=8,'ij'=2] {'ab','cd'}, dimensions={0} | all-to-all | bytes 1048576 | tf_op jit(solution)/shard_map/all_to_all | solution.py:48
  252.0 0.4 copy.30
  252.4 6.1 %reshape.40 = f32[16,8,256,2,2]{1,0,4,3,2:T(8,128)} reshape(f32[128,1,1024]{0,2,1:T(8,128)S(1)} %copy.30) | data formatting | bytes 1048576 | tf_op jit(solution)/shard_map/reshape | solution.py:55
  258.6 6.3 %copy.31 = f32[256,2,16,8,2]{0,1,4,3,2:T(2,128)S(1)} copy(f32[256,2,16,8,2]{3,2,1,4,0:T(8,128)} %bitcast.36) | data formatting | bytes 1048576 | tf_op jit(solution)/shard_map/transpose | solution.py:56
  265.0 2.6 collective-permute-start
  267.6 1.5 collective-permute-done
  269.1 0.0 copy-done
  269.1 0.1 fusion.10
  269.2 1.0 copy.33
  (3 shorter events, 0.0 us)
Async XLA Ops:
  6.5 82.8 %all-gather.2.cloned.1.call-start = ((), (), s32[]{:S(2)}) async-start(), calls=%async_computation.2 | async-start | bytes 8912896 | tf_op jit(solution)/shard_map/all_gather | solution.py:40
  8.6 197.5 %reduce-scatter.2.cloned.1.call-start = ((), (), s32[]{:S(2)}) async-start(), calls=%async_computation.3 | async-start | bytes 4718592 | tf_op jit(solution)/shard_map/reduce_scatter | solution.py:44
  109.2 20.0 %copy-start.1 = (s32[46]{0:T(128)S(1)}, s32[46]{0:T(128)}, u32[]{:S(2)}) copy-start(s32[46]{0:T(128)} %param.7) | copy-start | bytes 556
  221.5 47.6 %copy-start = (f32[2,256,256]{1,2,0:T(8,128)S(1)}, f32[2,256,256]{1,2,0:T(8,128)}, u32[]{:S(2)}) copy-start(f32[2,256,256]{1,2,0:T(8,128)} %reduce-scatter.2.cloned.1.call-done) | copy-start | bytes 1572868
  265.0 4.2 %collective-permute-start = (f32[256,2,256]{0,2,1:T(8,128)S(1)}, f32[256,2,256]{0,2,1:T(8,128)S(1)}, u32[]{:S(2)}, u32[]{:S(2)}) collective-permute-start(f32[256,2,256]{0,2,1:T(8,128)S(1)} %copy.32), channel_id=1, source_target_pairs={{0,1},{1,0},{2,3},{3,2},{4,5},{5,4},{6,7},{7,6},{8,9},{9,8},{10,11... | collective-permute-start | bytes 1572872 | tf_op jit(solution)/shard_map/ppermute | solution.py:16
Sparse Core Ops, SparseCore 0:
  9.8 79.5 all-gather.1
  150.9 55.0 reduce-scatter.1
where the time goes:
time: 278 us; the launch traced here: 277 us
  waiting for transfers between devices  136 us (49%)
  local copies, waits for them, and re-layouts  56.8 us (20%)
  matrix products  36.3 us (13%)
  blocking collectives  30.1 us (11%)
  between operations  14.1 us (5%)
    all_gather x1, waiting for transfers between devices, per_device(): gathered = lax.all_gather(amplitudes, 'ab', axis=1, tiled=True)  78.7 us
    reduce_scatter x1, waiting for transfers between devices, per_device(): lax.psum_scatter(partial_value, 'cd', scatter_dimension=0, tiled=True)  55.3 us
    all_to_all x1, blocking collectives, per_device(): lax.all_to_all(outgoing.reshape(blocks * cd_size, occ_dev * group_size *...  30.1 us
    dot_general x1, matrix products, place_rows(): jnp.einsum('okf,kef->oke', chosen, tile_rows, precision=lax.Precision.HIG...  20 us
    dot_general x1, matrix products, place_rows(): jnp.einsum('rk,okab->aorb', row_picks, terms, precision=lax.Precision.HIG...  16.3 us
    gather x1, local copies, waits for them, and re-layouts, per_device(): chosen = jnp.take(columns, tile_col, axis=1)  10.9 us
    reshape x1, local copies, waits for them, and re-layouts, per_device(): columns = gathered.reshape(occ_dev, -1, tile_size)  8.97 us
    transpose x1, local copies, waits for them, and re-layouts, per_device(): outgoing = jnp.transpose(outgoing, (2, 3, 1, 0, 4))  7.61 us
  transfers between devices with their start and end apart: 3, of which 3 were waited for; matrix products, arithmetic and copies ran while one was open for 0% of the time, Pallas kernels for 0%

commit v1 on v0

v1 whole, which is shorter than its diff:
```python
import math

import jax
import jax.numpy as jnp
from jax import lax
from jax.experimental import pallas as pl
from jax.experimental.pallas import tpu as pltpu
from jax.sharding import PartitionSpec as P

LANES = 128
SIDE = 4


def plane_route(dx, dy):
    route = []
    for y in range(SIDE):
        for x in range(SIDE):
            route.append((y * SIDE + x, (y + dy) % SIDE * SIDE + (x + dx) % SIDE))
    return route


def shift_plane(block, dx, dy):
    return lax.ppermute(block, "ab", plane_route(dx, dy))


def both_ways(block, dx, dy):
    return [shift_plane(block, dx, dy), shift_plane(block, -dx, -dy)]


def far_halves(pair, dx, dy):
    below, above = pair
    half = below.shape[0] // 2
    return [shift_plane(below[:half], dx, dy), shift_plane(above[half:], -dx, -dy)]


def gather_plane(lower, upper, tiles):
    along_x, along_y = (1, 0), (0, 1)
    near_low = both_ways(lower, *along_x)
    near_up = both_ways(upper, *along_y)
    line_low = jnp.concatenate([lower] + near_low + far_halves(near_low, *along_x), axis=0)
    line_up = jnp.concatenate([upper] + near_up + far_halves(near_up, *along_y), axis=0)
    near_low = both_ways(line_low, *along_y)
    near_up = both_ways(line_up, *along_x)
    near_low[0], near_low[1], near_up[0], near_up[1], tiles = lax.optimization_barrier(
        (*near_low, *near_up, tiles)
    )
    far_low = far_halves(near_low, *along_y)
    far_up = far_halves(near_up, *along_x)
    return [line_low] + near_low + far_low + [line_up] + near_up + far_up, tiles


def split_kernel(tiles_ref, out_ref, left_ref, rows_ref):
    for t in range(tiles_ref.shape[0]):
        for side in range(2):
            lanes = pl.ds(side * LANES, LANES)
            left_ref[...] = tiles_ref[t, :, lanes]
            for hi in range(8):
                for a in range(2):
                    for b in range(2):
                        rows_ref[pl.ds(hi * 32 + a * 2 + b, 8, stride=4), :] = left_ref[
                            pl.ds(hi * 32 + a * 16 + b, 8, stride=2), :
                        ]
            value = rows_ref[...]
            high = value.astype(jnp.bfloat16)
            out_ref[t, 0, :, lanes] = high
            out_ref[t, 1, :, lanes] = (value - high.astype(jnp.float32)).astype(jnp.bfloat16)


def split_tiles(integrals):
    slots, size, _ = integrals.shape
    step = 2
    return pl.pallas_call(
        split_kernel,
        grid=(slots // step,),
        in_specs=[pl.BlockSpec((step, size, size), lambda k: (k, 0, 0))],
        out_specs=pl.BlockSpec((step, 2, size, size), lambda k: (k, 0, 0, 0)),
        out_shape=jax.ShapeDtypeStruct((slots, 2, size, size), jnp.bfloat16),
        scratch_shapes=[pltpu.VMEM((size, LANES), jnp.float32)] * 2,
        cost_estimate=pl.CostEstimate(
            flops=slots * size * size * 4, bytes_accessed=slots * size * size * 8, transcendentals=0
        ),
        name="split_tiles",
    )(integrals)


def place_in_line(offset):
    return jnp.where(offset == 0, 0, jnp.where(offset == 1, 2, jnp.where(offset == 2, 3, 1)))


def ladder_kernel(row_ref, col_ref, count_ref, tiles_ref, *rest):
    pieces = rest[:10]
    out_ref, amp_ref, held_ref, acc_ref, amp_sem, held_sem = rest[10:]
    size = tiles_ref.shape[-1]
    count = count_ref[0]
    copies = []
    start = 0
    for i, piece in enumerate(pieces):
        rows = piece.shape[0]
        copies.append(pltpu.make_async_copy(piece, amp_ref.at[pl.ds(start, rows)], amp_sem.at[i]))
        start += rows
    for copy in copies:
        copy.start()

    def tile_copy(k):
        return pltpu.make_async_copy(tiles_ref.at[k], held_ref.at[k], held_sem.at[k])

    def fetch(k, carry):
        tile_copy(k).start()
        return carry

    lax.fori_loop(0, count, fetch, 0)
    acc_ref[...] = jnp.zeros_like(acc_ref)
    for copy in copies:
        copy.wait()
    me = lax.axis_index("ab")
    my_y = me // SIDE
    my_x = me % SIDE

    def add_slot(k, carry):
        tile_copy(k).wait()
        row = row_ref[k]
        col = col_ref[k]
        source = col // 2
        in_x = place_in_line((source % SIDE - my_x + SIDE) % SIDE)
        in_y = place_in_line((source // SIDE - my_y + SIDE) % SIDE)
        spot = jnp.where(col % 2 == 0, in_y * SIDE + in_x, SIDE * SIDE + in_x * SIDE + in_y)
        factor = amp_ref[pl.ds(pl.multiple_of(spot * size, size), size), :]
        high = factor.astype(jnp.bfloat16)
        low = (factor - high.astype(jnp.float32)).astype(jnp.bfloat16)
        tile_high = held_ref[k, 0]
        tile_low = held_ref[k, 1]
        term = jnp.dot(tile_high, high, preferred_element_type=jnp.float32)
        term += jnp.dot(tile_high, low, preferred_element_type=jnp.float32)
        term += jnp.dot(tile_low, high, preferred_element_type=jnp.float32)
        acc_ref[row] += term
        return carry

    lax.fori_loop(0, count, add_slot, 0)

    first = lax.broadcasted_iota(jnp.int32, (8, LANES), 0) < 4

    def put(row, carry):
        for hi in range(8):
            for g in range(4):
                left = acc_ref[row, pl.ds(hi * 32 + g * 8, 8), pl.ds(0, LANES)]
                right = acc_ref[row, pl.ds(hi * 32 + g * 8, 8), pl.ds(LANES, LANES)]
                spot = pl.multiple_of(row * 64, 64)
                out_ref[hi, pl.ds(spot + g * 16, 8), :] = jnp.where(first, left, pltpu.roll(right, 4, 0))
                out_ref[hi, pl.ds(spot + g * 16 + 8, 8), :] = jnp.where(first, pltpu.roll(left, 4, 0), right)
        return carry

    lax.fori_loop(0, acc_ref.shape[0], put, 0)


def ladder(tile_row, tile_col, tile_count, tiles, pieces, blocks):
    slots, _, size, _ = tiles.shape
    width = pieces[0].shape[1]
    total = sum(piece.shape[0] for piece in pieces)
    smem = pl.BlockSpec(memory_space=pltpu.SMEM)
    hbm = pl.BlockSpec(memory_space=pl.ANY)
    return pl.pallas_call(
        ladder_kernel,
        in_specs=[smem] * 3 + [hbm] * (1 + len(pieces)),
        out_specs=pl.BlockSpec(memory_space=pltpu.VMEM),
        out_shape=jax.ShapeDtypeStruct((8, blocks * 64, LANES), jnp.float32),
        scratch_shapes=[
            pltpu.VMEM((total, width), jnp.float32),
            pltpu.VMEM((slots, 2, size, size), jnp.bfloat16),
            pltpu.VMEM((blocks, size, width), jnp.float32),
            pltpu.SemaphoreType.DMA((len(pieces),)),
            pltpu.SemaphoreType.DMA((slots,)),
        ],
        compiler_params=pltpu.CompilerParams(vmem_limit_bytes=48 * 1024 * 1024),
        cost_estimate=pl.CostEstimate(
            flops=slots * 6 * size * size * width,
            bytes_accessed=slots * size * size * 4 + total * width * 4 + blocks * size * width * 4,
            transcendentals=0,
        ),
        name="ladder",
    )(tile_row, tile_col, tile_count, tiles, *pieces)


def finish_kernel(direct_ref, mirror_ref, out_ref, rows_ref):
    for o in range(2):
        for a in range(2):
            for b in range(2):
                rows_ref[pl.ds(b, LANES, stride=2), :] = (
                    direct_ref[pl.ds(o * 4 + a * 2 + b, LANES, stride=8), :]
                    + mirror_ref[pl.ds(o * 4 + b * 2 + a, LANES, stride=8), :]
                )
            out_ref[pl.ds(o * LANES, LANES), a, :] = rows_ref[...].T


def finish(direct, mirror):
    return pl.pallas_call(
        finish_kernel,
        in_specs=[pl.BlockSpec(memory_space=pltpu.VMEM)] * 2,
        out_specs=pl.BlockSpec(memory_space=pltpu.VMEM),
        out_shape=jax.ShapeDtypeStruct((2 * LANES, 2, 2 * LANES), jnp.float32),
        scratch_shapes=[pltpu.VMEM((2 * LANES, LANES), jnp.float32)],
        name="finish",
    )(direct, mirror)


def per_device(amplitudes, integrals, tile_row, tile_col, tile_count):
    occ_dev = amplitudes.shape[0]
    tile_size = integrals.shape[1]
    blocks = lax.axis_size("ab")
    cd_size = lax.axis_size("cd")
    across = amplitudes.T
    tiles = split_tiles(integrals)
    lower, upper = across[:tile_size], across[tile_size:]
    pieces, tiles = gather_plane(lower, upper, tiles)
    partial_value = ladder(tile_row, tile_col, tile_count, tiles, pieces, blocks)
    direct = lax.psum_scatter(partial_value, "cd", scatter_dimension=0, tiled=True)
    outgoing = direct.reshape(blocks * cd_size, 8, LANES)
    arrived = lax.all_to_all(outgoing, ("ab", "cd"), split_axis=0, concat_axis=0, tiled=True)
    partner = lax.ppermute(arrived, "ij", [(0, 1), (1, 0)])
    total = finish(direct.reshape(-1, LANES), partner.reshape(-1, LANES))
    return total.reshape(occ_dev, 1, 2, 2 * LANES)


def solution(mesh):
    in_specs = (
        P("ij", ("cd", "ab")),
        P(("ab", "cd"), None, None),
        P(("ab", "cd")),
        P(("ab", "cd")),
        P(("ab", "cd")),
    )
    out_specs = P("ij", "ab", "cd", None)
    return jax.shard_map(
        per_device, mesh=mesh, in_specs=in_specs, out_specs=out_specs, check_vma=False
    )
```

time: 278 us -> 194 us (0.70)
  waiting for transfers between devices: 136 us -> 81.6 us
  local copies, waits for them, and re-layouts: 56.8 us -> 7.89 us
  matrix products: 36.3 us -> 0 us
  Pallas kernels: 0 us -> 36.2 us
  starting transfers between devices: 2.67 us -> 22.9 us
    all_gather x1 -> x0, waiting for transfers between devices: 78.7 us -> none  [per_device(): gathered = lax.all_gather(amplitudes, 'ab', axis=1, tiled=True)]
    dot_general x2 -> x0, matrix products: 36.3 us -> none  [the longest x1 20 us: place_rows(): jnp.einsum('okf,kef->oke', chosen, tile_rows, precision=lax.Precision.HIG...]
    pallas_call x0 -> x3, Pallas kernels: none -> 36.2 us  [the longest x1 18 us: split_tiles(): pl.pallas_call(split_kernel, grid=(slots // step,), in_specs=[pl.BlockSpe...]
    ppermute x1 -> x17, starting transfers between devices: 2.63 us -> 22.9 us  [the longest x16 20.4 us: shift_plane(): return lax.ppermute(block, 'ab', plane_route(dx, dy))]
    transpose x3 -> x0, local copies, waits for them, and re-layouts: 19.2 us -> none  [the longest x1 7.61 us: per_device(): outgoing = jnp.transpose(outgoing, (2, 3, 1, 0, 4))]
    ppermute x1 -> x17, waiting for transfers between devices: 1.54 us -> 19.4 us  [the longest x16 17.9 us: shift_plane(): return lax.ppermute(block, 'ab', plane_route(dx, dy))]
    reshape x4 -> x0, local copies, waits for them, and re-layouts: 16.2 us -> none  [the longest x1 8.97 us: per_device(): columns = gathered.reshape(occ_dev, -1, tile_size)]
    gather x1 -> x0, local copies, waits for them, and re-layouts: 10.9 us -> none  [per_device(): chosen = jnp.take(columns, tile_col, axis=1)]
  transfers between devices with their start and end apart: 3 -> 18, of which waited for: 3 -> 10; matrix products, arithmetic and copies ran while one was open for 0% -> 1% of each run, Pallas kernels for 0% -> 9%
where the time goes in v1:
time: 194 us; the launch traced here: 193 us
  waiting for transfers between devices  81.6 us (42%)
  Pallas kernels  36.2 us (19%)
  blocking collectives  30.3 us (16%)
  starting transfers between devices  22.9 us (12%)
  between operations  14.2 us (7%)
  local copies, waits for them, and re-layouts  7.89 us (4%)
    reduce_scatter x1, waiting for transfers between devices, per_device(): lax.psum_scatter(partial_value, 'cd', scatter_dimension=0, tiled=True)  62.2 us
    all_to_all x1, blocking collectives, per_device(): lax.all_to_all(outgoing, ('ab', 'cd'), split_axis=0, concat_axis=0, tiled...  30.3 us
    ppermute x16, starting transfers between devices, shift_plane(): return lax.ppermute(block, 'ab', plane_route(dx, dy))  20.4 us
    pallas_call x1, Pallas kernels, split_tiles(): pl.pallas_call(split_kernel, grid=(slots // step,), in_specs=[pl.BlockSpe...  18 us
    ppermute x16, waiting for transfers between devices, shift_plane(): return lax.ppermute(block, 'ab', plane_route(dx, dy))  17.9 us
    pallas_call x1, Pallas kernels, ladder(): pl.pallas_call(ladder_kernel, in_specs=[smem] * 3 + [hbm] * (1 + len(piec...  15.9 us
    unnamed x13, local copies, waits for them, and re-layouts  4.18 us
  transfers between devices with their start and end apart: 18, of which 10 were waited for; matrix products, arithmetic and copies ran while one was open for 1% of the time, Pallas kernels for 9%

profile of v1, /device:TPU:1, one launch (start us, length us, event | category | flops | bytes accessed | tf_op | source)
XLA Modules:
  0.0 193.1 jit_solution(322840135150560748)
XLA Ops:
  6.5 1.2 copy.6
  7.8 0.8 fusion
  8.6 3.6 %collective-permute-start.7 = (f32[256,256]{1,0:T(8,128)S(1)}, f32[256,256]{1,0:T(8,128)S(1)}, u32[]{:S(2)}, u32[]{:S(2)}) collective-permute-start(f32[256,256]{1,0:T(8,128)S(1)} %get-tuple-element.15), channel_id=1, source_target_pairs={{0,192},{16,208},{32,224},{48,240},{64,0},{80,16},{96,32},{112,48}... | collective-permute-start | bytes 786440 | tf_op jit(solution)/shard_map/ppermute | solution.py:23
  12.1 0.0 collective-permute-start.6
  12.1 2.5 %collective-permute-start.1 = (f32[256,256]{1,0:T(8,128)S(1)}, f32[256,256]{1,0:T(8,128)S(1)}, u32[]{:S(2)}, u32[]{:S(2)}) collective-permute-start(f32[256,256]{1,0:T(8,128)S(1)} %get-tuple-element.18), channel_id=1, source_target_pairs={{0,48},{16,0},{32,16},{48,32},{64,112},{80,64},{96,80},{112,96},{1... | collective-permute-start | bytes 786440 | tf_op jit(solution)/shard_map/ppermute | solution.py:23
  14.6 0.0 collective-permute-start
  14.6 2.5 %collective-permute-done.7 = f32[256,256]{1,0:T(8,128)S(1)} collective-permute-done((f32[256,256]{1,0:T(8,128)S(1)}, f32[256,256]{1,0:T(8,128)S(1)}, u32[]{:S(2)}, u32[]{:S(2)}) %collective-permute-start.7) | collective-permute-done | bytes 262176 | tf_op jit(solution)/shard_map/ppermute | solution.py:23
  17.1 3.5 %collective-permute-start.9 = (f32[128,256]{1,0:T(8,128)S(1)}, f32[128,256]{1,0:T(8,128)S(1)}, u32[]{:S(2)}, u32[]{:S(2)}) collective-permute-start(f32[128,256]{1,0:T(8,128)S(1)} %slice.45), channel_id=1, source_target_pairs={{0,192},{16,208},{32,224},{48,240},{64,0},{80,16},{96,32},{112,48}... | collective-permute-start | bytes 393224 | tf_op jit(solution)/shard_map/ppermute | solution.py:23
  20.6 0.0 collective-permute-done.6
  20.6 0.1 collective-permute-start.8
  20.7 0.0 collective-permute-done.1
  20.7 2.6 %collective-permute-start.3 = (f32[128,256]{1,0:T(8,128)S(1)}, f32[128,256]{1,0:T(8,128)S(1)}, u32[]{:S(2)}, u32[]{:S(2)}) collective-permute-start(f32[128,256]{1,0:T(8,128)S(1)} %slice.42), channel_id=1, source_target_pairs={{0,48},{16,0},{32,16},{48,32},{64,112},{80,64},{96,80},{112,96},{1... | collective-permute-start | bytes 393224 | tf_op jit(solution)/shard_map/ppermute | solution.py:23
  23.3 0.0 collective-permute-done
  23.3 0.1 collective-permute-start.2
  23.4 0.7 constant_dynamic-update-slice_fusion.8
  24.1 0.7 constant_dynamic-update-slice_fusion.7
  24.9 3.5 %collective-permute-done.2 = f32[128,256]{1,0:T(8,128)S(1)} collective-permute-done((f32[128,256]{1,0:T(8,128)S(1)}, f32[128,256]{1,0:T(8,128)S(1)}, u32[]{:S(2)}, u32[]{:S(2)}) %collective-permute-start.2) | collective-permute-done | bytes 131104 | tf_op jit(solution)/shard_map/ppermute | solution.py:23
  28.4 0.0 collective-permute-done.3
  28.5 2.7 %collective-permute-start.5 = (f32[1024,256]{1,0:T(8,128)S(1)}, f32[1024,256]{1,0:T(8,128)S(1)}, u32[]{:S(2)}, u32[]{:S(2)}) collective-permute-start(f32[1024,256]{1,0:T(8,128)S(1)} %constant_dynamic-update-slice_fusion.rest_0_), channel_id=1, source_target_pairs={{0,192},{16,208},{32,224},{48,240},{64,0},{80,16},{96,32},{112,48}... | collective-permute-start | bytes 3145736 | tf_op jit(solution)/shard_map/ppermute | solution.py:23
  31.2 0.0 collective-permute-start.4
  31.2 0.0 collective-permute-done.8
  31.2 0.7 constant_dynamic-update-slice_fusion.6
  31.9 0.0 collective-permute-done.9
  31.9 0.7 constant_dynamic-update-slice_fusion.5.rest_5_
  32.5 0.0 collective-permute-start.11
  32.5 1.5 collective-permute-start.10
  34.0 18.0 %split_tiles.1.tiles_ref = bf16[46,2,256,256]{3,2,1,0:T(8,128)(2,1)} custom-call(f32[46,256,256]{2,1,0:T(8,128)} %tiles_ref.1), custom_call_target="tpu_custom_call" | custom-call | flops 12058624 | bytes 24117248 | tf_op jit(solution)/shard_map/split_tiles/pallas_call | solution.py:72
  52.0 0.0 collective-permute-done.5.rest_2_
  52.0 1.4 collective-permute-done.4.rest_1_
  53.3 0.3 collective-permute-done.11.rest_7_
  53.7 1.2 collective-permute-done.10.rest_6_
  55.0 1.1 slice.38
  56.1 1.1 slice.39
  57.1 0.4 collective-permute-start.15
  57.5 1.2 collective-permute-start.14
  58.7 2.4 %collective-permute-start.13 = (f32[512,256]{1,0:T(8,128)S(1)}, f32[512,256]{1,0:T(8,128)S(1)}, u32[]{:S(2)}, u32[]{:S(2)}) collective-permute-start(f32[512,256]{1,0:T(8,128)S(1)} %slice.37), channel_id=1, source_target_pairs={{0,192},{16,208},{32,224},{48,240},{64,0},{80,16},{96,32},{112,48}... | collective-permute-start | bytes 1572872 | tf_op jit(solution)/shard_map/ppermute | solution.py:23
  61.7 4.2 %collective-permute-done.15.rest_9_ = f32[512,256]{1,0:T(8,128)S(1)} collective-permute-done((f32[512,256]{1,0:T(8,128)S(1)}, f32[512,256]{1,0:T(8,128)S(1)}, u32[]{:S(2)}, u32[]{:S(2)}) %collective-permute-start.15) | collective-permute-done | bytes 524320 | tf_op jit(solution)/shard_map/ppermute | solution.py:23
  65.9 1.5 collective-permute-done.14.rest_8_
  67.4 0.0 collective-permute-done.13.rest_4_
  67.4 3.2 %collective-permute-done.12.rest_3_ = f32[512,256]{1,0:T(8,128)S(1)} collective-permute-done((f32[512,256]{1,0:T(8,128)S(1)}, f32[512,256]{1,0:T(8,128)S(1)}, u32[]{:S(2)}, u32[]{:S(2)}) %collective-permute-start.12) | collective-permute-done | bytes 524320 | tf_op jit(solution)/shard_map/ppermute | solution.py:23
  70.6 15.9 %ladder.1 = f32[8,1024,128]{2,1,0:T(8,128)} custom-call(s32[46]{0:T(128)S(1)} %copy-done, s32[46]{0:T(128)S(1)} %copy-done.1, s32[1]{0:T(128)S(6)} %copy.16.count_ref, bf16[46,2,256,256]{3,2,1,0:T(8,128)(2,1)} %split_tiles.1.tiles_ref, f32[1024,256]{1,0:T(8,128)S(1)} %constant_dynamic-update-slice_fusion.rest_0_, ...), custom_call_target="tpu_custom_call" | custom-call | flops 4630511616 | bytes 24641536 | tf_op jit(solution)/shard_map/ladder/pallas_call | solution.py:161
  86.6 0.0 reduce-scatter.2.cloned.1.call-update
  86.6 62.2 %reduce-scatter.2.cloned.1.call-done = f32[1,1024,128]{2,1,0:T(8,128)} async-done(((f32[8,1024,128]{2,1,0:T(8,128)}), f32[1,1024,128]{2,1,0:T(8,128)}) %reduce-scatter.2.cloned.1.call-update) | async-done | bytes 524304 | tf_op jit(solution)/shard_map/reduce_scatter | solution.py:215
  148.8 30.3 %all_to_all.5 = f32[128,8,128]{2,1,0:T(8,128)S(1)} all-to-all(f32[128,8,128]{2,1,0:T(8,128)} %bitcast.7), channel_id=1, replica_groups=mesh['ab'=16,'cd'=8,'ij'=2] {'ab','cd'}, dimensions={0} | all-to-all | bytes 1048576 | tf_op jit(solution)/shard_map/all_to_all | solution.py:217
  179.1 2.5 %collective-permute-start.16 = (f32[128,8,128]{2,1,0:T(8,128)S(1)}, f32[128,8,128]{2,1,0:T(8,128)S(1)}, u32[]{:S(2)}, u32[]{:S(2)}) collective-permute-start(f32[128,8,128]{2,1,0:T(8,128)S(1)} %all_to_all.5), channel_id=1, source_target_pairs={{0,1},{1,0},{2,3},{3,2},{4,5},{5,4},{6,7},{7,6},{8,9},{9,8},{10,11... | collective-permute-start | bytes 1572872 | tf_op jit(solution)/shard_map/ppermute | solution.py:218
  181.6 1.5 collective-permute-done.16
  183.2 0.8 copy-done.2
  184.0 2.3 %finish.1 = f32[256,2,256]{2,1,0:T(2,128)} custom-call(f32[1024,128]{1,0:T(8,128)} %bitcast.8, f32[1024,128]{1,0:T(8,128)} %bitcast.10), custom_call_target="tpu_custom_call" | custom-call | tf_op jit(solution)/shard_map/finish/pallas_call | solution.py:195
  (17 shorter events, 0.2 us)
Async XLA Ops:
  6.5 142.3 %reduce-scatter.2.cloned.1.call-start = ((), (), s32[]{:S(2)}) async-start(), calls=%async_computation.2 | async-start | bytes 4718592 | tf_op jit(solution)/shard_map/reduce_scatter | solution.py:215
  8.6 8.5 %collective-permute-start.7 = (f32[256,256]{1,0:T(8,128)S(1)}, f32[256,256]{1,0:T(8,128)S(1)}, u32[]{:S(2)}, u32[]{:S(2)}) collective-permute-start(f32[256,256]{1,0:T(8,128)S(1)} %get-tuple-element.15), channel_id=1, source_target_pairs={{0,192},{16,208},{32,224},{48,240},{64,0},{80,16},{96,32},{112,48}... | collective-permute-start | bytes 786440 | tf_op jit(solution)/shard_map/ppermute | solution.py:23
  12.1 8.5 %collective-permute-start.6 = (f32[256,256]{1,0:T(8,128)S(1)}, f32[256,256]{1,0:T(8,128)S(1)}, u32[]{:S(2)}, u32[]{:S(2)}) collective-permute-start(f32[256,256]{1,0:T(8,128)S(1)} %get-tuple-element.15), channel_id=1, source_target_pairs={{0,64},{16,80},{32,96},{48,112},{64,128},{80,144},{96,160},{112,17... | collective-permute-start | bytes 786440 | tf_op jit(solution)/shard_map/ppermute | solution.py:23
  12.1 8.6 %collective-permute-start.1 = (f32[256,256]{1,0:T(8,128)S(1)}, f32[256,256]{1,0:T(8,128)S(1)}, u32[]{:S(2)}, u32[]{:S(2)}) collective-permute-start(f32[256,256]{1,0:T(8,128)S(1)} %get-tuple-element.18), channel_id=1, source_target_pairs={{0,48},{16,0},{32,16},{48,32},{64,112},{80,64},{96,80},{112,96},{1... | collective-permute-start | bytes 786440 | tf_op jit(solution)/shard_map/ppermute | solution.py:23
  14.6 8.7 %collective-permute-start = (f32[256,256]{1,0:T(8,128)S(1)}, f32[256,256]{1,0:T(8,128)S(1)}, u32[]{:S(2)}, u32[]{:S(2)}) collective-permute-start(f32[256,256]{1,0:T(8,128)S(1)} %get-tuple-element.18), channel_id=1, source_target_pairs={{0,16},{16,32},{32,48},{48,0},{64,80},{80,96},{96,112},{112,64},{1... | collective-permute-start | bytes 786440 | tf_op jit(solution)/shard_map/ppermute | solution.py:23
  17.1 14.8 %collective-permute-start.9 = (f32[128,256]{1,0:T(8,128)S(1)}, f32[128,256]{1,0:T(8,128)S(1)}, u32[]{:S(2)}, u32[]{:S(2)}) collective-permute-start(f32[128,256]{1,0:T(8,128)S(1)} %slice.45), channel_id=1, source_target_pairs={{0,192},{16,208},{32,224},{48,240},{64,0},{80,16},{96,32},{112,48}... | collective-permute-start | bytes 393224 | tf_op jit(solution)/shard_map/ppermute | solution.py:23
  20.6 10.6 %collective-permute-start.8 = (f32[128,256]{1,0:T(8,128)S(1)}, f32[128,256]{1,0:T(8,128)S(1)}, u32[]{:S(2)}, u32[]{:S(2)}) collective-permute-start(f32[128,256]{1,0:T(8,128)S(1)} %slice.44), channel_id=1, source_target_pairs={{0,64},{16,80},{32,96},{48,112},{64,128},{80,144},{96,160},{112,17... | collective-permute-start | bytes 393224 | tf_op jit(solution)/shard_map/ppermute | solution.py:23
  20.7 7.7 %collective-permute-start.3 = (f32[128,256]{1,0:T(8,128)S(1)}, f32[128,256]{1,0:T(8,128)S(1)}, u32[]{:S(2)}, u32[]{:S(2)}) collective-permute-start(f32[128,256]{1,0:T(8,128)S(1)} %slice.42), channel_id=1, source_target_pairs={{0,48},{16,0},{32,16},{48,32},{64,112},{80,64},{96,80},{112,96},{1... | collective-permute-start | bytes 393224 | tf_op jit(solution)/shard_map/ppermute | solution.py:23
  23.3 5.1 %collective-permute-start.2 = (f32[128,256]{1,0:T(8,128)S(1)}, f32[128,256]{1,0:T(8,128)S(1)}, u32[]{:S(2)}, u32[]{:S(2)}) collective-permute-start(f32[128,256]{1,0:T(8,128)S(1)} %slice.41), channel_id=1, source_target_pairs={{0,16},{16,32},{32,48},{48,0},{64,80},{80,96},{96,112},{112,64},{1... | collective-permute-start | bytes 393224 | tf_op jit(solution)/shard_map/ppermute | solution.py:23
  28.5 23.5 %collective-permute-start.5 = (f32[1024,256]{1,0:T(8,128)S(1)}, f32[1024,256]{1,0:T(8,128)S(1)}, u32[]{:S(2)}, u32[]{:S(2)}) collective-permute-start(f32[1024,256]{1,0:T(8,128)S(1)} %constant_dynamic-update-slice_fusion.rest_0_), channel_id=1, source_target_pairs={{0,192},{16,208},{32,224},{48,240},{64,0},{80,16},{96,32},{112,48}... | collective-permute-start | bytes 3145736 | tf_op jit(solution)/shard_map/ppermute | solution.py:23
  31.2 22.2 %collective-permute-start.4 = (f32[1024,256]{1,0:T(8,128)S(1)}, f32[1024,256]{1,0:T(8,128)S(1)}, u32[]{:S(2)}, u32[]{:S(2)}) collective-permute-start(f32[1024,256]{1,0:T(8,128)S(1)} %constant_dynamic-update-slice_fusion.rest_0_), channel_id=1, source_target_pairs={{0,64},{16,80},{32,96},{48,112},{64,128},{80,144},{96,160},{112,17... | collective-permute-start | bytes 3145736 | tf_op jit(solution)/shard_map/ppermute | solution.py:23
  32.5 38.1 %copy-start = (s32[46]{0:T(128)S(1)}, s32[46]{0:T(128)}, u32[]{:S(2)}) copy-start(s32[46]{0:T(128)} %row_ref.1) | copy-start | bytes 556
  32.5 38.1 %copy-start.1 = (s32[46]{0:T(128)S(1)}, s32[46]{0:T(128)}, u32[]{:S(2)}) copy-start(s32[46]{0:T(128)} %col_ref.1) | copy-start | bytes 556
  32.5 21.2 %collective-permute-start.11 = (f32[1024,256]{1,0:T(8,128)}, f32[1024,256]{1,0:T(8,128)}, u32[]{:S(2)}, u32[]{:S(2)}) collective-permute-start(f32[1024,256]{1,0:T(8,128)} %constant_dynamic-update-slice_fusion.5.rest_5_), channel_id=1, source_target_pairs={{0,48},{16,0},{32,16},{48,32},{64,112},{80,64},{96,80},{112,96},{1... | collective-permute-start | bytes 3145736 | tf_op jit(solution)/shard_map/ppermute | solution.py:23
  32.5 22.4 %collective-permute-start.10 = (f32[1024,256]{1,0:T(8,128)}, f32[1024,256]{1,0:T(8,128)}, u32[]{:S(2)}, u32[]{:S(2)}) collective-permute-start(f32[1024,256]{1,0:T(8,128)} %constant_dynamic-update-slice_fusion.5.rest_5_), channel_id=1, source_target_pairs={{0,16},{16,32},{32,48},{48,0},{64,80},{80,96},{96,112},{112,64},{1... | collective-permute-start | bytes 3145736 | tf_op jit(solution)/shard_map/ppermute | solution.py:23
  57.1 8.8 %collective-permute-start.15 = (f32[512,256]{1,0:T(8,128)S(1)}, f32[512,256]{1,0:T(8,128)S(1)}, u32[]{:S(2)}, u32[]{:S(2)}) collective-permute-start(f32[512,256]{1,0:T(8,128)S(1)} %slice.39), channel_id=1, source_target_pairs={{0,48},{16,0},{32,16},{48,32},{64,112},{80,64},{96,80},{112,96},{1... | collective-permute-start | bytes 1572872 | tf_op jit(solution)/shard_map/ppermute | solution.py:23
  57.5 9.9 %collective-permute-start.14 = (f32[512,256]{1,0:T(8,128)S(1)}, f32[512,256]{1,0:T(8,128)S(1)}, u32[]{:S(2)}, u32[]{:S(2)}) collective-permute-start(f32[512,256]{1,0:T(8,128)S(1)} %slice.38), channel_id=1, source_target_pairs={{0,16},{16,32},{32,48},{48,0},{64,80},{80,96},{96,112},{112,64},{1... | collective-permute-start | bytes 1572872 | tf_op jit(solution)/shard_map/ppermute | solution.py:23
  58.7 8.7 %collective-permute-start.13 = (f32[512,256]{1,0:T(8,128)S(1)}, f32[512,256]{1,0:T(8,128)S(1)}, u32[]{:S(2)}, u32[]{:S(2)}) collective-permute-start(f32[512,256]{1,0:T(8,128)S(1)} %slice.37), channel_id=1, source_target_pairs={{0,192},{16,208},{32,224},{48,240},{64,0},{80,16},{96,32},{112,48}... | collective-permute-start | bytes 1572872 | tf_op jit(solution)/shard_map/ppermute | solution.py:23
  61.1 9.5 %collective-permute-start.12 = (f32[512,256]{1,0:T(8,128)S(1)}, f32[512,256]{1,0:T(8,128)S(1)}, u32[]{:S(2)}, u32[]{:S(2)}) collective-permute-start(f32[512,256]{1,0:T(8,128)S(1)} %slice.36), channel_id=1, source_target_pairs={{0,64},{16,80},{32,96},{48,112},{64,128},{80,144},{96,160},{112,17... | collective-permute-start | bytes 1572872 | tf_op jit(solution)/shard_map/ppermute | solution.py:23
  179.1 4.1 %collective-permute-start.16 = (f32[128,8,128]{2,1,0:T(8,128)S(1)}, f32[128,8,128]{2,1,0:T(8,128)S(1)}, u32[]{:S(2)}, u32[]{:S(2)}) collective-permute-start(f32[128,8,128]{2,1,0:T(8,128)S(1)} %all_to_all.5), channel_id=1, source_target_pairs={{0,1},{1,0},{2,3},{3,2},{4,5},{5,4},{6,7},{7,6},{8,9},{9,8},{10,11... | collective-permute-start | bytes 1572872 | tf_op jit(solution)/shard_map/ppermute | solution.py:218
  183.2 0.8 copy-start.2
Sparse Core Ops, SparseCore 0:
  86.7 62.0 reduce-scatter.1

commit v2 on v1

v2 whole, which is shorter than its diff:
```python
import functools

import jax
import jax.numpy as jnp
from jax import lax
from jax.experimental import pallas as pl
from jax.experimental.pallas import tpu as pltpu
from jax.sharding import PartitionSpec as P

LANES = 128
SIDE = 4
CHUNKS = 2
HELD = 16
GROUP = 4


def plane_route(dx, dy):
    route = []
    for y in range(SIDE):
        for x in range(SIDE):
            route.append((y * SIDE + x, (y + dy) % SIDE * SIDE + (x + dx) % SIDE))
    return route


def both_ways(block, dx, dy):
    return [
        lax.ppermute(block, "ab", plane_route(dx, dy)),
        lax.ppermute(block, "ab", plane_route(-dx, -dy)),
    ]


def far_halves(pair, dx, dy):
    below, above = pair
    half = below.shape[0] // 2
    return [
        lax.ppermute(below[:half], "ab", plane_route(dx, dy)),
        lax.ppermute(above[half:], "ab", plane_route(-dx, -dy)),
    ]


def gather_line(block, dx, dy):
    pair = both_ways(block, dx, dy)
    return pair + far_halves(pair, dx, dy)


def first_line(block, dx, dy):
    far = lax.ppermute(block, "ab", plane_route(2 * dx, 2 * dy))
    return jnp.concatenate([block] + both_ways(block, dx, dy) + [far], axis=0)


def gather_plane(block):
    half = block.shape[0] // 2
    along_x, along_y = (1, 0), (0, 1)
    low = first_line(block[:half], *along_x)
    up = first_line(block[half:], *along_y)
    return [low] + gather_line(low, *along_y) + [up] + gather_line(up, *along_x)


def place_in_line(offset):
    return jnp.where(offset == 0, 0, jnp.where(offset == 1, 2, jnp.where(offset == 2, 3, 1)))


def ladder_kernel(row_ref, col_ref, count_ref, tiles_ref, *rest, pieces_given):
    pieces = rest[:pieces_given]
    out_ref, amp_ref, held_ref, amp_sem, held_sem = rest[-5:]
    size = tiles_ref.shape[-1]
    count = count_ref[0]
    copies = []
    start = 0
    for i, piece in enumerate(pieces):
        rows = piece.shape[0]
        copies.append(pltpu.make_async_copy(piece, amp_ref.at[pl.ds(start, rows)], amp_sem.at[i]))
        start += rows
    for copy in copies:
        copy.start()

    def tile_copy(k):
        spot = lax.rem(k, HELD)
        return pltpu.make_async_copy(tiles_ref.at[k], held_ref.at[spot], held_sem.at[spot])

    def fetch(k):
        @pl.when(k < count)
        def _():
            tile_copy(k).start()

    for k in range(HELD):
        fetch(k)
    out_ref[...] = jnp.zeros_like(out_ref)
    for copy in copies:
        copy.wait()
    me = lax.axis_index("ab")
    my_y = me // SIDE
    my_x = me % SIDE

    def spot_of(col):
        if len(pieces) == 1:
            return col
        source = col // 2
        in_x = place_in_line((source % SIDE - my_x + SIDE) % SIDE)
        in_y = place_in_line((source // SIDE - my_y + SIDE) % SIDE)
        return jnp.where(col % 2 == 0, in_y * SIDE + in_x, SIDE * SIDE + in_x * SIDE + in_y)

    def split(value):
        high = value.astype(jnp.bfloat16)
        return high, (value - high.astype(jnp.float32)).astype(jnp.bfloat16)

    def term_of(k):
        spot = spot_of(col_ref[k])
        high, low = split(amp_ref[pl.ds(pl.multiple_of(spot * size, size), size), :])
        both = jnp.concatenate([high, low], axis=1)
        tile_high, tile_low = split(held_ref[lax.rem(k, HELD)])
        wide = jnp.dot(tile_high, both, preferred_element_type=jnp.float32)
        term = jnp.dot(tile_low, high, preferred_element_type=jnp.float32)
        return term + wide[:, :LANES] + wide[:, LANES:]

    def add_term(k, term):
        spot = pl.multiple_of(row_ref[k] * 32, 32)
        for hi in range(8):
            out_ref[hi, pl.ds(spot, 32), :] += term[hi * 32 : hi * 32 + 32]

    def add_group(j, carry):
        for i in range(GROUP):
            tile_copy(GROUP * j + i).wait()
        terms = [term_of(GROUP * j + i) for i in range(GROUP)]
        for i in range(GROUP):
            add_term(GROUP * j + i, terms[i])
        for i in range(GROUP):
            fetch(GROUP * j + i + HELD)
        return carry

    def add_one(k, carry):
        tile_copy(k).wait()
        add_term(k, term_of(k))
        return carry

    groups = count // GROUP
    lax.fori_loop(0, groups, add_group, 0)
    lax.fori_loop(groups * GROUP, count, add_one, 0)


def ladder(tile_row, tile_col, tile_count, after, tiles, pieces, blocks):
    slots, size, _ = tiles.shape
    total = sum(piece.shape[0] for piece in pieces)
    smem = pl.BlockSpec(memory_space=pltpu.SMEM)
    hbm = pl.BlockSpec(memory_space=pl.ANY)
    return pl.pallas_call(
        functools.partial(ladder_kernel, pieces_given=len(pieces)),
        in_specs=[smem] * 3 + [hbm] * (1 + len(pieces) + len(after)),
        out_specs=pl.BlockSpec(memory_space=pltpu.VMEM),
        out_shape=jax.ShapeDtypeStruct((8, blocks * 32, LANES), jnp.float32),
        scratch_shapes=[
            pltpu.VMEM((total, LANES), jnp.float32),
            pltpu.VMEM((HELD, size, size), jnp.float32),
            pltpu.SemaphoreType.DMA((len(pieces),)),
            pltpu.SemaphoreType.DMA((HELD,)),
        ],
        compiler_params=pltpu.CompilerParams(vmem_limit_bytes=56 * 1024 * 1024),
        cost_estimate=pl.CostEstimate(
            flops=slots * 6 * size * size * LANES,
            bytes_accessed=slots * size * size * 4 + total * LANES * 4 + blocks * size * LANES * 4,
            transcendentals=0,
        ),
        name="ladder",
    )(tile_row, tile_col, tile_count, tiles, *pieces, *after)


def shift_line(block, step):
    size = lax.axis_size("cd")
    return lax.ppermute(block, "cd", [(i, (i + step) % size) for i in range(size)])


def ring_terms(partial_value):
    size = lax.axis_size("cd")
    me = lax.axis_index("cd")
    half = partial_value.shape[1] // 2

    def block_for(distance):
        return lax.dynamic_index_in_dim(
            partial_value, lax.rem(me + (distance + size), size), 0, False, allow_negative_indices=False
        )

    far = block_for(size // 2)
    up = shift_line(far[:half], 1)
    down = shift_line(far[half:], -1)
    for distance in range(size // 2 - 1, 0, -1):
        ahead = block_for(distance)
        behind = block_for(-distance)
        if distance == size // 2 - 1:
            up = jnp.concatenate([ahead[:half] + up, ahead[half:]], axis=0)
            down = jnp.concatenate([behind[:half], behind[half:] + down], axis=0)
        else:
            up = ahead + up
            down = behind + down
        up = shift_line(up, 1)
        down = shift_line(down, -1)
    return [up, down, block_for(0)], [partial_value]


def merge_kernel(*refs, terms):
    out_ref, held_ref = refs[-2:]
    start = 0
    for c in range(CHUNKS):
        value = refs[start][...]
        for ref in refs[start + 1 : start + terms[c]]:
            value = value + ref[...]
        start += terms[c]
        held_ref[...] = value
        for row in range(held_ref.shape[0] // 32):
            for a in range(2):
                for b in range(2):
                    out_ref[pl.ds(row * 64 + c * 4 + a * 2 + b, 8, stride=8), :] = held_ref[
                        pl.ds(row * 32 + a * 16 + b, 8, stride=2), :
                    ]


def merge(chunks):
    rows = chunks[0][0].shape[0]
    flat = [term for terms in chunks for term in terms]
    return pl.pallas_call(
        functools.partial(merge_kernel, terms=[len(terms) for terms in chunks]),
        in_specs=[pl.BlockSpec(memory_space=pltpu.VMEM)] * len(flat),
        out_specs=pl.BlockSpec(memory_space=pltpu.VMEM),
        out_shape=jax.ShapeDtypeStruct((CHUNKS * rows, LANES), jnp.float32),
        scratch_shapes=[pltpu.VMEM((rows, LANES), jnp.float32)],
        name="merge",
    )(*flat)


def finish_kernel(direct_ref, mirror_ref, out_ref, rows_ref):
    for o in range(CHUNKS):
        for a in range(2):
            for b in range(2):
                rows_ref[pl.ds(b, LANES, stride=2), :] = (
                    direct_ref[pl.ds(o * 4 + a * 2 + b, LANES, stride=8), :]
                    + mirror_ref[pl.ds(o * 4 + b * 2 + a, LANES, stride=8), :]
                )
            out_ref[pl.ds(o * LANES, LANES), a, :] = rows_ref[...].T


def finish(direct, mirror):
    return pl.pallas_call(
        finish_kernel,
        in_specs=[pl.BlockSpec(memory_space=pltpu.VMEM)] * 2,
        out_specs=pl.BlockSpec(memory_space=pltpu.VMEM),
        out_shape=jax.ShapeDtypeStruct((CHUNKS * LANES, 2, 2 * LANES), jnp.float32),
        scratch_shapes=[pltpu.VMEM((2 * LANES, LANES), jnp.float32)],
        name="finish",
    )(direct, mirror)


def per_device(amplitudes, integrals, tile_row, tile_col, tile_count):
    occ_dev = amplitudes.shape[0]
    blocks = lax.axis_size("ab")

    def partial_of(pieces, after):
        return ladder(tile_row, tile_col, tile_count, after, integrals, pieces, blocks)

    first, second = amplitudes[:LANES].T, amplitudes[LANES:].T
    pieces = [lax.all_gather(second, "ab", axis=0, tiled=True)]
    terms, after = ring_terms(partial_of(gather_plane(first), []))
    summed = lax.psum_scatter(partial_of(pieces, after), "cd", scatter_dimension=0, tiled=True)
    direct = merge([terms, [summed[0]]])
    outgoing = direct.reshape(-1, 8, LANES)
    arrived = lax.all_to_all(outgoing, ("ab", "cd"), split_axis=0, concat_axis=0, tiled=True)
    partner = lax.ppermute(arrived, "ij", [(0, 1), (1, 0)]).reshape(direct.shape)
    return finish(direct, partner).reshape(occ_dev, 1, 2, 2 * LANES)


def solution(mesh):
    in_specs = (
        P("ij", ("cd", "ab")),
        P(("ab", "cd"), None, None),
        P(("ab", "cd")),
        P(("ab", "cd")),
        P(("ab", "cd")),
    )
    out_specs = P("ij", "ab", "cd", None)
    return jax.shard_map(
        per_device, mesh=mesh, in_specs=in_specs, out_specs=out_specs, check_vma=False
    )
```

time: 194 us -> 185 us (0.954)
  starting transfers between devices: 22.9 us -> 40.4 us
  waiting for transfers between devices: 81.6 us -> 67.9 us
  Pallas kernels: 36.2 us -> 26.3 us
  blocking collectives: 30.3 us -> 28.1 us
    reduce_scatter x1, waiting for transfers between devices: 62.2 us -> 0.01 us  [per_device(): lax.psum_scatter(partial_of(pieces, after), 'cd', scatter_dimension=0, ti...]
    ppermute x17 -> x23, waiting for transfers between devices: 19.4 us -> 54.7 us  [the longest x8 36.9 us: shift_line(): lax.ppermute(block, 'cd', [(i, (i + step) % size) for i in range(size)])]
    ppermute x17 -> x23, starting transfers between devices: 22.9 us -> 40.3 us  [the longest x8 12.4 us: shift_line(): lax.ppermute(block, 'cd', [(i, (i + step) % size) for i in range(size)])]
    all_gather x0 -> x1, waiting for transfers between devices: none -> 13.2 us  [per_device(): pieces = [lax.all_gather(second, 'ab', axis=0, tiled=True)]]
    pallas_call x2 -> x3, Pallas kernels: 33.9 us -> 24 us  [the longest x2 21.8 us: ladder(): pl.pallas_call(functools.partial(ladder_kernel, pieces_given=len(pieces))...]
    all_to_all x1, blocking collectives: 30.3 us -> 28.1 us  [per_device(): lax.all_to_all(outgoing, ('ab', 'cd'), split_axis=0, concat_axis=0, tiled...]
    unnamed x13 -> x30, local copies, waits for them, and re-layouts: 4.18 us -> 4.93 us
  transfers between devices with their start and end apart: 18 -> 25, of which waited for: 10 -> 14; matrix products, arithmetic and copies ran while one was open for 1% -> 1% of each run, Pallas kernels for 9% -> 6%
where the time goes in v2:
time: 185 us; the launch traced here: 184 us
  waiting for transfers between devices  67.9 us (37%)
  starting transfers between devices  40.4 us (22%)
  blocking collectives  28.1 us (15%)
  Pallas kernels  26.3 us (14%)
  between operations  14.3 us (8%)
  local copies, waits for them, and re-layouts  6.85 us (4%)
    ppermute x8, waiting for transfers between devices, shift_line(): lax.ppermute(block, 'cd', [(i, (i + step) % size) for i in range(size)])  36.9 us
    all_to_all x1, blocking collectives, per_device(): lax.all_to_all(outgoing, ('ab', 'cd'), split_axis=0, concat_axis=0, tiled...  28.1 us
    pallas_call x2, Pallas kernels, ladder(): pl.pallas_call(functools.partial(ladder_kernel, pieces_given=len(pieces))...  21.8 us
    all_gather x1, waiting for transfers between devices, per_device(): pieces = [lax.all_gather(second, 'ab', axis=0, tiled=True)]  13.2 us
    ppermute x8, starting transfers between devices, shift_line(): lax.ppermute(block, 'cd', [(i, (i + step) % size) for i in range(size)])  12.4 us
    ppermute x4, waiting for transfers between devices, both_ways(): lax.ppermute(block, 'ab', plane_route(dx, dy))  10.6 us
    ppermute x1, starting transfers between devices, per_device(): lax.ppermute(arrived, 'ij', [(0, 1), (1, 0)]).reshape(direct.shape)  6.7 us
    ppermute x4, starting transfers between devices, both_ways(): lax.ppermute(block, 'ab', plane_route(-dx, -dy))  6.42 us
  transfers between devices with their start and end apart: 25, of which 14 were waited for; matrix products, arithmetic and copies ran while one was open for 1% of the time, Pallas kernels for 6%

profile of v2, /device:TPU:1, one launch (start us, length us, event | category | flops | bytes accessed | tf_op | source)
XLA Modules:
  0.0 184.1 jit_solution(9684308025438291928)
XLA Ops:
  6.5 1.1 fusion.2
  7.6 0.8 copy.10
  8.5 0.1 copy.9
  8.7 2.2 %collective-permute-start.7 = (f32[256,128]{1,0:T(8,128)S(1)}, f32[256,128]{1,0:T(8,128)S(1)}, u32[]{:S(2)}, u32[]{:S(2)}) collective-permute-start(f32[256,128]{1,0:T(8,128)S(1)} %get-tuple-element.15), channel_id=1, source_target_pairs={{0,64},{16,80},{32,96},{48,112},{64,128},{80,144},{96,160},{112,17... | collective-permute-start | bytes 393224 | tf_op jit(solution)/shard_map/ppermute | solution.py:27
  10.9 1.5 collective-permute-start.8
  12.4 1.6 collective-permute-start.9
  14.0 1.2 collective-permute-start
  15.2 1.5 collective-permute-start.1
  16.6 1.5 collective-permute-start.2
  18.2 0.5 collective-permute-done.9
  18.8 2.0 %collective-permute-start.10 = (f32[1024,128]{1,0:T(8,128)S(1)}, f32[1024,128]{1,0:T(8,128)S(1)}, u32[]{:S(2)}, u32[]{:S(2)}) collective-permute-start(f32[1024,128]{1,0:T(8,128)S(1)} %pad_maximum_fusion.1.rest_5_), channel_id=1, source_target_pairs={{0,16},{16,32},{32,48},{48,0},{64,80},{80,96},{96,112},{112,64},{1... | collective-permute-start | bytes 1572872 | tf_op jit(solution)/shard_map/ppermute | solution.py:27
  20.7 1.4 collective-permute-start.11
  22.1 1.4 collective-permute-done.2
  23.5 0.7 collective-permute-start.3
  24.2 2.1 %collective-permute-start.4 = (f32[1024,128]{1,0:T(8,128)S(1)}, f32[1024,128]{1,0:T(8,128)S(1)}, u32[]{:S(2)}, u32[]{:S(2)}) collective-permute-start(f32[1024,128]{1,0:T(8,128)S(1)} %pad_maximum_fusion.rest_0_), channel_id=1, source_target_pairs={{0,192},{16,208},{32,224},{48,240},{64,0},{80,16},{96,32},{112,48}... | collective-permute-start | bytes 1572872 | tf_op jit(solution)/shard_map/ppermute | solution.py:28
  26.3 10.6 %collective-permute-done.10.rest_6_ = f32[1024,128]{1,0:T(8,128)S(1)} collective-permute-done((f32[1024,128]{1,0:T(8,128)S(1)}, f32[1024,128]{1,0:T(8,128)S(1)}, u32[]{:S(2)}, u32[]{:S(2)}) %collective-permute-start.10) | collective-permute-done | bytes 524320 | tf_op jit(solution)/shard_map/ppermute | solution.py:27
  36.9 1.0 collective-permute-start.12
  37.9 1.9 %collective-permute-start.13 = (f32[512,128]{1,0:T(8,128)S(1)}, f32[512,128]{1,0:T(8,128)S(1)}, u32[]{:S(2)}, u32[]{:S(2)}) collective-permute-start(f32[512,128]{1,0:T(8,128)S(1)} %slice.85), channel_id=1, source_target_pairs={{0,48},{16,0},{32,16},{48,32},{64,112},{80,64},{96,80},{112,96},{1... | collective-permute-start | bytes 786440 | tf_op jit(solution)/shard_map/ppermute | solution.py:37
  39.8 1.5 collective-permute-start.5
  41.3 1.3 collective-permute-start.6
  43.3 0.1 collective-permute-done.12.rest_8_
  43.4 0.6 collective-permute-done.13.rest_9_
  44.0 2.5 %collective-permute-done.5.rest_3_ = f32[512,128]{1,0:T(8,128)S(1)} collective-permute-done((f32[512,128]{1,0:T(8,128)S(1)}, f32[512,128]{1,0:T(8,128)S(1)}, u32[]{:S(2)}, u32[]{:S(2)}) %collective-permute-start.5) | collective-permute-done | bytes 262176 | tf_op jit(solution)/shard_map/ppermute | solution.py:36
  46.6 0.5 collective-permute-done.6.rest_4_
  47.1 0.2 copy-done.10
  47.3 0.7 copy-done.11
  48.0 11.0 %ladder.2.rest_1_ = f32[8,512,128]{2,1,0:T(8,128)} custom-call(s32[46]{0:T(128)} %row_ref.3, s32[46]{0:T(128)} %col_ref.3, s32[1]{0:T(128)S(6)} %copy.11.count_ref, f32[46,256,256]{2,1,0:T(8,128)} %tiles_ref.3, f32[1024,128]{1,0:T(8,128)} %copy-done.2, f32[1024,128]{1,0:T(8,128)} %copy-done.5, f32[1024,128]{1,0:T(8,128)} %copy-done.6, ...), custom_call_target="tpu_custom_call" | custom-call | flops 2315255808 | bytes 18350080 | tf_op jit(solution)/shard_map/ladder/pallas_call | solution.py:146
  59.0 13.2 %all-gather.2.cloned.1.call-done.rest_0_ = f32[8192,128]{1,0:T(8,128)} async-done(((f32[512,128]{1,0:T(8,128)}), f32[8192,128]{1,0:T(8,128)}) %all-gather.2.cloned.1.call-update) | async-done | bytes 4194320 | tf_op jit(solution)/shard_map/all_gather | solution.py:259
  72.2 10.8 %ladder.3 = f32[8,512,128]{2,1,0:T(8,128)} custom-call(s32[46]{0:T(128)} %row_ref.3, s32[46]{0:T(128)} %col_ref.3, s32[1]{0:T(128)S(6)} %copy.11.count_ref, f32[46,256,256]{2,1,0:T(8,128)} %tiles_ref.3, f32[8192,128]{1,0:T(8,128)} %all-gather.2.cloned.1.call-done.rest_0_, f32[8,512,128]{2,1,0:T(8,128)} %ladder.2.rest_1_), custom_call_target="tpu_custom_call" | custom-call | flops 2315255808 | bytes 18350080 | tf_op jit(solution)/shard_map/ladder/pallas_call | solution.py:146
  83.0 1.5 copy-done
  84.7 2.7 %collective-permute-start.18 = (f32[256,128]{1,0:T(8,128)S(1)}, f32[256,128]{1,0:T(8,128)S(1)}, u32[]{:S(2)}, u32[]{:S(2)}) collective-permute-start(f32[256,128]{1,0:T(8,128)S(1)} %get-tuple-element.9), channel_id=1, source_target_pairs={{0,14},{2,0},{4,2},{6,4},{8,6},{10,8},{12,10},{14,12},{1,15},{3,1}... | collective-permute-start | bytes 393224 | tf_op jit(solution)/shard_map/ppermute | solution.py:169
  87.4 2.9 %collective-permute-done.14 = f32[256,128]{1,0:T(8,128)S(1)} collective-permute-done((f32[256,128]{1,0:T(8,128)S(1)}, f32[256,128]{1,0:T(8,128)S(1)}, u32[]{:S(2)}, u32[]{:S(2)}) %collective-permute-start.14) | collective-permute-done | bytes 131104 | tf_op jit(solution)/shard_map/ppermute | solution.py:169
  90.4 2.2 %collective-permute-start.19 = (f32[512,128]{1,0:T(8,128)S(1)}, f32[512,128]{1,0:T(8,128)S(1)}, u32[]{:S(2)}, u32[]{:S(2)}) collective-permute-start(f32[512,128]{1,0:T(8,128)S(1)} %pad_maximum_fusion.3), channel_id=1, source_target_pairs={{0,14},{2,0},{4,2},{6,4},{8,6},{10,8},{12,10},{14,12},{1,15},{3,1}... | collective-permute-start | bytes 786440 | tf_op jit(solution)/shard_map/ppermute | solution.py:169
  92.7 8.6 %collective-permute-done.19 = f32[512,128]{1,0:T(8,128)S(1)} collective-permute-done((f32[512,128]{1,0:T(8,128)S(1)}, f32[512,128]{1,0:T(8,128)S(1)}, u32[]{:S(2)}, u32[]{:S(2)}) %collective-permute-start.19) | collective-permute-done | bytes 262176 | tf_op jit(solution)/shard_map/ppermute | solution.py:169
  101.3 3.6 %collective-permute-start.20 = (f32[512,128]{1,0:T(8,128)S(1)}, f32[512,128]{1,0:T(8,128)S(1)}, u32[]{:S(2)}, u32[]{:S(2)}) collective-permute-start(f32[512,128]{1,0:T(8,128)S(1)} %bitcast_add_fusion), channel_id=1, source_target_pairs={{0,14},{2,0},{4,2},{6,4},{8,6},{10,8},{12,10},{14,12},{1,15},{3,1}... | collective-permute-start | bytes 786440 | tf_op jit(solution)/shard_map/ppermute | solution.py:169
  104.9 9.9 %collective-permute-done.20 = f32[512,128]{1,0:T(8,128)S(1)} collective-permute-done((f32[512,128]{1,0:T(8,128)S(1)}, f32[512,128]{1,0:T(8,128)S(1)}, u32[]{:S(2)}, u32[]{:S(2)}) %collective-permute-start.20) | collective-permute-done | bytes 262176 | tf_op jit(solution)/shard_map/ppermute | solution.py:169
  114.9 0.1 collective-permute-start.16
  114.9 3.6 %collective-permute-start.21 = (f32[512,128]{1,0:T(8,128)S(1)}, f32[512,128]{1,0:T(8,128)S(1)}, u32[]{:S(2)}, u32[]{:S(2)}) collective-permute-start(f32[512,128]{1,0:T(8,128)S(1)} %get-tuple-element.5), channel_id=1, source_target_pairs={{0,14},{2,0},{4,2},{6,4},{8,6},{10,8},{12,10},{14,12},{1,15},{3,1}... | collective-permute-start | bytes 786440 | tf_op jit(solution)/shard_map/ppermute | solution.py:169
  118.5 9.8 %collective-permute-done.16 = f32[512,128]{1,0:T(8,128)S(1)} collective-permute-done((f32[512,128]{1,0:T(8,128)S(1)}, f32[512,128]{1,0:T(8,128)S(1)}, u32[]{:S(2)}, u32[]{:S(2)}) %collective-permute-start.16) | collective-permute-done | bytes 262176 | tf_op jit(solution)/shard_map/ppermute | solution.py:169
  128.5 0.7 dynamic-slice_bitcast_fusion.refs_2_
  129.2 5.7 %collective-permute-done.17.refs_0_ = f32[512,128]{1,0:T(8,128)S(1)} collective-permute-done((f32[512,128]{1,0:T(8,128)S(1)}, f32[512,128]{1,0:T(8,128)S(1)}, u32[]{:S(2)}, u32[]{:S(2)}) %collective-permute-start.17) | collective-permute-done | bytes 262176 | tf_op jit(solution)/shard_map/ppermute | solution.py:169
  134.9 0.7 copy-done.13
  135.6 2.1 %merge.1.direct_ref = f32[1024,128]{1,0:T(8,128)} custom-call(f32[512,128]{1,0:T(8,128)} %copy-done.13, f32[512,128]{1,0:T(8,128)} %copy-done.12, f32[512,128]{1,0:T(8,128)} %dynamic-slice_bitcast_fusion.refs_2_, f32[512,128]{1,0:T(8,128)} %bitcast.38), custom_call_target="tpu_custom_call" | custom-call | tf_op jit(solution)/shard_map/merge/pallas_call | solution.py:219
  137.7 28.1 %all_to_all.5 = f32[128,8,128]{2,1,0:T(8,128)S(1)} all-to-all(f32[128,8,128]{2,1,0:T(8,128)} %bitcast.34), channel_id=1, replica_groups=mesh['ab'=16,'cd'=8,'ij'=2] {'ab','cd'}, dimensions={0} | all-to-all | bytes 1048576 | tf_op jit(solution)/shard_map/all_to_all | solution.py:264
  165.8 6.7 %collective-permute-start.22 = (f32[128,8,128]{2,1,0:T(8,128)S(1)}, f32[128,8,128]{2,1,0:T(8,128)S(1)}, u32[]{:S(2)}, u32[]{:S(2)}) collective-permute-start(f32[128,8,128]{2,1,0:T(8,128)S(1)} %all_to_all.5), channel_id=1, source_target_pairs={{0,1},{1,0},{2,3},{3,2},{4,5},{5,4},{6,7},{7,6},{8,9},{9,8},{10,11... | collective-permute-start | bytes 1572872 | tf_op jit(solution)/shard_map/ppermute | solution.py:265
  172.5 1.5 collective-permute-done.22
  174.1 0.8 copy-done.7
  174.9 2.3 %finish.1 = f32[256,2,256]{2,1,0:T(2,128)} custom-call(f32[1024,128]{1,0:T(8,128)} %merge.1.direct_ref, f32[1024,128]{1,0:T(8,128)} %bitcast.37), custom_call_target="tpu_custom_call" | custom-call | tf_op jit(solution)/shard_map/finish/pallas_call | solution.py:241
  (55 shorter events, 0.8 us)
Async XLA Ops:
  6.5 65.7 %all-gather.2.cloned.1.call-start = ((), (), s32[]{:S(2)}) async-start(), calls=%async_computation.2 | async-start | bytes 4456448 | tf_op jit(solution)/shard_map/all_gather | solution.py:259
  8.5 126.4 %reduce-scatter.2.cloned.1.call-start = ((), (), s32[]{:S(2)}) async-start(), calls=%async_computation.3 | async-start | bytes 2359296 | tf_op jit(solution)/shard_map/reduce_scatter | solution.py:261
  8.7 8.0 %collective-permute-start.7 = (f32[256,128]{1,0:T(8,128)S(1)}, f32[256,128]{1,0:T(8,128)S(1)}, u32[]{:S(2)}, u32[]{:S(2)}) collective-permute-start(f32[256,128]{1,0:T(8,128)S(1)} %get-tuple-element.15), channel_id=1, source_target_pairs={{0,64},{16,80},{32,96},{48,112},{64,128},{80,144},{96,160},{112,17... | collective-permute-start | bytes 393224 | tf_op jit(solution)/shard_map/ppermute | solution.py:27
  10.9 7.3 %collective-permute-start.8 = (f32[256,128]{1,0:T(8,128)S(1)}, f32[256,128]{1,0:T(8,128)S(1)}, u32[]{:S(2)}, u32[]{:S(2)}) collective-permute-start(f32[256,128]{1,0:T(8,128)S(1)} %get-tuple-element.15), channel_id=1, source_target_pairs={{0,192},{16,208},{32,224},{48,240},{64,0},{80,16},{96,32},{112,48}... | collective-permute-start | bytes 393224 | tf_op jit(solution)/shard_map/ppermute | solution.py:28
  12.4 6.3 %collective-permute-start.9 = (f32[256,128]{1,0:T(8,128)S(1)}, f32[256,128]{1,0:T(8,128)S(1)}, u32[]{:S(2)}, u32[]{:S(2)}) collective-permute-start(f32[256,128]{1,0:T(8,128)S(1)} %get-tuple-element.15), channel_id=1, source_target_pairs={{0,128},{16,144},{32,160},{48,176},{64,192},{80,208},{96,224},{112... | collective-permute-start | bytes 393224 | tf_op jit(solution)/shard_map/ppermute | solution.py:47
  14.0 8.1 %collective-permute-start = (f32[256,128]{1,0:T(8,128)S(1)}, f32[256,128]{1,0:T(8,128)S(1)}, u32[]{:S(2)}, u32[]{:S(2)}) collective-permute-start(f32[256,128]{1,0:T(8,128)S(1)} %get-tuple-element.16), channel_id=1, source_target_pairs={{0,16},{16,32},{32,48},{48,0},{64,80},{80,96},{96,112},{112,64},{1... | collective-permute-start | bytes 393224 | tf_op jit(solution)/shard_map/ppermute | solution.py:27
  15.2 6.9 %collective-permute-start.1 = (f32[256,128]{1,0:T(8,128)S(1)}, f32[256,128]{1,0:T(8,128)S(1)}, u32[]{:S(2)}, u32[]{:S(2)}) collective-permute-start(f32[256,128]{1,0:T(8,128)S(1)} %get-tuple-element.16), channel_id=1, source_target_pairs={{0,48},{16,0},{32,16},{48,32},{64,112},{80,64},{96,80},{112,96},{1... | collective-permute-start | bytes 393224 | tf_op jit(solution)/shard_map/ppermute | solution.py:28
  16.6 6.8 %collective-permute-start.2 = (f32[256,128]{1,0:T(8,128)S(1)}, f32[256,128]{1,0:T(8,128)S(1)}, u32[]{:S(2)}, u32[]{:S(2)}) collective-permute-start(f32[256,128]{1,0:T(8,128)S(1)} %get-tuple-element.16), channel_id=1, source_target_pairs={{0,32},{16,48},{32,0},{48,16},{64,96},{80,112},{96,64},{112,80},{1... | collective-permute-start | bytes 393224 | tf_op jit(solution)/shard_map/ppermute | solution.py:47
  18.7 28.3 %copy-start.1 = (f32[1024,128]{1,0:T(8,128)}, f32[1024,128]{1,0:T(8,128)S(1)}, u32[]{:S(2)}) copy-start(f32[1024,128]{1,0:T(8,128)S(1)} %pad_maximum_fusion.1.rest_5_) | copy-start | bytes 1572868
  18.8 18.1 %collective-permute-start.10 = (f32[1024,128]{1,0:T(8,128)S(1)}, f32[1024,128]{1,0:T(8,128)S(1)}, u32[]{:S(2)}, u32[]{:S(2)}) collective-permute-start(f32[1024,128]{1,0:T(8,128)S(1)} %pad_maximum_fusion.1.rest_5_), channel_id=1, source_target_pairs={{0,16},{16,32},{32,48},{48,0},{64,80},{80,96},{96,112},{112,64},{1... | collective-permute-start | bytes 1572872 | tf_op jit(solution)/shard_map/ppermute | solution.py:27
  20.7 17.1 %collective-permute-start.11 = (f32[1024,128]{1,0:T(8,128)S(1)}, f32[1024,128]{1,0:T(8,128)S(1)}, u32[]{:S(2)}, u32[]{:S(2)}) collective-permute-start(f32[1024,128]{1,0:T(8,128)S(1)} %pad_maximum_fusion.1.rest_5_), channel_id=1, source_target_pairs={{0,48},{16,0},{32,16},{48,32},{64,112},{80,64},{96,80},{112,96},{1... | collective-permute-start | bytes 1572872 | tf_op jit(solution)/shard_map/ppermute | solution.py:28
  23.5 23.6 %copy-start.2 = (f32[1024,128]{1,0:T(8,128)}, f32[1024,128]{1,0:T(8,128)S(1)}, u32[]{:S(2)}) copy-start(f32[1024,128]{1,0:T(8,128)S(1)} %pad_maximum_fusion.rest_0_) | copy-start | bytes 1572868
  23.5 16.2 %collective-permute-start.3 = (f32[1024,128]{1,0:T(8,128)S(1)}, f32[1024,128]{1,0:T(8,128)S(1)}, u32[]{:S(2)}, u32[]{:S(2)}) collective-permute-start(f32[1024,128]{1,0:T(8,128)S(1)} %pad_maximum_fusion.rest_0_), channel_id=1, source_target_pairs={{0,64},{16,80},{32,96},{48,112},{64,128},{80,144},{96,160},{112,17... | collective-permute-start | bytes 1572872 | tf_op jit(solution)/shard_map/ppermute | solution.py:27
  24.2 17.1 %collective-permute-start.4 = (f32[1024,128]{1,0:T(8,128)S(1)}, f32[1024,128]{1,0:T(8,128)S(1)}, u32[]{:S(2)}, u32[]{:S(2)}) collective-permute-start(f32[1024,128]{1,0:T(8,128)S(1)} %pad_maximum_fusion.rest_0_), channel_id=1, source_target_pairs={{0,192},{16,208},{32,224},{48,240},{64,0},{80,16},{96,32},{112,48}... | collective-permute-start | bytes 1572872 | tf_op jit(solution)/shard_map/ppermute | solution.py:28
  36.9 10.2 %copy-start.3 = (f32[1024,128]{1,0:T(8,128)}, f32[1024,128]{1,0:T(8,128)S(1)}, u32[]{:S(2)}) copy-start(f32[1024,128]{1,0:T(8,128)S(1)} %collective-permute-done.10.rest_6_) | copy-start | bytes 1572868
  36.9 6.5 %collective-permute-start.12 = (f32[512,128]{1,0:T(8,128)S(1)}, f32[512,128]{1,0:T(8,128)S(1)}, u32[]{:S(2)}, u32[]{:S(2)}) collective-permute-start(f32[512,128]{1,0:T(8,128)S(1)} %slice.84), channel_id=1, source_target_pairs={{0,16},{16,32},{32,48},{48,0},{64,80},{80,96},{96,112},{112,64},{1... | collective-permute-start | bytes 786440 | tf_op jit(solution)/shard_map/ppermute | solution.py:36
  37.9 9.2 %copy-start.4 = (f32[1024,128]{1,0:T(8,128)}, f32[1024,128]{1,0:T(8,128)S(1)}, u32[]{:S(2)}) copy-start(f32[1024,128]{1,0:T(8,128)S(1)} %collective-permute-done.11.rest_7_) | copy-start | bytes 1572868
  37.9 6.2 %collective-permute-start.13 = (f32[512,128]{1,0:T(8,128)S(1)}, f32[512,128]{1,0:T(8,128)S(1)}, u32[]{:S(2)}, u32[]{:S(2)}) collective-permute-start(f32[512,128]{1,0:T(8,128)S(1)} %slice.85), channel_id=1, source_target_pairs={{0,48},{16,0},{32,16},{48,32},{64,112},{80,64},{96,80},{112,96},{1... | collective-permute-start | bytes 786440 | tf_op jit(solution)/shard_map/ppermute | solution.py:37
  39.8 7.3 %copy-start.5 = (f32[1024,128]{1,0:T(8,128)}, f32[1024,128]{1,0:T(8,128)S(1)}, u32[]{:S(2)}) copy-start(f32[1024,128]{1,0:T(8,128)S(1)} %collective-permute-done.3.rest_1_) | copy-start | bytes 1572868
  39.8 6.8 %collective-permute-start.5 = (f32[512,128]{1,0:T(8,128)S(1)}, f32[512,128]{1,0:T(8,128)S(1)}, u32[]{:S(2)}, u32[]{:S(2)}) collective-permute-start(f32[512,128]{1,0:T(8,128)S(1)} %slice.81), channel_id=1, source_target_pairs={{0,64},{16,80},{32,96},{48,112},{64,128},{80,144},{96,160},{112,17... | collective-permute-start | bytes 786440 | tf_op jit(solution)/shard_map/ppermute | solution.py:36
  41.3 5.8 %copy-start.6 = (f32[1024,128]{1,0:T(8,128)}, f32[1024,128]{1,0:T(8,128)S(1)}, u32[]{:S(2)}) copy-start(f32[1024,128]{1,0:T(8,128)S(1)} %collective-permute-done.4.rest_2_) | copy-start | bytes 1572868
  41.3 5.8 %collective-permute-start.6 = (f32[512,128]{1,0:T(8,128)S(1)}, f32[512,128]{1,0:T(8,128)S(1)}, u32[]{:S(2)}, u32[]{:S(2)}) collective-permute-start(f32[512,128]{1,0:T(8,128)S(1)} %slice.82), channel_id=1, source_target_pairs={{0,192},{16,208},{32,224},{48,240},{64,0},{80,16},{96,32},{112,48}... | collective-permute-start | bytes 786440 | tf_op jit(solution)/shard_map/ppermute | solution.py:37
  43.4 3.7 %copy-start.8 = (f32[512,128]{1,0:T(8,128)}, f32[512,128]{1,0:T(8,128)S(1)}, u32[]{:S(2)}) copy-start(f32[512,128]{1,0:T(8,128)S(1)} %collective-permute-done.12.rest_8_) | copy-start | bytes 786436
  44.0 3.1 %copy-start.9 = (f32[512,128]{1,0:T(8,128)}, f32[512,128]{1,0:T(8,128)S(1)}, u32[]{:S(2)}) copy-start(f32[512,128]{1,0:T(8,128)S(1)} %collective-permute-done.13.rest_9_) | copy-start | bytes 786436
  46.6 0.7 copy-start.10
  47.3 0.7 copy-start.11
  83.0 1.6 copy-start
  84.6 5.7 %collective-permute-start.14 = (f32[256,128]{1,0:T(8,128)S(1)}, f32[256,128]{1,0:T(8,128)S(1)}, u32[]{:S(2)}, u32[]{:S(2)}) collective-permute-start(f32[256,128]{1,0:T(8,128)S(1)} %get-tuple-element.8), channel_id=1, source_target_pairs={{0,2},{2,4},{4,6},{6,8},{8,10},{10,12},{12,14},{14,0},{1,3},{3,5},... | collective-permute-start | bytes 393224 | tf_op jit(solution)/shard_map/ppermute | solution.py:169
  84.7 5.6 %collective-permute-start.18 = (f32[256,128]{1,0:T(8,128)S(1)}, f32[256,128]{1,0:T(8,128)S(1)}, u32[]{:S(2)}, u32[]{:S(2)}) collective-permute-start(f32[256,128]{1,0:T(8,128)S(1)} %get-tuple-element.9), channel_id=1, source_target_pairs={{0,14},{2,0},{4,2},{6,4},{8,6},{10,8},{12,10},{14,12},{1,15},{3,1}... | collective-permute-start | bytes 393224 | tf_op jit(solution)/shard_map/ppermute | solution.py:169
  90.4 10.9 %collective-permute-start.19 = (f32[512,128]{1,0:T(8,128)S(1)}, f32[512,128]{1,0:T(8,128)S(1)}, u32[]{:S(2)}, u32[]{:S(2)}) collective-permute-start(f32[512,128]{1,0:T(8,128)S(1)} %pad_maximum_fusion.3), channel_id=1, source_target_pairs={{0,14},{2,0},{4,2},{6,4},{8,6},{10,8},{12,10},{14,12},{1,15},{3,1}... | collective-permute-start | bytes 786440 | tf_op jit(solution)/shard_map/ppermute | solution.py:169
  92.6 12.3 %collective-permute-start.15 = (f32[512,128]{1,0:T(8,128)S(1)}, f32[512,128]{1,0:T(8,128)S(1)}, u32[]{:S(2)}, u32[]{:S(2)}) collective-permute-start(f32[512,128]{1,0:T(8,128)S(1)} %pad_maximum_fusion.2), channel_id=1, source_target_pairs={{0,2},{2,4},{4,6},{6,8},{8,10},{10,12},{12,14},{14,0},{1,3},{3,5},... | collective-permute-start | bytes 786440 | tf_op jit(solution)/shard_map/ppermute | solution.py:169
  101.3 13.5 %collective-permute-start.20 = (f32[512,128]{1,0:T(8,128)S(1)}, f32[512,128]{1,0:T(8,128)S(1)}, u32[]{:S(2)}, u32[]{:S(2)}) collective-permute-start(f32[512,128]{1,0:T(8,128)S(1)} %bitcast_add_fusion), channel_id=1, source_target_pairs={{0,14},{2,0},{4,2},{6,4},{8,6},{10,8},{12,10},{14,12},{1,15},{3,1}... | collective-permute-start | bytes 786440 | tf_op jit(solution)/shard_map/ppermute | solution.py:169
  114.9 13.5 %collective-permute-start.16 = (f32[512,128]{1,0:T(8,128)S(1)}, f32[512,128]{1,0:T(8,128)S(1)}, u32[]{:S(2)}, u32[]{:S(2)}) collective-permute-start(f32[512,128]{1,0:T(8,128)S(1)} %get-tuple-element.6), channel_id=1, source_target_pairs={{0,2},{2,4},{4,6},{6,8},{8,10},{10,12},{12,14},{14,0},{1,3},{3,5},... | collective-permute-start | bytes 786440 | tf_op jit(solution)/shard_map/ppermute | solution.py:169
  114.9 14.3 %collective-permute-start.21 = (f32[512,128]{1,0:T(8,128)S(1)}, f32[512,128]{1,0:T(8,128)S(1)}, u32[]{:S(2)}, u32[]{:S(2)}) collective-permute-start(f32[512,128]{1,0:T(8,128)S(1)} %get-tuple-element.5), channel_id=1, source_target_pairs={{0,14},{2,0},{4,2},{6,4},{8,6},{10,8},{12,10},{14,12},{1,15},{3,1}... | collective-permute-start | bytes 786440 | tf_op jit(solution)/shard_map/ppermute | solution.py:169
  128.4 6.5 %collective-permute-start.17 = (f32[512,128]{1,0:T(8,128)S(1)}, f32[512,128]{1,0:T(8,128)S(1)}, u32[]{:S(2)}, u32[]{:S(2)}) collective-permute-start(f32[512,128]{1,0:T(8,128)S(1)} %bitcast_add_fusion.3), channel_id=1, source_target_pairs={{0,2},{2,4},{4,6},{6,8},{8,10},{10,12},{12,14},{14,0},{1,3},{3,5},... | collective-permute-start | bytes 786440 | tf_op jit(solution)/shard_map/ppermute | solution.py:169
  129.2 5.7 %copy-start.12 = (f32[512,128]{1,0:T(8,128)}, f32[512,128]{1,0:T(8,128)S(1)}, u32[]{:S(2)}) copy-start(f32[512,128]{1,0:T(8,128)S(1)} %collective-permute-done.21.refs_1_) | copy-start | bytes 786436
  134.9 0.7 copy-start.13
  165.8 8.2 %collective-permute-start.22 = (f32[128,8,128]{2,1,0:T(8,128)S(1)}, f32[128,8,128]{2,1,0:T(8,128)S(1)}, u32[]{:S(2)}, u32[]{:S(2)}) collective-permute-start(f32[128,8,128]{2,1,0:T(8,128)S(1)} %all_to_all.5), channel_id=1, source_target_pairs={{0,1},{1,0},{2,3},{3,2},{4,5},{5,4},{6,7},{7,6},{8,9},{9,8},{10,11... | collective-permute-start | bytes 1572872 | tf_op jit(solution)/shard_map/ppermute | solution.py:265
  174.1 0.8 copy-start.7
Sparse Core Ops, SparseCore 0:
  9.8 62.3 all-gather.1
  83.2 47.5 reduce-scatter.1

commit v3 on v2

v3 whole, which is shorter than its diff:
```python
import functools

import jax
import jax.numpy as jnp
from jax import lax
from jax.experimental import pallas as pl
from jax.experimental.pallas import tpu as pltpu
from jax.sharding import PartitionSpec as P

LANES = 128
SIDE = 4
CHUNKS = 2
HELD = 16
GROUP = 2


def plane_route(dx, dy):
    route = []
    for y in range(SIDE):
        for x in range(SIDE):
            route.append((y * SIDE + x, (y + dy) % SIDE * SIDE + (x + dx) % SIDE))
    return route


def both_ways(block, dx, dy):
    return [
        lax.ppermute(block, "ab", plane_route(dx, dy)),
        lax.ppermute(block, "ab", plane_route(-dx, -dy)),
    ]


def far_halves(pair, dx, dy):
    below, above = pair
    half = below.shape[0] // 2
    return [
        lax.ppermute(below[:half], "ab", plane_route(dx, dy)),
        lax.ppermute(above[half:], "ab", plane_route(-dx, -dy)),
    ]


def first_line(block, dx, dy):
    far = lax.ppermute(block, "ab", plane_route(2 * dx, 2 * dy))
    return jnp.concatenate([block] + both_ways(block, dx, dy) + [far], axis=0)


def gather_plane(block):
    half = block.shape[0] // 2
    along_x, along_y = (1, 0), (0, 1)
    low = first_line(block[:half], *along_x)
    up = first_line(block[half:], *along_y)
    near_low = both_ways(low, *along_y)
    near_up = both_ways(up, *along_x)
    pieces = [low] + near_low + far_halves(near_low, *along_y)
    return pieces + [up] + near_up + far_halves(near_up, *along_x)


def place_in_line(offset):
    return jnp.where(offset == 0, 0, jnp.where(offset == 1, 2, jnp.where(offset == 2, 3, 1)))


def out_parts(rows, size):
    half = rows // 2
    parts = [(size // 2, 0, half), (size // 2, half, half)]
    for distance in range(size // 2 - 1, 0, -1):
        parts += [(distance, 0, rows), (-distance, 0, rows)]
    return parts + [(0, 0, rows)]


def ladder_kernel(row_ref, col_ref, count_ref, tiles_ref, *rest, pieces_given, outs_given):
    pieces = rest[:pieces_given]
    outs = rest[pieces_given : pieces_given + outs_given]
    amp_ref, held_ref, acc_ref, amp_sem, held_sem, out_sem = rest[pieces_given + outs_given :]
    size = tiles_ref.shape[-1]
    count = count_ref[0]
    copies = []
    start = 0
    for i, piece in enumerate(pieces):
        rows = piece.shape[0]
        copies.append(pltpu.make_async_copy(piece, amp_ref.at[pl.ds(start, rows)], amp_sem.at[i]))
        start += rows
    for copy in copies:
        copy.start()

    def tile_copy(k):
        spot = lax.rem(k, HELD)
        return pltpu.make_async_copy(tiles_ref.at[k], held_ref.at[spot], held_sem.at[spot])

    def fetch(k):
        @pl.when(k < count)
        def _():
            tile_copy(k).start()

    for k in range(HELD):
        fetch(k)
    acc_ref[...] = jnp.zeros_like(acc_ref)
    for copy in copies:
        copy.wait()
    me = lax.axis_index("ab")
    my_y = me // SIDE
    my_x = me % SIDE

    def spot_of(col):
        source = col // 2
        in_x = place_in_line((source % SIDE - my_x + SIDE) % SIDE)
        in_y = place_in_line((source // SIDE - my_y + SIDE) % SIDE)
        return jnp.where(col % 2 == 0, in_y * SIDE + in_x, SIDE * SIDE + in_x * SIDE + in_y)

    def split(value):
        high = value.astype(jnp.bfloat16)
        return high, (value - high.astype(jnp.float32)).astype(jnp.bfloat16)

    def term_of(k):
        spot = spot_of(col_ref[k])
        high, low = split(amp_ref[pl.ds(pl.multiple_of(spot * size, size), size), :])
        tile_high, tile_low = split(held_ref[lax.rem(k, HELD)])
        term = jnp.dot(tile_high, high, preferred_element_type=jnp.float32)
        term += jnp.dot(tile_high, low, preferred_element_type=jnp.float32)
        return term + jnp.dot(tile_low, high, preferred_element_type=jnp.float32)

    def add_term(k, term):
        spot = pl.multiple_of(row_ref[k] * 32, 32)
        for hi in range(8):
            for c in range(CHUNKS):
                acc_ref[c, hi, pl.ds(spot, 32), :] += term[
                    hi * 32 : hi * 32 + 32, c * LANES : (c + 1) * LANES
                ]

    def add_group(j, carry):
        for i in range(GROUP):
            tile_copy(GROUP * j + i).wait()
        terms = [term_of(GROUP * j + i) for i in range(GROUP)]
        for i in range(GROUP):
            add_term(GROUP * j + i, terms[i])
        for i in range(GROUP):
            fetch(GROUP * j + i + HELD)
        return carry

    def add_one(k, carry):
        tile_copy(k).wait()
        add_term(k, term_of(k))
        return carry

    groups = count // GROUP
    lax.fori_loop(0, groups, add_group, 0)
    lax.fori_loop(groups * GROUP, count, add_one, 0)

    me_cd = lax.axis_index("cd")
    size_cd = acc_ref.shape[1]
    parts = out_parts(acc_ref.shape[2], size_cd)
    copies = []
    for i, (distance, first, rows) in enumerate(parts):
        block = lax.rem(me_cd + (distance + size_cd), size_cd)
        for c in range(CHUNKS):
            spot = c * len(parts) + i
            source = acc_ref.at[c, block, pl.ds(first, rows)]
            copies.append(pltpu.make_async_copy(source, outs[spot], out_sem.at[spot]))
    for copy in copies:
        copy.start()
    for copy in copies:
        copy.wait()


def ladder(tile_row, tile_col, tile_count, tiles, pieces, blocks):
    slots, size, _ = tiles.shape
    width = pieces[0].shape[1]
    total = sum(piece.shape[0] for piece in pieces)
    size_cd = lax.axis_size("cd")
    parts = out_parts(blocks * 32, size_cd)
    smem = pl.BlockSpec(memory_space=pltpu.SMEM)
    hbm = pl.BlockSpec(memory_space=pl.ANY)
    outs = [jax.ShapeDtypeStruct((rows, LANES), jnp.float32) for _, _, rows in parts] * CHUNKS
    given = pl.pallas_call(
        functools.partial(ladder_kernel, pieces_given=len(pieces), outs_given=len(outs)),
        in_specs=[smem] * 3 + [hbm] * (1 + len(pieces)),
        out_specs=[hbm] * len(outs),
        out_shape=outs,
        scratch_shapes=[
            pltpu.VMEM((total, width), jnp.float32),
            pltpu.VMEM((HELD, size, size), jnp.float32),
            pltpu.VMEM((CHUNKS, size_cd, blocks * 32, LANES), jnp.float32),
            pltpu.SemaphoreType.DMA((len(pieces),)),
            pltpu.SemaphoreType.DMA((HELD,)),
            pltpu.SemaphoreType.DMA((len(outs),)),
        ],
        compiler_params=pltpu.CompilerParams(vmem_limit_bytes=56 * 1024 * 1024),
        cost_estimate=pl.CostEstimate(
            flops=slots * 6 * size * size * width,
            bytes_accessed=slots * size * size * 4 + total * width * 4 + blocks * size * width * 4,
            transcendentals=0,
        ),
        name="ladder",
    )(tile_row, tile_col, tile_count, tiles, *pieces)
    return [given[c * len(parts) : (c + 1) * len(parts)] for c in range(CHUNKS)]


def shift_line(block, step):
    size = lax.axis_size("cd")
    return lax.ppermute(block, "cd", [(i, (i + step) % size) for i in range(size)])


def ring_terms(given):
    up, down = shift_line(given[0], 1), shift_line(given[1], -1)
    half = up.shape[0]
    for step in range(2, len(given) - 1, 2):
        ahead, behind = given[step : step + 2]
        if step == 2:
            up = jnp.concatenate([ahead[:half] + up, ahead[half:]], axis=0)
            down = jnp.concatenate([behind[:half], behind[half:] + down], axis=0)
        else:
            up = ahead + up
            down = behind + down
        up = shift_line(up, 1)
        down = shift_line(down, -1)
    return [up, down, given[-1]]


def bring(refs, held_ref, sem):
    copies = [pltpu.make_async_copy(ref, held_ref.at[i], sem.at[i]) for i, ref in enumerate(refs)]
    for copy in copies:
        copy.start()
    for copy in copies:
        copy.wait()


def merge_kernel(*refs, terms):
    out_ref, held_ref, terms_ref, sem = refs[-4:]
    bring(refs[:-4], terms_ref, sem)
    start = 0
    for c in range(CHUNKS):
        value = terms_ref[start]
        for i in range(start + 1, start + terms[c]):
            value = value + terms_ref[i]
        start += terms[c]
        held_ref[...] = value
        for row in range(held_ref.shape[0] // 32):
            for a in range(2):
                for b in range(2):
                    out_ref[pl.ds(row * 64 + c * 4 + a * 2 + b, 8, stride=8), :] = held_ref[
                        pl.ds(row * 32 + a * 16 + b, 8, stride=2), :
                    ]


def merge(chunks):
    rows = chunks[0][0].shape[0]
    flat = [term for terms in chunks for term in terms]
    return pl.pallas_call(
        functools.partial(merge_kernel, terms=[len(terms) for terms in chunks]),
        in_specs=[pl.BlockSpec(memory_space=pl.ANY)] * len(flat),
        out_specs=pl.BlockSpec(memory_space=pltpu.VMEM),
        out_shape=jax.ShapeDtypeStruct((CHUNKS * rows, LANES), jnp.float32),
        scratch_shapes=[
            pltpu.VMEM((rows, LANES), jnp.float32),
            pltpu.VMEM((len(flat), rows, LANES), jnp.float32),
            pltpu.SemaphoreType.DMA((len(flat),)),
        ],
        name="merge",
    )(*flat)


def finish_kernel(direct_any, mirror_any, out_ref, rows_ref, held_ref, sem):
    bring([direct_any, mirror_any], held_ref, sem)
    direct_ref, mirror_ref = held_ref.at[0], held_ref.at[1]
    for o in range(CHUNKS):
        for a in range(2):
            for b in range(2):
                rows_ref[pl.ds(b, LANES, stride=2), :] = (
                    direct_ref[pl.ds(o * 4 + a * 2 + b, LANES, stride=8), :]
                    + mirror_ref[pl.ds(o * 4 + b * 2 + a, LANES, stride=8), :]
                )
            out_ref[pl.ds(o * LANES, LANES), a, :] = rows_ref[...].T


def finish(direct, mirror):
    return pl.pallas_call(
        finish_kernel,
        in_specs=[pl.BlockSpec(memory_space=pl.ANY)] * 2,
        out_specs=pl.BlockSpec(memory_space=pltpu.VMEM),
        out_shape=jax.ShapeDtypeStruct((CHUNKS * LANES, 2, 2 * LANES), jnp.float32),
        scratch_shapes=[
            pltpu.VMEM((2 * LANES, LANES), jnp.float32),
            pltpu.VMEM((2, *direct.shape), jnp.float32),
            pltpu.SemaphoreType.DMA((2,)),
        ],
        name="finish",
    )(direct, mirror)


def per_device(amplitudes, integrals, tile_row, tile_col, tile_count):
    occ_dev = amplitudes.shape[0]
    blocks = lax.axis_size("ab")

    pieces = gather_plane(amplitudes.T)
    given = ladder(tile_row, tile_col, tile_count, integrals, pieces, blocks)
    sums = [ring_terms(blocks_of) for blocks_of in given]
    direct = merge(sums)
    outgoing = direct.reshape(-1, 8, LANES)
    arrived = lax.all_to_all(outgoing, ("ab", "cd"), split_axis=0, concat_axis=0, tiled=True)
    partner = lax.ppermute(arrived, "ij", [(0, 1), (1, 0)]).reshape(direct.shape)
    return finish(direct, partner).reshape(occ_dev, 1, 2, 2 * LANES)


def solution(mesh):
    in_specs = (
        P("ij", ("cd", "ab")),
        P(("ab", "cd"), None, None),
        P(("ab", "cd")),
        P(("ab", "cd")),
        P(("ab", "cd")),
    )
    out_specs = P("ij", "ab", "cd", None)
    return jax.shard_map(
        per_device, mesh=mesh, in_specs=in_specs, out_specs=out_specs, check_vma=False
    )
```

time: 185 us -> 168 us (0.908)
  waiting for transfers between devices: 67.9 us -> 52.5 us
  starting transfers between devices: 40.4 us -> 55.7 us
  between operations: 14.3 us -> 1.2 us
  other arithmetic: 0.25 us -> 12.1 us
  Pallas kernels: 26.3 us -> 15.7 us
  local copies, waits for them, and re-layouts: 6.85 us -> 2.97 us
    ppermute x4, waiting for transfers between devices: 0.01 us -> 24.7 us  [both_ways(): lax.ppermute(block, 'ab', plane_route(-dx, -dy))]
    ppermute x8 -> x16, waiting for transfers between devices: 36.9 us -> 13.7 us  [shift_line(): lax.ppermute(block, 'cd', [(i, (i + step) % size) for i in range(size)])]
    ppermute x8 -> x16, starting transfers between devices: 12.4 us -> 28.5 us  [shift_line(): lax.ppermute(block, 'cd', [(i, (i + step) % size) for i in range(size)])]
    all_gather x1 -> x0, waiting for transfers between devices: 13.2 us -> none  [per_device(): pieces = [lax.all_gather(second, 'ab', axis=0, tiled=True)]]
    pallas_call x3 -> x2, Pallas kernels: 24.2 us -> 13.4 us  [the longest x1 11 us: ladder(): pl.pallas_call(functools.partial(ladder_kernel, pieces_given=len(pieces),...]
    ppermute x4, waiting for transfers between devices: 10.6 us -> 0.43 us  [both_ways(): lax.ppermute(block, 'ab', plane_route(dx, dy))]
    ppermute x2, waiting for transfers between devices: 1.13 us -> 7.09 us  [far_halves(): lax.ppermute(above[half:], 'ab', plane_route(-dx, -dy))]
    add x1 -> x4, other arithmetic: 0.03 us -> 3.96 us  [ring_terms(): up = ahead + up]
  transfers between devices with their start and end apart: 25 -> 31, of which waited for: 14 -> 15; matrix products, arithmetic and copies ran while one was open for 1% -> 7% of each run, Pallas kernels for 6% -> 0%
where the time goes in v3:
time: 168 us
  starting transfers between devices  55.7 us (33%)
  waiting for transfers between devices  52.5 us (31%)
  blocking collectives  27.7 us (16%)
  Pallas kernels  15.7 us (9%)
  other arithmetic  12.1 us (7%)
  local copies, waits for them, and re-layouts  2.97 us (2%)
    ppermute x16, starting transfers between devices, shift_line(): lax.ppermute(block, 'cd', [(i, (i + step) % size) for i in range(size)])  28.5 us
    all_to_all x1, blocking collectives, per_device(): lax.all_to_all(outgoing, ('ab', 'cd'), split_axis=0, concat_axis=0, tiled...  27.7 us
    ppermute x4, waiting for transfers between devices, both_ways(): lax.ppermute(block, 'ab', plane_route(-dx, -dy))  24.7 us
    ppermute x16, waiting for transfers between devices, shift_line(): lax.ppermute(block, 'cd', [(i, (i + step) % size) for i in range(size)])  13.7 us
    pallas_call x1, Pallas kernels, ladder(): pl.pallas_call(functools.partial(ladder_kernel, pieces_given=len(pieces),...  11 us
    ppermute x2, waiting for transfers between devices, far_halves(): lax.ppermute(above[half:], 'ab', plane_route(-dx, -dy))  7.09 us
    ppermute x4, starting transfers between devices, both_ways(): lax.ppermute(block, 'ab', plane_route(-dx, -dy))  6.92 us
    ppermute x2, starting transfers between devices, first_line(): far = lax.ppermute(block, 'ab', plane_route(2 * dx, 2 * dy))  6.57 us
  transfers between devices with their start and end apart: 31, of which 15 were waited for; matrix products, arithmetic and copies ran while one was open for 7% of the time, Pallas kernels for 0%

profile of v3, /device:TPU:1, one launch (start us, length us, event | category | flops | bytes accessed | tf_op | source)
XLA Modules:
  0.0 167.9 jit_solution(16164698901327862700)
XLA Ops:
  0.0 1.2 copy.6
  1.3 3.7 %collective-permute-start.2 = (f32[256,256]{1,0:T(8,128)S(1)}, f32[256,256]{1,0:T(8,128)S(1)}, u32[]{:S(2)}, u32[]{:S(2)}) collective-permute-start(f32[256,256]{1,0:T(8,128)S(1)} %get-tuple-element.42), channel_id=1, source_target_pairs={{0,32},{16,48},{32,0},{48,16},{64,96},{80,112},{96,64},{112,80},{1... | collective-permute-start | bytes 786440 | tf_op jit(solution)/shard_map/ppermute | solution.py:42
  4.9 0.9 collective-permute-start.1
  6.4 2.9 %collective-permute-start.9 = (f32[256,256]{1,0:T(8,128)S(1)}, f32[256,256]{1,0:T(8,128)S(1)}, u32[]{:S(2)}, u32[]{:S(2)}) collective-permute-start(f32[256,256]{1,0:T(8,128)S(1)} %get-tuple-element.41), channel_id=1, source_target_pairs={{0,128},{16,144},{32,160},{48,176},{64,192},{80,208},{96,224},{112... | collective-permute-start | bytes 786440 | tf_op jit(solution)/shard_map/ppermute | solution.py:42
  9.3 0.8 collective-permute-start.8
  10.1 2.1 %collective-permute-start.7 = (f32[256,256]{1,0:T(8,128)S(1)}, f32[256,256]{1,0:T(8,128)S(1)}, u32[]{:S(2)}, u32[]{:S(2)}) collective-permute-start(f32[256,256]{1,0:T(8,128)S(1)} %get-tuple-element.41), channel_id=1, source_target_pairs={{0,64},{16,80},{32,96},{48,112},{64,128},{80,144},{96,160},{112,17... | collective-permute-start | bytes 786440 | tf_op jit(solution)/shard_map/ppermute | solution.py:27
  12.2 4.4 %collective-permute-done.1 = f32[256,256]{1,0:T(8,128)S(1)} collective-permute-done((f32[256,256]{1,0:T(8,128)S(1)}, f32[256,256]{1,0:T(8,128)S(1)}, u32[]{:S(2)}, u32[]{:S(2)}) %collective-permute-start.1) | collective-permute-done | bytes 262176 | tf_op jit(solution)/shard_map/ppermute | solution.py:28
  17.1 3.1 %collective-permute-start.4 = (f32[1024,256]{1,0:T(8,128)S(1)}, f32[1024,256]{1,0:T(8,128)S(1)}, u32[]{:S(2)}, u32[]{:S(2)}) collective-permute-start(f32[1024,256]{1,0:T(8,128)S(1)} %pad_maximum_fusion.rest_0_), channel_id=1, source_target_pairs={{0,192},{16,208},{32,224},{48,240},{64,0},{80,16},{96,32},{112,48}... | collective-permute-start | bytes 3145736 | tf_op jit(solution)/shard_map/ppermute | solution.py:28
  20.3 0.8 collective-permute-done.8
  21.2 2.1 %collective-permute-start.11 = (f32[1024,256]{1,0:T(8,128)S(1)}, f32[1024,256]{1,0:T(8,128)S(1)}, u32[]{:S(2)}, u32[]{:S(2)}) collective-permute-start(f32[1024,256]{1,0:T(8,128)S(1)} %pad_maximum_fusion.1.rest_5_), channel_id=1, source_target_pairs={{0,48},{16,0},{32,16},{48,32},{64,112},{80,64},{96,80},{112,96},{1... | collective-permute-start | bytes 3145736 | tf_op jit(solution)/shard_map/ppermute | solution.py:28
  23.3 19.4 %collective-permute-done.4.rest_2_ = f32[1024,256]{1,0:T(8,128)S(1)} collective-permute-done((f32[1024,256]{1,0:T(8,128)S(1)}, f32[1024,256]{1,0:T(8,128)S(1)}, u32[]{:S(2)}, u32[]{:S(2)}) %collective-permute-start.4) | collective-permute-done | bytes 1048608 | tf_op jit(solution)/shard_map/ppermute | solution.py:28
  42.8 3.5 %collective-permute-start.6 = (f32[512,256]{1,0:T(8,128)S(1)}, f32[512,256]{1,0:T(8,128)S(1)}, u32[]{:S(2)}, u32[]{:S(2)}) collective-permute-start(f32[512,256]{1,0:T(8,128)S(1)} %slice.58), channel_id=1, source_target_pairs={{0,192},{16,208},{32,224},{48,240},{64,0},{80,16},{96,32},{112,48}... | collective-permute-start | bytes 1572872 | tf_op jit(solution)/shard_map/ppermute | solution.py:37
  46.5 2.3 %collective-permute-start.13 = (f32[512,256]{1,0:T(8,128)S(1)}, f32[512,256]{1,0:T(8,128)S(1)}, u32[]{:S(2)}, u32[]{:S(2)}) collective-permute-start(f32[512,256]{1,0:T(8,128)S(1)} %slice.61), channel_id=1, source_target_pairs={{0,48},{16,0},{32,16},{48,32},{64,112},{80,64},{96,80},{112,96},{1... | collective-permute-start | bytes 1572872 | tf_op jit(solution)/shard_map/ppermute | solution.py:37
  49.6 7.1 %collective-permute-done.6.rest_4_ = f32[512,256]{1,0:T(8,128)S(1)} collective-permute-done((f32[512,256]{1,0:T(8,128)S(1)}, f32[512,256]{1,0:T(8,128)S(1)}, u32[]{:S(2)}, u32[]{:S(2)}) %collective-permute-start.6) | collective-permute-done | bytes 524320 | tf_op jit(solution)/shard_map/ppermute | solution.py:37
  56.7 2.8 %collective-permute-done.5.rest_3_ = f32[512,256]{1,0:T(8,128)S(1)} collective-permute-done((f32[512,256]{1,0:T(8,128)S(1)}, f32[512,256]{1,0:T(8,128)S(1)}, u32[]{:S(2)}, u32[]{:S(2)}) %collective-permute-start.5) | collective-permute-done | bytes 524320 | tf_op jit(solution)/shard_map/ppermute | solution.py:36
  59.5 2.2 %collective-permute-done.12.rest_8_ = f32[512,256]{1,0:T(8,128)} collective-permute-done((f32[512,256]{1,0:T(8,128)S(1)}, f32[512,256]{1,0:T(8,128)}, u32[]{:S(2)}, u32[]{:S(2)}) %collective-permute-start.12) | collective-permute-done | bytes 524320 | tf_op jit(solution)/shard_map/ppermute | solution.py:36
  61.8 11.0 %ladder.1 = (f32[256,128]{1,0:T(8,128)}, f32[256,128]{1,0:T(8,128)}, f32[512,128]{1,0:T(8,128)}, f32[512,128]{1,0:T(8,128)}, f32[512,128]{1,0:T(8,128)}, /*index...) custom-call(s32[46]{0:T(128)} %row_ref.1, ...), custom_call_target="tpu_custom_call" | custom-call | flops 4630511616 | bytes 24641536 | tf_op jit(solution)/shard_map/ladder/pallas_call | solution.py:172
  72.8 8.3 %collective-permute-start.26 = (f32[256,128]{1,0:T(8,128)}, f32[256,128]{1,0:T(8,128)S(1)}, u32[]{:S(2)}, u32[]{:S(2)}) collective-permute-start(f32[256,128]{1,0:T(8,128)} %get-tuple-element.39), channel_id=1, source_target_pairs={{0,14},{2,0},{4,2},{6,4},{8,6},{10,8},{12,10},{14,12},{1,15},{3,1}... | collective-permute-start | bytes 393224 | tf_op jit(solution)/shard_map/ppermute | solution.py:198
  81.1 2.7 %collective-permute-start.18 = (f32[256,128]{1,0:T(8,128)}, f32[256,128]{1,0:T(8,128)S(1)}, u32[]{:S(2)}, u32[]{:S(2)}) collective-permute-start(f32[256,128]{1,0:T(8,128)} %get-tuple-element.30), channel_id=1, source_target_pairs={{0,14},{2,0},{4,2},{6,4},{8,6},{10,8},{12,10},{14,12},{1,15},{3,1}... | collective-permute-start | bytes 393224 | tf_op jit(solution)/shard_map/ppermute | solution.py:198
  83.8 1.0 fusion.1
  84.8 2.7 %collective-permute-start.27 = (f32[512,128]{1,0:T(8,128)S(1)}, f32[512,128]{1,0:T(8,128)S(1)}, u32[]{:S(2)}, u32[]{:S(2)}) collective-permute-start(f32[512,128]{1,0:T(8,128)S(1)} %pad_maximum_fusion.5), channel_id=1, source_target_pairs={{0,14},{2,0},{4,2},{6,4},{8,6},{10,8},{12,10},{14,12},{1,15},{3,1}... | collective-permute-start | bytes 786440 | tf_op jit(solution)/shard_map/ppermute | solution.py:198
  87.6 2.3 %collective-permute-done.22 = f32[256,128]{1,0:T(8,128)S(1)} collective-permute-done((f32[256,128]{1,0:T(8,128)}, f32[256,128]{1,0:T(8,128)S(1)}, u32[]{:S(2)}, u32[]{:S(2)}) %collective-permute-start.22) | collective-permute-done | bytes 131104 | tf_op jit(solution)/shard_map/ppermute | solution.py:198
  89.9 1.0 slice_add_fusion.1
  91.0 1.0 fusion.2
  92.0 2.7 %collective-permute-start.19 = (f32[512,128]{1,0:T(8,128)S(1)}, f32[512,128]{1,0:T(8,128)S(1)}, u32[]{:S(2)}, u32[]{:S(2)}) collective-permute-start(f32[512,128]{1,0:T(8,128)S(1)} %pad_maximum_fusion.3), channel_id=1, source_target_pairs={{0,14},{2,0},{4,2},{6,4},{8,6},{10,8},{12,10},{14,12},{1,15},{3,1}... | collective-permute-start | bytes 786440 | tf_op jit(solution)/shard_map/ppermute | solution.py:198
  94.8 1.0 slice_add_fusion.3
  95.9 1.0 add.46
  96.9 2.7 %collective-permute-start.28 = (f32[512,128]{1,0:T(8,128)S(1)}, f32[512,128]{1,0:T(8,128)S(1)}, u32[]{:S(2)}, u32[]{:S(2)}) collective-permute-start(f32[512,128]{1,0:T(8,128)S(1)} %add.46), channel_id=1, source_target_pairs={{0,14},{2,0},{4,2},{6,4},{8,6},{10,8},{12,10},{14,12},{1,15},{3,1}... | collective-permute-start | bytes 786440 | tf_op jit(solution)/shard_map/ppermute | solution.py:198
  99.6 1.0 add.43
  100.7 1.0 add.40
  101.7 2.7 %collective-permute-start.20 = (f32[512,128]{1,0:T(8,128)S(1)}, f32[512,128]{1,0:T(8,128)S(1)}, u32[]{:S(2)}, u32[]{:S(2)}) collective-permute-start(f32[512,128]{1,0:T(8,128)S(1)} %add.40), channel_id=1, source_target_pairs={{0,14},{2,0},{4,2},{6,4},{8,6},{10,8},{12,10},{14,12},{1,15},{3,1}... | collective-permute-start | bytes 786440 | tf_op jit(solution)/shard_map/ppermute | solution.py:198
  105.1 1.0 add.37
  106.2 1.0 add.47
  107.2 3.1 %collective-permute-start.29 = (f32[512,128]{1,0:T(8,128)S(1)}, f32[512,128]{1,0:T(8,128)S(1)}, u32[]{:S(2)}, u32[]{:S(2)}) collective-permute-start(f32[512,128]{1,0:T(8,128)S(1)} %add.47), channel_id=1, source_target_pairs={{0,14},{2,0},{4,2},{6,4},{8,6},{10,8},{12,10},{14,12},{1,15},{3,1}... | collective-permute-start | bytes 786440 | tf_op jit(solution)/shard_map/ppermute | solution.py:198
  110.7 1.0 add.44
  111.8 1.0 add.41
  112.8 2.8 %collective-permute-start.21 = (f32[512,128]{1,0:T(8,128)S(1)}, f32[512,128]{1,0:T(8,128)S(1)}, u32[]{:S(2)}, u32[]{:S(2)}) collective-permute-start(f32[512,128]{1,0:T(8,128)S(1)} %add.41), channel_id=1, source_target_pairs={{0,14},{2,0},{4,2},{6,4},{8,6},{10,8},{12,10},{14,12},{1,15},{3,1}... | collective-permute-start | bytes 786440 | tf_op jit(solution)/shard_map/ppermute | solution.py:198
  116.1 1.0 add.38
  117.4 4.2 %collective-permute-done.25.refs_3_ = f32[512,128]{1,0:T(8,128)S(1)} collective-permute-done((f32[512,128]{1,0:T(8,128)S(1)}, f32[512,128]{1,0:T(8,128)S(1)}, u32[]{:S(2)}, u32[]{:S(2)}) %collective-permute-start.25) | collective-permute-done | bytes 262176 | tf_op jit(solution)/shard_map/ppermute | solution.py:198
  121.6 0.7 collective-permute-done.21.refs_1_
  122.3 5.0 %collective-permute-done.17.refs_0_ = f32[512,128]{1,0:T(8,128)S(1)} collective-permute-done((f32[512,128]{1,0:T(8,128)S(1)}, f32[512,128]{1,0:T(8,128)S(1)}, u32[]{:S(2)}, u32[]{:S(2)}) %collective-permute-start.17) | collective-permute-done | bytes 262176 | tf_op jit(solution)/shard_map/ppermute | solution.py:198
  127.3 0.7 copy-done.13
  128.0 2.4 %merge.1.direct_any = f32[1024,128]{1,0:T(8,128)} custom-call(f32[512,128]{1,0:T(8,128)} %copy-done.13, f32[512,128]{1,0:T(8,128)} %copy-done.12, f32[512,128]{1,0:T(8,128)} %get-tuple-element.31.refs_2_, f32[512,128]{1,0:T(8,128)} %copy-done.11, f32[512,128]{1,0:T(8,128)} %copy-done.10, f32[512,128]{1,0:T(8,128)} %get-tuple-element.40.refs_5_), custom_call_target="tpu_custom_call" | custom-call | tf_op jit(solution)/shard_map/merge/pallas_call | solution.py:246
  130.3 27.7 %all_to_all.5 = f32[128,8,128]{2,1,0:T(8,128)S(1)} all-to-all(f32[128,8,128]{2,1,0:T(8,128)} %bitcast.6), channel_id=1, replica_groups=mesh['ab'=16,'cd'=8,'ij'=2] {'ab','cd'}, dimensions={0} | all-to-all | bytes 1048576 | tf_op jit(solution)/shard_map/all_to_all | solution.py:297
  158.0 5.0 %collective-permute-start.30 = (f32[128,8,128]{2,1,0:T(8,128)S(1)}, f32[128,8,128]{2,1,0:T(8,128)S(1)}, u32[]{:S(2)}, u32[]{:S(2)}) collective-permute-start(f32[128,8,128]{2,1,0:T(8,128)S(1)} %all_to_all.5), channel_id=1, source_target_pairs={{0,1},{1,0},{2,3},{3,2},{4,5},{5,4},{6,7},{7,6},{8,9},{9,8},{10,11... | collective-permute-start | bytes 1572872 | tf_op jit(solution)/shard_map/ppermute | solution.py:298
  163.0 1.5 collective-permute-done.30
  164.6 0.8 copy-done.9
  165.4 2.3 %finish.1 = f32[256,2,256]{2,1,0:T(2,128)} custom-call(f32[1024,128]{1,0:T(8,128)} %merge.1.direct_any, f32[1024,128]{1,0:T(8,128)} %bitcast.8), custom_call_target="tpu_custom_call" | custom-call | tf_op jit(solution)/shard_map/finish/pallas_call | solution.py:274
  (70 shorter events, 4.0 us)
Async XLA Ops:
  1.3 8.8 %collective-permute-start.2 = (f32[256,256]{1,0:T(8,128)S(1)}, f32[256,256]{1,0:T(8,128)S(1)}, u32[]{:S(2)}, u32[]{:S(2)}) collective-permute-start(f32[256,256]{1,0:T(8,128)S(1)} %get-tuple-element.42), channel_id=1, source_target_pairs={{0,32},{16,48},{32,0},{48,16},{64,96},{80,112},{96,64},{112,80},{1... | collective-permute-start | bytes 786440 | tf_op jit(solution)/shard_map/ppermute | solution.py:42
  4.9 11.7 %collective-permute-start.1 = (f32[256,256]{1,0:T(8,128)S(1)}, f32[256,256]{1,0:T(8,128)S(1)}, u32[]{:S(2)}, u32[]{:S(2)}) collective-permute-start(f32[256,256]{1,0:T(8,128)S(1)} %get-tuple-element.42), channel_id=1, source_target_pairs={{0,48},{16,0},{32,16},{48,32},{64,112},{80,64},{96,80},{112,96},{1... | collective-permute-start | bytes 786440 | tf_op jit(solution)/shard_map/ppermute | solution.py:28
  5.8 11.2 %collective-permute-start = (f32[256,256]{1,0:T(8,128)S(1)}, f32[256,256]{1,0:T(8,128)S(1)}, u32[]{:S(2)}, u32[]{:S(2)}) collective-permute-start(f32[256,256]{1,0:T(8,128)S(1)} %get-tuple-element.42), channel_id=1, source_target_pairs={{0,16},{16,32},{32,48},{48,0},{64,80},{80,96},{96,112},{112,64},{1... | collective-permute-start | bytes 786440 | tf_op jit(solution)/shard_map/ppermute | solution.py:27
  6.4 13.9 %collective-permute-start.9 = (f32[256,256]{1,0:T(8,128)S(1)}, f32[256,256]{1,0:T(8,128)S(1)}, u32[]{:S(2)}, u32[]{:S(2)}) collective-permute-start(f32[256,256]{1,0:T(8,128)S(1)} %get-tuple-element.41), channel_id=1, source_target_pairs={{0,128},{16,144},{32,160},{48,176},{64,192},{80,208},{96,224},{112... | collective-permute-start | bytes 786440 | tf_op jit(solution)/shard_map/ppermute | solution.py:42
  9.3 11.8 %collective-permute-start.8 = (f32[256,256]{1,0:T(8,128)S(1)}, f32[256,256]{1,0:T(8,128)S(1)}, u32[]{:S(2)}, u32[]{:S(2)}) collective-permute-start(f32[256,256]{1,0:T(8,128)S(1)} %get-tuple-element.41), channel_id=1, source_target_pairs={{0,192},{16,208},{32,224},{48,240},{64,0},{80,16},{96,32},{112,48}... | collective-permute-start | bytes 786440 | tf_op jit(solution)/shard_map/ppermute | solution.py:28
  10.1 11.0 %collective-permute-start.7 = (f32[256,256]{1,0:T(8,128)S(1)}, f32[256,256]{1,0:T(8,128)S(1)}, u32[]{:S(2)}, u32[]{:S(2)}) collective-permute-start(f32[256,256]{1,0:T(8,128)S(1)} %get-tuple-element.41), channel_id=1, source_target_pairs={{0,64},{16,80},{32,96},{48,112},{64,128},{80,144},{96,160},{112,17... | collective-permute-start | bytes 786440 | tf_op jit(solution)/shard_map/ppermute | solution.py:27
  17.1 44.6 %copy-start = (f32[1024,256]{1,0:T(8,128)}, f32[1024,256]{1,0:T(8,128)S(1)}, u32[]{:S(2)}) copy-start(f32[1024,256]{1,0:T(8,128)S(1)} %pad_maximum_fusion.rest_0_) | copy-start | bytes 3145732
  17.1 25.6 %collective-permute-start.4 = (f32[1024,256]{1,0:T(8,128)S(1)}, f32[1024,256]{1,0:T(8,128)S(1)}, u32[]{:S(2)}, u32[]{:S(2)}) collective-permute-start(f32[1024,256]{1,0:T(8,128)S(1)} %pad_maximum_fusion.rest_0_), channel_id=1, source_target_pairs={{0,192},{16,208},{32,224},{48,240},{64,0},{80,16},{96,32},{112,48}... | collective-permute-start | bytes 3145736 | tf_op jit(solution)/shard_map/ppermute | solution.py:28
  20.3 26.0 %collective-permute-start.3 = (f32[1024,256]{1,0:T(8,128)S(1)}, f32[1024,256]{1,0:T(8,128)S(1)}, u32[]{:S(2)}, u32[]{:S(2)}) collective-permute-start(f32[1024,256]{1,0:T(8,128)S(1)} %pad_maximum_fusion.rest_0_), channel_id=1, source_target_pairs={{0,64},{16,80},{32,96},{48,112},{64,128},{80,144},{96,160},{112,17... | collective-permute-start | bytes 3145736 | tf_op jit(solution)/shard_map/ppermute | solution.py:27
  21.2 40.6 %copy-start.1 = (f32[1024,256]{1,0:T(8,128)}, f32[1024,256]{1,0:T(8,128)S(1)}, u32[]{:S(2)}) copy-start(f32[1024,256]{1,0:T(8,128)S(1)} %pad_maximum_fusion.1.rest_5_) | copy-start | bytes 3145732
  21.2 25.2 %collective-permute-start.11 = (f32[1024,256]{1,0:T(8,128)S(1)}, f32[1024,256]{1,0:T(8,128)S(1)}, u32[]{:S(2)}, u32[]{:S(2)}) collective-permute-start(f32[1024,256]{1,0:T(8,128)S(1)} %pad_maximum_fusion.1.rest_5_), channel_id=1, source_target_pairs={{0,48},{16,0},{32,16},{48,32},{64,112},{80,64},{96,80},{112,96},{1... | collective-permute-start | bytes 3145736 | tf_op jit(solution)/shard_map/ppermute | solution.py:28
  23.3 25.5 %collective-permute-start.10 = (f32[1024,256]{1,0:T(8,128)S(1)}, f32[1024,256]{1,0:T(8,128)S(1)}, u32[]{:S(2)}, u32[]{:S(2)}) collective-permute-start(f32[1024,256]{1,0:T(8,128)S(1)} %pad_maximum_fusion.1.rest_5_), channel_id=1, source_target_pairs={{0,16},{16,32},{32,48},{48,0},{64,80},{80,96},{96,112},{112,64},{1... | collective-permute-start | bytes 3145736 | tf_op jit(solution)/shard_map/ppermute | solution.py:27
  42.7 19.0 %copy-start.2 = (f32[1024,256]{1,0:T(8,128)}, f32[1024,256]{1,0:T(8,128)S(1)}, u32[]{:S(2)}) copy-start(f32[1024,256]{1,0:T(8,128)S(1)} %collective-permute-done.4.rest_2_) | copy-start | bytes 3145732
  42.8 13.9 %collective-permute-start.6 = (f32[512,256]{1,0:T(8,128)S(1)}, f32[512,256]{1,0:T(8,128)S(1)}, u32[]{:S(2)}, u32[]{:S(2)}) collective-permute-start(f32[512,256]{1,0:T(8,128)S(1)} %slice.58), channel_id=1, source_target_pairs={{0,192},{16,208},{32,224},{48,240},{64,0},{80,16},{96,32},{112,48}... | collective-permute-start | bytes 1572872 | tf_op jit(solution)/shard_map/ppermute | solution.py:37
  46.3 15.5 %copy-start.3 = (f32[1024,256]{1,0:T(8,128)}, f32[1024,256]{1,0:T(8,128)S(1)}, u32[]{:S(2)}) copy-start(f32[1024,256]{1,0:T(8,128)S(1)} %collective-permute-done.3.rest_1_) | copy-start | bytes 3145732
  46.3 13.2 %collective-permute-start.5 = (f32[512,256]{1,0:T(8,128)S(1)}, f32[512,256]{1,0:T(8,128)S(1)}, u32[]{:S(2)}, u32[]{:S(2)}) collective-permute-start(f32[512,256]{1,0:T(8,128)S(1)} %slice.57), channel_id=1, source_target_pairs={{0,64},{16,80},{32,96},{48,112},{64,128},{80,144},{96,160},{112,17... | collective-permute-start | bytes 1572872 | tf_op jit(solution)/shard_map/ppermute | solution.py:36
  46.4 15.3 %copy-start.4 = (f32[1024,256]{1,0:T(8,128)}, f32[1024,256]{1,0:T(8,128)S(1)}, u32[]{:S(2)}) copy-start(f32[1024,256]{1,0:T(8,128)S(1)} %collective-permute-done.11.rest_7_) | copy-start | bytes 3145732
  46.5 13.1 %collective-permute-start.13 = (f32[512,256]{1,0:T(8,128)S(1)}, f32[512,256]{1,0:T(8,128)S(1)}, u32[]{:S(2)}, u32[]{:S(2)}) collective-permute-start(f32[512,256]{1,0:T(8,128)S(1)} %slice.61), channel_id=1, source_target_pairs={{0,48},{16,0},{32,16},{48,32},{64,112},{80,64},{96,80},{112,96},{1... | collective-permute-start | bytes 1572872 | tf_op jit(solution)/shard_map/ppermute | solution.py:37
  48.8 13.0 %copy-start.5 = (f32[1024,256]{1,0:T(8,128)}, f32[1024,256]{1,0:T(8,128)S(1)}, u32[]{:S(2)}) copy-start(f32[1024,256]{1,0:T(8,128)S(1)} %collective-permute-done.10.rest_6_) | copy-start | bytes 3145732
  48.8 12.9 %collective-permute-start.12 = (f32[512,256]{1,0:T(8,128)S(1)}, f32[512,256]{1,0:T(8,128)}, u32[]{:S(2)}, u32[]{:S(2)}) collective-permute-start(f32[512,256]{1,0:T(8,128)S(1)} %slice.60), channel_id=1, source_target_pairs={{0,16},{16,32},{32,48},{48,0},{64,80},{80,96},{96,112},{112,64},{1... | collective-permute-start | bytes 1572872 | tf_op jit(solution)/shard_map/ppermute | solution.py:36
  56.7 5.1 %copy-start.6 = (f32[512,256]{1,0:T(8,128)}, f32[512,256]{1,0:T(8,128)S(1)}, u32[]{:S(2)}) copy-start(f32[512,256]{1,0:T(8,128)S(1)} %collective-permute-done.6.rest_4_) | copy-start | bytes 1572868
  59.5 2.3 %copy-start.7 = (f32[512,256]{1,0:T(8,128)}, f32[512,256]{1,0:T(8,128)S(1)}, u32[]{:S(2)}) copy-start(f32[512,256]{1,0:T(8,128)S(1)} %collective-permute-done.5.rest_3_) | copy-start | bytes 1572868
  59.5 2.3 %copy-start.8 = (f32[512,256]{1,0:T(8,128)}, f32[512,256]{1,0:T(8,128)S(1)}, u32[]{:S(2)}) copy-start(f32[512,256]{1,0:T(8,128)S(1)} %collective-permute-done.13.rest_9_) | copy-start | bytes 1572868
  72.8 11.0 %collective-permute-start.26 = (f32[256,128]{1,0:T(8,128)}, f32[256,128]{1,0:T(8,128)S(1)}, u32[]{:S(2)}, u32[]{:S(2)}) collective-permute-start(f32[256,128]{1,0:T(8,128)} %get-tuple-element.39), channel_id=1, source_target_pairs={{0,14},{2,0},{4,2},{6,4},{8,6},{10,8},{12,10},{14,12},{1,15},{3,1}... | collective-permute-start | bytes 393224 | tf_op jit(solution)/shard_map/ppermute | solution.py:198
  81.1 13.6 %collective-permute-start.14 = (f32[256,128]{1,0:T(8,128)}, f32[256,128]{1,0:T(8,128)S(1)}, u32[]{:S(2)}, u32[]{:S(2)}) collective-permute-start(f32[256,128]{1,0:T(8,128)} %get-tuple-element.26), channel_id=1, source_target_pairs={{0,2},{2,4},{4,6},{6,8},{8,10},{10,12},{12,14},{14,0},{1,3},{3,5},... | collective-permute-start | bytes 393224 | tf_op jit(solution)/shard_map/ppermute | solution.py:198
  81.1 9.9 %collective-permute-start.18 = (f32[256,128]{1,0:T(8,128)}, f32[256,128]{1,0:T(8,128)S(1)}, u32[]{:S(2)}, u32[]{:S(2)}) collective-permute-start(f32[256,128]{1,0:T(8,128)} %get-tuple-element.30), channel_id=1, source_target_pairs={{0,14},{2,0},{4,2},{6,4},{8,6},{10,8},{12,10},{14,12},{1,15},{3,1}... | collective-permute-start | bytes 393224 | tf_op jit(solution)/shard_map/ppermute | solution.py:198
  83.8 6.1 %collective-permute-start.22 = (f32[256,128]{1,0:T(8,128)}, f32[256,128]{1,0:T(8,128)S(1)}, u32[]{:S(2)}, u32[]{:S(2)}) collective-permute-start(f32[256,128]{1,0:T(8,128)} %get-tuple-element.35), channel_id=1, source_target_pairs={{0,2},{2,4},{4,6},{6,8},{8,10},{10,12},{12,14},{14,0},{1,3},{3,5},... | collective-permute-start | bytes 393224 | tf_op jit(solution)/shard_map/ppermute | solution.py:198
  84.8 11.0 %collective-permute-start.27 = (f32[512,128]{1,0:T(8,128)S(1)}, f32[512,128]{1,0:T(8,128)S(1)}, u32[]{:S(2)}, u32[]{:S(2)}) collective-permute-start(f32[512,128]{1,0:T(8,128)S(1)} %pad_maximum_fusion.5), channel_id=1, source_target_pairs={{0,14},{2,0},{4,2},{6,4},{8,6},{10,8},{12,10},{14,12},{1,15},{3,1}... | collective-permute-start | bytes 786440 | tf_op jit(solution)/shard_map/ppermute | solution.py:198
  90.9 8.7 %collective-permute-start.23 = (f32[512,128]{1,0:T(8,128)S(1)}, f32[512,128]{1,0:T(8,128)S(1)}, u32[]{:S(2)}, u32[]{:S(2)}) collective-permute-start(f32[512,128]{1,0:T(8,128)S(1)} %pad_maximum_fusion.4), channel_id=1, source_target_pairs={{0,2},{2,4},{4,6},{6,8},{8,10},{10,12},{12,14},{14,0},{1,3},{3,5},... | collective-permute-start | bytes 786440 | tf_op jit(solution)/shard_map/ppermute | solution.py:198
  92.0 8.7 %collective-permute-start.19 = (f32[512,128]{1,0:T(8,128)S(1)}, f32[512,128]{1,0:T(8,128)S(1)}, u32[]{:S(2)}, u32[]{:S(2)}) collective-permute-start(f32[512,128]{1,0:T(8,128)S(1)} %pad_maximum_fusion.3), channel_id=1, source_target_pairs={{0,14},{2,0},{4,2},{6,4},{8,6},{10,8},{12,10},{14,12},{1,15},{3,1}... | collective-permute-start | bytes 786440 | tf_op jit(solution)/shard_map/ppermute | solution.py:198
  95.8 9.3 %collective-permute-start.15 = (f32[512,128]{1,0:T(8,128)S(1)}, f32[512,128]{1,0:T(8,128)S(1)}, u32[]{:S(2)}, u32[]{:S(2)}) collective-permute-start(f32[512,128]{1,0:T(8,128)S(1)} %pad_maximum_fusion.2), channel_id=1, source_target_pairs={{0,2},{2,4},{4,6},{6,8},{8,10},{10,12},{12,14},{14,0},{1,3},{3,5},... | collective-permute-start | bytes 786440 | tf_op jit(solution)/shard_map/ppermute | solution.py:198
  96.9 9.3 %collective-permute-start.28 = (f32[512,128]{1,0:T(8,128)S(1)}, f32[512,128]{1,0:T(8,128)S(1)}, u32[]{:S(2)}, u32[]{:S(2)}) collective-permute-start(f32[512,128]{1,0:T(8,128)S(1)} %add.46), channel_id=1, source_target_pairs={{0,14},{2,0},{4,2},{6,4},{8,6},{10,8},{12,10},{14,12},{1,15},{3,1}... | collective-permute-start | bytes 786440 | tf_op jit(solution)/shard_map/ppermute | solution.py:198
  100.6 10.1 %collective-permute-start.24 = (f32[512,128]{1,0:T(8,128)S(1)}, f32[512,128]{1,0:T(8,128)S(1)}, u32[]{:S(2)}, u32[]{:S(2)}) collective-permute-start(f32[512,128]{1,0:T(8,128)S(1)} %add.43), channel_id=1, source_target_pairs={{0,2},{2,4},{4,6},{6,8},{8,10},{10,12},{12,14},{14,0},{1,3},{3,5},... | collective-permute-start | bytes 786440 | tf_op jit(solution)/shard_map/ppermute | solution.py:198
  101.7 10.1 %collective-permute-start.20 = (f32[512,128]{1,0:T(8,128)S(1)}, f32[512,128]{1,0:T(8,128)S(1)}, u32[]{:S(2)}, u32[]{:S(2)}) collective-permute-start(f32[512,128]{1,0:T(8,128)S(1)} %add.40), channel_id=1, source_target_pairs={{0,14},{2,0},{4,2},{6,4},{8,6},{10,8},{12,10},{14,12},{1,15},{3,1}... | collective-permute-start | bytes 786440 | tf_op jit(solution)/shard_map/ppermute | solution.py:198
  106.1 10.0 %collective-permute-start.16 = (f32[512,128]{1,0:T(8,128)S(1)}, f32[512,128]{1,0:T(8,128)S(1)}, u32[]{:S(2)}, u32[]{:S(2)}) collective-permute-start(f32[512,128]{1,0:T(8,128)S(1)} %add.37), channel_id=1, source_target_pairs={{0,2},{2,4},{4,6},{6,8},{8,10},{10,12},{12,14},{14,0},{1,3},{3,5},... | collective-permute-start | bytes 786440 | tf_op jit(solution)/shard_map/ppermute | solution.py:198
  107.2 10.3 %collective-permute-start.29 = (f32[512,128]{1,0:T(8,128)S(1)}, f32[512,128]{1,0:T(8,128)S(1)}, u32[]{:S(2)}, u32[]{:S(2)}) collective-permute-start(f32[512,128]{1,0:T(8,128)S(1)} %add.47), channel_id=1, source_target_pairs={{0,14},{2,0},{4,2},{6,4},{8,6},{10,8},{12,10},{14,12},{1,15},{3,1}... | collective-permute-start | bytes 786440 | tf_op jit(solution)/shard_map/ppermute | solution.py:198
  111.7 10.0 %collective-permute-start.25 = (f32[512,128]{1,0:T(8,128)S(1)}, f32[512,128]{1,0:T(8,128)S(1)}, u32[]{:S(2)}, u32[]{:S(2)}) collective-permute-start(f32[512,128]{1,0:T(8,128)S(1)} %add.44), channel_id=1, source_target_pairs={{0,2},{2,4},{4,6},{6,8},{8,10},{10,12},{12,14},{14,0},{1,3},{3,5},... | collective-permute-start | bytes 786440 | tf_op jit(solution)/shard_map/ppermute | solution.py:198
  112.8 9.5 %collective-permute-start.21 = (f32[512,128]{1,0:T(8,128)S(1)}, f32[512,128]{1,0:T(8,128)S(1)}, u32[]{:S(2)}, u32[]{:S(2)}) collective-permute-start(f32[512,128]{1,0:T(8,128)S(1)} %add.41), channel_id=1, source_target_pairs={{0,14},{2,0},{4,2},{6,4},{8,6},{10,8},{12,10},{14,12},{1,15},{3,1}... | collective-permute-start | bytes 786440 | tf_op jit(solution)/shard_map/ppermute | solution.py:198
  117.1 10.2 %collective-permute-start.17 = (f32[512,128]{1,0:T(8,128)S(1)}, f32[512,128]{1,0:T(8,128)S(1)}, u32[]{:S(2)}, u32[]{:S(2)}) collective-permute-start(f32[512,128]{1,0:T(8,128)S(1)} %add.38), channel_id=1, source_target_pairs={{0,2},{2,4},{4,6},{6,8},{8,10},{10,12},{12,14},{14,0},{1,3},{3,5},... | collective-permute-start | bytes 786440 | tf_op jit(solution)/shard_map/ppermute | solution.py:198
  117.4 9.8 %copy-start.10 = (f32[512,128]{1,0:T(8,128)}, f32[512,128]{1,0:T(8,128)S(1)}, u32[]{:S(2)}) copy-start(f32[512,128]{1,0:T(8,128)S(1)} %collective-permute-done.29.refs_4_) | copy-start | bytes 786436
  121.6 5.6 %copy-start.11 = (f32[512,128]{1,0:T(8,128)}, f32[512,128]{1,0:T(8,128)S(1)}, u32[]{:S(2)}) copy-start(f32[512,128]{1,0:T(8,128)S(1)} %collective-permute-done.25.refs_3_) | copy-start | bytes 786436
  122.3 5.0 %copy-start.12 = (f32[512,128]{1,0:T(8,128)}, f32[512,128]{1,0:T(8,128)S(1)}, u32[]{:S(2)}) copy-start(f32[512,128]{1,0:T(8,128)S(1)} %collective-permute-done.21.refs_1_) | copy-start | bytes 786436
  127.3 0.7 copy-start.13
  158.0 6.6 %collective-permute-start.30 = (f32[128,8,128]{2,1,0:T(8,128)S(1)}, f32[128,8,128]{2,1,0:T(8,128)S(1)}, u32[]{:S(2)}, u32[]{:S(2)}) collective-permute-start(f32[128,8,128]{2,1,0:T(8,128)S(1)} %all_to_all.5), channel_id=1, source_target_pairs={{0,1},{1,0},{2,3},{3,2},{4,5},{5,4},{6,7},{7,6},{8,9},{9,8},{10,11... | collective-permute-start | bytes 1572872 | tf_op jit(solution)/shard_map/ppermute | solution.py:298
  164.6 0.8 copy-start.9

commit v4 on v3

--- a/solution.py
+++ b/solution.py
@@ -50,12 +50,8 @@
     up = first_line(block[half:], *along_y)
     near_low = both_ways(low, *along_y)
     near_up = both_ways(up, *along_x)
-    pieces = [low] + near_low + far_halves(near_low, *along_y)
-    return pieces + [up] + near_up + far_halves(near_up, *along_x)
-
-
-def place_in_line(offset):
-    return jnp.where(offset == 0, 0, jnp.where(offset == 1, 2, jnp.where(offset == 2, 3, 1)))
+    far = far_halves(near_low, *along_y) + far_halves(near_up, *along_x)
+    return [low] + near_low + [up] + near_up, far
 
 
 def out_parts(rows, size):
@@ -66,13 +62,15 @@
     return parts + [(0, 0, rows)]
 
 
-def ladder_kernel(row_ref, col_ref, count_ref, tiles_ref, *rest, pieces_given, outs_given):
+def ladder_kernel(row_ref, col_ref, count_ref, tiles_ref, *rest, pieces_given, last):
     pieces = rest[:pieces_given]
-    outs = rest[pieces_given : pieces_given + outs_given]
-    amp_ref, held_ref, acc_ref, amp_sem, held_sem, out_sem = rest[pieces_given + outs_given :]
+    outs = rest[pieces_given + last : -9]
+    amp_ref, held_ref, acc_ref, slot_ref, place_ref, amp_sem, held_sem, out_sem, acc_sem = rest[-9:]
     size = tiles_ref.shape[-1]
-    count = count_ref[0]
+    lines = 1 if last else SIDE - 1
     copies = []
+    if last:
+        copies.append(pltpu.make_async_copy(rest[pieces_given], acc_ref, acc_sem))
     start = 0
     for i, piece in enumerate(pieces):
         rows = piece.shape[0]
@@ -81,69 +79,85 @@
     for copy in copies:
         copy.start()
 
-    def tile_copy(k):
-        spot = lax.rem(k, HELD)
-        return pltpu.make_async_copy(tiles_ref.at[k], held_ref.at[spot], held_sem.at[spot])
-
-    def fetch(k):
-        @pl.when(k < count)
+    me = lax.axis_index("ab")
+    my_y = me >> 2
+    my_x = me & 3
+
+    def pick(k, found):
+        col = col_ref[k]
+        in_x = (120 >> (2 * (((col >> 1) - my_x) & 3))) & 3
+        in_y = (120 >> (2 * (((col >> 3) - my_y) & 3))) & 3
+        odd = col & 1
+        line = jnp.where(odd == 0, in_y, in_x)
+        spot = jnp.where(odd == 0, in_x, in_y)
+        slot_ref[found] = k
+        if last:
+            place_ref[found] = odd * SIDE + spot
+            return found + jnp.where(line == SIDE - 1, 1, 0)
+        place_ref[found] = (odd * lines + line) * SIDE + spot
+        return found + jnp.where(line == SIDE - 1, 0, 1)
+
+    count = lax.fori_loop(0, count_ref[0], pick, 0)
+
+    def tile_copy(j):
+        spot = lax.rem(j, HELD)
+        return pltpu.make_async_copy(tiles_ref.at[slot_ref[j]], held_ref.at[spot], held_sem.at[spot])
+
+    def fetch(j):
+        @pl.when(j < count)
         def _():
-            tile_copy(k).start()
-
-    for k in range(HELD):
-        fetch(k)
-    acc_ref[...] = jnp.zeros_like(acc_ref)
+            tile_copy(j).start()
+
+    for j in range(HELD):
+        fetch(j)
+    if not last:
+        acc_ref[...] = jnp.zeros_like(acc_ref)
     for copy in copies:
         copy.wait()
-    me = lax.axis_index("ab")
-    my_y = me // SIDE
-    my_x = me % SIDE
-
-    def spot_of(col):
-        source = col // 2
-        in_x = place_in_line((source % SIDE - my_x + SIDE) % SIDE)
-        in_y = place_in_line((source // SIDE - my_y + SIDE) % SIDE)
-        return jnp.where(col % 2 == 0, in_y * SIDE + in_x, SIDE * SIDE + in_x * SIDE + in_y)
 
     def split(value):
         high = value.astype(jnp.bfloat16)
         return high, (value - high.astype(jnp.float32)).astype(jnp.bfloat16)
 
-    def term_of(k):
-        spot = spot_of(col_ref[k])
-        high, low = split(amp_ref[pl.ds(pl.multiple_of(spot * size, size), size), :])
-        tile_high, tile_low = split(held_ref[lax.rem(k, HELD)])
+    def term_of(j):
+        high, low = split(amp_ref[pl.ds(pl.multiple_of(place_ref[j] * size, size), size), :])
+        tile_high, tile_low = split(held_ref[lax.rem(j, HELD)])
         term = jnp.dot(tile_high, high, preferred_element_type=jnp.float32)
         term += jnp.dot(tile_high, low, preferred_element_type=jnp.float32)
         return term + jnp.dot(tile_low, high, preferred_element_type=jnp.float32)
 
-    def add_term(k, term):
-        spot = pl.multiple_of(row_ref[k] * 32, 32)
+    def add_term(j, term):
+        spot = pl.multiple_of(row_ref[slot_ref[j]] * 32, 32)
         for hi in range(8):
             for c in range(CHUNKS):
                 acc_ref[c, hi, pl.ds(spot, 32), :] += term[
                     hi * 32 : hi * 32 + 32, c * LANES : (c + 1) * LANES
                 ]
 
-    def add_group(j, carry):
+    def add_group(g, carry):
         for i in range(GROUP):
-            tile_copy(GROUP * j + i).wait()
-        terms = [term_of(GROUP * j + i) for i in range(GROUP)]
+            tile_copy(GROUP * g + i).wait()
+        terms = [term_of(GROUP * g + i) for i in range(GROUP)]
         for i in range(GROUP):
-            add_term(GROUP * j + i, terms[i])
+            add_term(GROUP * g + i, terms[i])
         for i in range(GROUP):
-            fetch(GROUP * j + i + HELD)
+            fetch(GROUP * g + i + HELD)
         return carry
 
-    def add_one(k, carry):
-        tile_copy(k).wait()
-        add_term(k, term_of(k))
+    def add_one(j, carry):
+        tile_copy(j).wait()
+        add_term(j, term_of(j))
         return carry
 
     groups = count // GROUP
     lax.fori_loop(0, groups, add_group, 0)
     lax.fori_loop(groups * GROUP, count, add_one, 0)
 
+    if not last:
+        copy = pltpu.make_async_copy(acc_ref, outs[0], acc_sem)
+        copy.start()
+        copy.wait()
+        return
     me_cd = lax.axis_index("cd")
     size_cd = acc_ref.shape[1]
     parts = out_parts(acc_ref.shape[2], size_cd)
@@ -160,37 +174,45 @@
         copy.wait()
 
 
-def ladder(tile_row, tile_col, tile_count, tiles, pieces, blocks):
+def ladder(tile_row, tile_col, tile_count, tiles, pieces, so_far, blocks):
     slots, size, _ = tiles.shape
     width = pieces[0].shape[1]
     total = sum(piece.shape[0] for piece in pieces)
     size_cd = lax.axis_size("cd")
-    parts = out_parts(blocks * 32, size_cd)
     smem = pl.BlockSpec(memory_space=pltpu.SMEM)
     hbm = pl.BlockSpec(memory_space=pl.ANY)
-    outs = [jax.ShapeDtypeStruct((rows, LANES), jnp.float32) for _, _, rows in parts] * CHUNKS
-    given = pl.pallas_call(
-        functools.partial(ladder_kernel, pieces_given=len(pieces), outs_given=len(outs)),
-        in_specs=[smem] * 3 + [hbm] * (1 + len(pieces)),
+    acc = (CHUNKS, size_cd, blocks * 32, LANES)
+    if so_far:
+        outs = [(rows, LANES) for _, _, rows in out_parts(blocks * 32, size_cd)] * CHUNKS
+    else:
+        outs = [acc]
+    share = total / (2 * SIDE * SIDE * size)
+    return pl.pallas_call(
+        functools.partial(ladder_kernel, pieces_given=len(pieces), last=len(so_far)),
+        in_specs=[smem] * 3 + [hbm] * (1 + len(pieces) + len(so_far)),
         out_specs=[hbm] * len(outs),
-        out_shape=outs,
+        out_shape=[jax.ShapeDtypeStruct(shape, jnp.float32) for shape in outs],
         scratch_shapes=[
             pltpu.VMEM((total, width), jnp.float32),
             pltpu.VMEM((HELD, size, size), jnp.float32),
-            pltpu.VMEM((CHUNKS, size_cd, blocks * 32, LANES), jnp.float32),
+            pltpu.VMEM(acc, jnp.float32),
+            pltpu.SMEM((slots,), jnp.int32),
+            pltpu.SMEM((slots,), jnp.int32),
             pltpu.SemaphoreType.DMA((len(pieces),)),
             pltpu.SemaphoreType.DMA((HELD,)),
             pltpu.SemaphoreType.DMA((len(outs),)),
+            pltpu.SemaphoreType.DMA,
         ],
         compiler_params=pltpu.CompilerParams(vmem_limit_bytes=56 * 1024 * 1024),
         cost_estimate=pl.CostEstimate(
-            flops=slots * 6 * size * size * width,
-            bytes_accessed=slots * size * size * 4 + total * width * 4 + blocks * size * width * 4,
+            flops=int(share * slots * 6 * size * size * width),
+            bytes_accessed=int(share * slots * size * size * 4)
+            + total * width * 4
+            + (1 + len(so_far)) * blocks * size * width * 4,
             transcendentals=0,
         ),
-        name="ladder",
-    )(tile_row, tile_col, tile_count, tiles, *pieces)
-    return [given[c * len(parts) : (c + 1) * len(parts)] for c in range(CHUNKS)]
+        name="ladder_last" if so_far else "ladder",
+    )(tile_row, tile_col, tile_count, tiles, *pieces, *so_far)
 
 
 def shift_line(block, step):
@@ -289,9 +311,11 @@
     occ_dev = amplitudes.shape[0]
     blocks = lax.axis_size("ab")
 
-    pieces = gather_plane(amplitudes.T)
-    given = ladder(tile_row, tile_col, tile_count, integrals, pieces, blocks)
-    sums = [ring_terms(blocks_of) for blocks_of in given]
+    near, far = gather_plane(amplitudes.T)
+    so_far = ladder(tile_row, tile_col, tile_count, integrals, near, [], blocks)
+    given = ladder(tile_row, tile_col, tile_count, integrals, far, so_far, blocks)
+    each = len(given) // CHUNKS
+    sums = [ring_terms(given[c * each : (c + 1) * each]) for c in range(CHUNKS)]
     direct = merge(sums)
     outgoing = direct.reshape(-1, 8, LANES)
     arrived = lax.all_to_all(outgoing, ("ab", "cd"), split_axis=0, concat_axis=0, tiled=True)

time: 168 us -> 161 us (0.958)
  waiting for transfers between devices: 52.5 us -> 39 us
  Pallas kernels: 15.7 us -> 25.4 us
  starting transfers between devices: 55.7 us -> 49.1 us
  local copies, waits for them, and re-layouts: 2.97 us -> 7.55 us
    ppermute x4, waiting for transfers between devices: 24.7 us -> 0.01 us  [both_ways(): lax.ppermute(block, 'ab', plane_route(-dx, -dy))]
    ppermute x4, waiting for transfers between devices: 0.43 us -> 20.8 us  [both_ways(): lax.ppermute(block, 'ab', plane_route(dx, dy))]
    pallas_call x1 -> x2, Pallas kernels: 11 us -> 20.7 us  [ladder(): pl.pallas_call(functools.partial(ladder_kernel, pieces_given=len(pieces),...]
    ppermute x16, starting transfers between devices: 28.5 us -> 19.9 us  [shift_line(): lax.ppermute(block, 'cd', [(i, (i + step) % size) for i in range(size)])]
    ppermute x2, waiting for transfers between devices: 7.09 us -> 0.01 us  [far_halves(): lax.ppermute(above[half:], 'ab', plane_route(-dx, -dy))]
    ppermute x2, waiting for transfers between devices: 5.05 us -> 0.01 us  [far_halves(): lax.ppermute(below[:half], 'ab', plane_route(dx, dy))]
    ppermute x2, waiting for transfers between devices: 0.01 us -> 4.36 us  [first_line(): far = lax.ppermute(block, 'ab', plane_route(2 * dx, 2 * dy))]
    ppermute x4, starting transfers between devices: 2.68 us -> 5.18 us  [both_ways(): lax.ppermute(block, 'ab', plane_route(dx, dy))]
  transfers between devices with their start and end apart: 31 -> 31, of which waited for: 15 -> 14; matrix products, arithmetic and copies ran while one was open for 7% -> 10% of each run, Pallas kernels for 0% -> 7%
where the time goes in v4:
time: 161 us; the launch traced here: 160 us
  starting transfers between devices  49.1 us (30%)
  waiting for transfers between devices  39 us (24%)
  blocking collectives  26.1 us (16%)
  Pallas kernels  25.4 us (16%)
  other arithmetic  12.1 us (8%)
  local copies, waits for them, and re-layouts  7.55 us (5%)
    all_to_all x1, blocking collectives, per_device(): lax.all_to_all(outgoing, ('ab', 'cd'), split_axis=0, concat_axis=0, tiled...  26.1 us
    ppermute x4, waiting for transfers between devices, both_ways(): lax.ppermute(block, 'ab', plane_route(dx, dy))  20.8 us
    pallas_call x2, Pallas kernels, ladder(): pl.pallas_call(functools.partial(ladder_kernel, pieces_given=len(pieces),...  20.7 us
    ppermute x16, starting transfers between devices, shift_line(): lax.ppermute(block, 'cd', [(i, (i + step) % size) for i in range(size)])  19.9 us
    ppermute x16, waiting for transfers between devices, shift_line(): lax.ppermute(block, 'cd', [(i, (i + step) % size) for i in range(size)])  12.2 us
    ppermute x4, starting transfers between devices, both_ways(): lax.ppermute(block, 'ab', plane_route(-dx, -dy))  6.74 us
    ppermute x1, starting transfers between devices, per_device(): lax.ppermute(arrived, 'ij', [(0, 1), (1, 0)]).reshape(direct.shape)  6.2 us
    ppermute x2, starting transfers between devices, first_line(): far = lax.ppermute(block, 'ab', plane_route(2 * dx, 2 * dy))  5.76 us
  transfers between devices with their start and end apart: 31, of which 14 were waited for; matrix products, arithmetic and copies ran while one was open for 10% of the time, Pallas kernels for 7%

profile of v4, /device:TPU:1, one launch (start us, length us, event | category | flops | bytes accessed | tf_op | source)
XLA Modules:
  0.0 160.4 jit_solution(3950106904315134906)
XLA Ops:
  0.0 1.2 copy.6
  1.3 2.2 %collective-permute-start.7 = (f32[256,256]{1,0:T(8,128)S(1)}, f32[256,256]{1,0:T(8,128)S(1)}, u32[]{:S(2)}, u32[]{:S(2)}) collective-permute-start(f32[256,256]{1,0:T(8,128)S(1)} %get-tuple-element.41), channel_id=1, source_target_pairs={{0,64},{16,80},{32,96},{48,112},{64,128},{80,144},{96,160},{112,17... | collective-permute-start | bytes 786440 | tf_op jit(solution)/shard_map/ppermute | solution.py:27
  3.5 1.5 collective-permute-start.8
  5.0 1.6 collective-permute-start.9
  6.6 1.2 collective-permute-start
  7.8 1.5 collective-permute-start.1
  9.3 4.2 %collective-permute-start.2 = (f32[256,256]{1,0:T(8,128)S(1)}, f32[256,256]{1,0:T(8,128)S(1)}, u32[]{:S(2)}, u32[]{:S(2)}) collective-permute-start(f32[256,256]{1,0:T(8,128)S(1)} %get-tuple-element.42), channel_id=1, source_target_pairs={{0,32},{16,48},{32,0},{48,16},{64,96},{80,112},{96,64},{112,80},{1... | collective-permute-start | bytes 786440 | tf_op jit(solution)/shard_map/ppermute | solution.py:42
  13.5 4.0 %collective-permute-done.9 = f32[256,256]{1,0:T(8,128)S(1)} collective-permute-done((f32[256,256]{1,0:T(8,128)S(1)}, f32[256,256]{1,0:T(8,128)S(1)}, u32[]{:S(2)}, u32[]{:S(2)}) %collective-permute-start.9) | collective-permute-done | bytes 262176 | tf_op jit(solution)/shard_map/ppermute | solution.py:42
  17.5 1.3 collective-permute-start.10
  18.8 1.5 collective-permute-start.12
  21.2 2.3 %collective-permute-start.5 = (f32[1024,256]{1,0:T(8,128)S(1)}, f32[1024,256]{1,0:T(8,128)S(1)}, u32[]{:S(2)}, u32[]{:S(2)}) collective-permute-start(f32[1024,256]{1,0:T(8,128)S(1)} %pad_maximum_fusion.rest_0_), channel_id=1, source_target_pairs={{0,192},{16,208},{32,224},{48,240},{64,0},{80,16},{96,32},{112,48}... | collective-permute-start | bytes 3145736 | tf_op jit(solution)/shard_map/ppermute | solution.py:28
  23.5 20.8 %collective-permute-done.10.rest_4_ = f32[1024,256]{1,0:T(8,128)S(1)} collective-permute-done((f32[1024,256]{1,0:T(8,128)S(1)}, f32[1024,256]{1,0:T(8,128)S(1)}, u32[]{:S(2)}, u32[]{:S(2)}) %collective-permute-start.10) | collective-permute-done | bytes 1048608 | tf_op jit(solution)/shard_map/ppermute | solution.py:27
  44.3 0.9 slice.60
  45.3 0.9 slice.61
  46.1 2.7 %collective-permute-start.13 = (f32[512,256]{1,0:T(8,128)}, f32[512,256]{1,0:T(8,128)S(1)}, u32[]{:S(2)}, u32[]{:S(2)}) collective-permute-start(f32[512,256]{1,0:T(8,128)} %slice.61), channel_id=1, source_target_pairs={{0,48},{16,0},{32,16},{48,32},{64,112},{80,64},{96,80},{112,96},{1... | collective-permute-start | bytes 1572872 | tf_op jit(solution)/shard_map/ppermute | solution.py:37
  48.8 0.9 slice.57
  49.7 0.9 slice.58
  50.7 2.7 %collective-permute-start.6 = (f32[512,256]{1,0:T(8,128)}, f32[512,256]{1,0:T(8,128)}, u32[]{:S(2)}, u32[]{:S(2)}) collective-permute-start(f32[512,256]{1,0:T(8,128)} %slice.58), channel_id=1, source_target_pairs={{0,192},{16,208},{32,224},{48,240},{64,0},{80,16},{96,32},{112,48}... | collective-permute-start | bytes 1572872 | tf_op jit(solution)/shard_map/ppermute | solution.py:37
  54.0 11.8 %ladder.1.rest_4_ = f32[2,8,512,128]{3,2,1,0:T(8,128)} custom-call(s32[46]{0:T(128)} %row_ref.3, s32[46]{0:T(128)} %col_ref.3, s32[1]{0:T(128)S(6)} %copy.8.count_ref, f32[46,256,256]{2,1,0:T(8,128)} %tiles_ref.3, f32[1024,256]{1,0:T(8,128)} %copy-done.1, f32[1024,256]{1,0:T(8,128)} %copy-done.4, f32[1024,256]{1,0:T(8,128)} %copy-done.5, ...), custom_call_target="tpu_custom_call" | custom-call | flops 3472883712 | bytes 19529728 | tf_op jit(solution)/shard_map/ladder/pallas_call | solution.py:190
  67.0 9.0 %ladder_last.1 = (f32[256,128]{1,0:T(8,128)}, f32[256,128]{1,0:T(8,128)}, f32[512,128]{1,0:T(8,128)}, f32[512,128]{1,0:T(8,128)}, f32[512,128]{1,0:T(8,128)}, /*...) custom-call(s32[46]{0:T(128)} %row_ref.3, ...), custom_call_target="tpu_custom_call" | custom-call | flops 1157627904 | bytes 13500416 | tf_op jit(solution)/shard_map/ladder_last/pallas_call | solution.py:190
  76.0 1.5 collective-permute-start.22
  77.5 2.0 %collective-permute-start.18 = (f32[256,128]{1,0:T(8,128)}, f32[256,128]{1,0:T(8,128)S(1)}, u32[]{:S(2)}, u32[]{:S(2)}) collective-permute-start(f32[256,128]{1,0:T(8,128)} %get-tuple-element.30), channel_id=1, source_target_pairs={{0,14},{2,0},{4,2},{6,4},{8,6},{10,8},{12,10},{14,12},{1,15},{3,1}... | collective-permute-start | bytes 393224 | tf_op jit(solution)/shard_map/ppermute | solution.py:220
  80.1 1.0 fusion.1
  81.1 2.2 %collective-permute-start.27 = (f32[512,128]{1,0:T(8,128)S(1)}, f32[512,128]{1,0:T(8,128)S(1)}, u32[]{:S(2)}, u32[]{:S(2)}) collective-permute-start(f32[512,128]{1,0:T(8,128)S(1)} %pad_maximum_fusion.5), channel_id=1, source_target_pairs={{0,14},{2,0},{4,2},{6,4},{8,6},{10,8},{12,10},{14,12},{1,15},{3,1}... | collective-permute-start | bytes 786440 | tf_op jit(solution)/shard_map/ppermute | solution.py:220
  83.2 1.0 slice_add_fusion.1
  84.4 1.0 fusion.2
  85.4 2.7 %collective-permute-start.19 = (f32[512,128]{1,0:T(8,128)S(1)}, f32[512,128]{1,0:T(8,128)S(1)}, u32[]{:S(2)}, u32[]{:S(2)}) collective-permute-start(f32[512,128]{1,0:T(8,128)S(1)} %pad_maximum_fusion.3), channel_id=1, source_target_pairs={{0,14},{2,0},{4,2},{6,4},{8,6},{10,8},{12,10},{14,12},{1,15},{3,1}... | collective-permute-start | bytes 786440 | tf_op jit(solution)/shard_map/ppermute | solution.py:220
  88.1 1.0 slice_add_fusion.3
  89.3 1.0 add.46
  90.2 2.7 %collective-permute-start.28 = (f32[512,128]{1,0:T(8,128)S(1)}, f32[512,128]{1,0:T(8,128)S(1)}, u32[]{:S(2)}, u32[]{:S(2)}) collective-permute-start(f32[512,128]{1,0:T(8,128)S(1)} %add.46), channel_id=1, source_target_pairs={{0,14},{2,0},{4,2},{6,4},{8,6},{10,8},{12,10},{14,12},{1,15},{3,1}... | collective-permute-start | bytes 786440 | tf_op jit(solution)/shard_map/ppermute | solution.py:220
  93.0 1.0 add.43
  94.1 1.0 add.40
  95.1 2.7 %collective-permute-start.20 = (f32[512,128]{1,0:T(8,128)S(1)}, f32[512,128]{1,0:T(8,128)S(1)}, u32[]{:S(2)}, u32[]{:S(2)}) collective-permute-start(f32[512,128]{1,0:T(8,128)S(1)} %add.40), channel_id=1, source_target_pairs={{0,14},{2,0},{4,2},{6,4},{8,6},{10,8},{12,10},{14,12},{1,15},{3,1}... | collective-permute-start | bytes 786440 | tf_op jit(solution)/shard_map/ppermute | solution.py:220
  98.0 1.0 add.37
  99.6 1.0 add.47
  100.6 2.9 %collective-permute-start.29 = (f32[512,128]{1,0:T(8,128)S(1)}, f32[512,128]{1,0:T(8,128)S(1)}, u32[]{:S(2)}, u32[]{:S(2)}) collective-permute-start(f32[512,128]{1,0:T(8,128)S(1)} %add.47), channel_id=1, source_target_pairs={{0,14},{2,0},{4,2},{6,4},{8,6},{10,8},{12,10},{14,12},{1,15},{3,1}... | collective-permute-start | bytes 786440 | tf_op jit(solution)/shard_map/ppermute | solution.py:220
  103.6 1.0 add.44
  105.2 1.0 add.41
  106.2 2.6 %collective-permute-start.21 = (f32[512,128]{1,0:T(8,128)S(1)}, f32[512,128]{1,0:T(8,128)S(1)}, u32[]{:S(2)}, u32[]{:S(2)}) collective-permute-start(f32[512,128]{1,0:T(8,128)S(1)} %add.41), channel_id=1, source_target_pairs={{0,14},{2,0},{4,2},{6,4},{8,6},{10,8},{12,10},{14,12},{1,15},{3,1}... | collective-permute-start | bytes 786440 | tf_op jit(solution)/shard_map/ppermute | solution.py:220
  109.0 1.0 add.38
  110.8 3.7 %collective-permute-done.25.refs_3_ = f32[512,128]{1,0:T(8,128)S(1)} collective-permute-done((f32[512,128]{1,0:T(8,128)S(1)}, f32[512,128]{1,0:T(8,128)S(1)}, u32[]{:S(2)}, u32[]{:S(2)}) %collective-permute-start.25) | collective-permute-done | bytes 262176 | tf_op jit(solution)/shard_map/ppermute | solution.py:220
  114.6 1.9 %collective-permute-done.21.refs_1_ = f32[512,128]{1,0:T(8,128)S(1)} collective-permute-done((f32[512,128]{1,0:T(8,128)S(1)}, f32[512,128]{1,0:T(8,128)S(1)}, u32[]{:S(2)}, u32[]{:S(2)}) %collective-permute-start.21) | collective-permute-done | bytes 262176 | tf_op jit(solution)/shard_map/ppermute | solution.py:220
  116.4 3.8 %collective-permute-done.17.refs_0_ = f32[512,128]{1,0:T(8,128)S(1)} collective-permute-done((f32[512,128]{1,0:T(8,128)S(1)}, f32[512,128]{1,0:T(8,128)S(1)}, u32[]{:S(2)}, u32[]{:S(2)}) %collective-permute-start.17) | collective-permute-done | bytes 262176 | tf_op jit(solution)/shard_map/ppermute | solution.py:220
  120.9 2.4 %merge.1.direct_any = f32[1024,128]{1,0:T(8,128)} custom-call(f32[512,128]{1,0:T(8,128)} %copy-done.13, f32[512,128]{1,0:T(8,128)} %copy-done.12, f32[512,128]{1,0:T(8,128)} %get-tuple-element.31.refs_2_, f32[512,128]{1,0:T(8,128)} %copy-done.11, f32[512,128]{1,0:T(8,128)} %copy-done.10, f32[512,128]{1,0:T(8,128)} %get-tuple-element.40.refs_5_), custom_call_target="tpu_custom_call" | custom-call | tf_op jit(solution)/shard_map/merge/pallas_call | solution.py:268
  123.2 26.1 %all_to_all.5 = f32[128,8,128]{2,1,0:T(8,128)S(1)} all-to-all(f32[128,8,128]{2,1,0:T(8,128)} %bitcast.6), channel_id=1, replica_groups=mesh['ab'=16,'cd'=8,'ij'=2] {'ab','cd'}, dimensions={0} | all-to-all | bytes 1048576 | tf_op jit(solution)/shard_map/all_to_all | solution.py:321
  149.3 6.2 %collective-permute-start.30 = (f32[128,8,128]{2,1,0:T(8,128)S(1)}, f32[128,8,128]{2,1,0:T(8,128)S(1)}, u32[]{:S(2)}, u32[]{:S(2)}) collective-permute-start(f32[128,8,128]{2,1,0:T(8,128)S(1)} %all_to_all.5), channel_id=1, source_target_pairs={{0,1},{1,0},{2,3},{3,2},{4,5},{5,4},{6,7},{7,6},{8,9},{9,8},{10,11... | collective-permute-start | bytes 1572872 | tf_op jit(solution)/shard_map/ppermute | solution.py:322
  155.5 1.5 collective-permute-done.30
  157.9 2.3 %finish.1 = f32[256,2,256]{2,1,0:T(2,128)} custom-call(f32[1024,128]{1,0:T(8,128)} %merge.1.direct_any, f32[1024,128]{1,0:T(8,128)} %bitcast.8), custom_call_target="tpu_custom_call" | custom-call | tf_op jit(solution)/shard_map/finish/pallas_call | solution.py:296
  (71 shorter events, 7.2 us)
Async XLA Ops:
  1.3 8.0 %collective-permute-start.7 = (f32[256,256]{1,0:T(8,128)S(1)}, f32[256,256]{1,0:T(8,128)S(1)}, u32[]{:S(2)}, u32[]{:S(2)}) collective-permute-start(f32[256,256]{1,0:T(8,128)S(1)} %get-tuple-element.41), channel_id=1, source_target_pairs={{0,64},{16,80},{32,96},{48,112},{64,128},{80,144},{96,160},{112,17... | collective-permute-start | bytes 786440 | tf_op jit(solution)/shard_map/ppermute | solution.py:27
  3.5 10.0 %collective-permute-start.8 = (f32[256,256]{1,0:T(8,128)S(1)}, f32[256,256]{1,0:T(8,128)S(1)}, u32[]{:S(2)}, u32[]{:S(2)}) collective-permute-start(f32[256,256]{1,0:T(8,128)S(1)} %get-tuple-element.41), channel_id=1, source_target_pairs={{0,192},{16,208},{32,224},{48,240},{64,0},{80,16},{96,32},{112,48}... | collective-permute-start | bytes 786440 | tf_op jit(solution)/shard_map/ppermute | solution.py:28
  5.0 12.4 %collective-permute-start.9 = (f32[256,256]{1,0:T(8,128)S(1)}, f32[256,256]{1,0:T(8,128)S(1)}, u32[]{:S(2)}, u32[]{:S(2)}) collective-permute-start(f32[256,256]{1,0:T(8,128)S(1)} %get-tuple-element.41), channel_id=1, source_target_pairs={{0,128},{16,144},{32,160},{48,176},{64,192},{80,208},{96,224},{112... | collective-permute-start | bytes 786440 | tf_op jit(solution)/shard_map/ppermute | solution.py:42
  6.6 13.7 %collective-permute-start = (f32[256,256]{1,0:T(8,128)S(1)}, f32[256,256]{1,0:T(8,128)S(1)}, u32[]{:S(2)}, u32[]{:S(2)}) collective-permute-start(f32[256,256]{1,0:T(8,128)S(1)} %get-tuple-element.42), channel_id=1, source_target_pairs={{0,16},{16,32},{32,48},{48,0},{64,80},{80,96},{96,112},{112,64},{1... | collective-permute-start | bytes 786440 | tf_op jit(solution)/shard_map/ppermute | solution.py:27
  7.8 12.5 %collective-permute-start.1 = (f32[256,256]{1,0:T(8,128)S(1)}, f32[256,256]{1,0:T(8,128)S(1)}, u32[]{:S(2)}, u32[]{:S(2)}) collective-permute-start(f32[256,256]{1,0:T(8,128)S(1)} %get-tuple-element.42), channel_id=1, source_target_pairs={{0,48},{16,0},{32,16},{48,32},{64,112},{80,64},{96,80},{112,96},{1... | collective-permute-start | bytes 786440 | tf_op jit(solution)/shard_map/ppermute | solution.py:28
  9.3 11.4 %collective-permute-start.2 = (f32[256,256]{1,0:T(8,128)S(1)}, f32[256,256]{1,0:T(8,128)S(1)}, u32[]{:S(2)}, u32[]{:S(2)}) collective-permute-start(f32[256,256]{1,0:T(8,128)S(1)} %get-tuple-element.42), channel_id=1, source_target_pairs={{0,32},{16,48},{32,0},{48,16},{64,96},{80,112},{96,64},{112,80},{1... | collective-permute-start | bytes 786440 | tf_op jit(solution)/shard_map/ppermute | solution.py:42
  17.5 36.5 %copy-start = (f32[1024,256]{1,0:T(8,128)}, f32[1024,256]{1,0:T(8,128)S(1)}, u32[]{:S(2)}) copy-start(f32[1024,256]{1,0:T(8,128)S(1)} %pad_maximum_fusion.1.rest_3_) | copy-start | bytes 3145732
  17.5 26.8 %collective-permute-start.10 = (f32[1024,256]{1,0:T(8,128)S(1)}, f32[1024,256]{1,0:T(8,128)S(1)}, u32[]{:S(2)}, u32[]{:S(2)}) collective-permute-start(f32[1024,256]{1,0:T(8,128)S(1)} %pad_maximum_fusion.1.rest_3_), channel_id=1, source_target_pairs={{0,16},{16,32},{32,48},{48,0},{64,80},{80,96},{96,112},{112,64},{1... | collective-permute-start | bytes 3145736 | tf_op jit(solution)/shard_map/ppermute | solution.py:27
  18.8 26.4 %collective-permute-start.12 = (f32[1024,256]{1,0:T(8,128)S(1)}, f32[1024,256]{1,0:T(8,128)S(1)}, u32[]{:S(2)}, u32[]{:S(2)}) collective-permute-start(f32[1024,256]{1,0:T(8,128)S(1)} %pad_maximum_fusion.1.rest_3_), channel_id=1, source_target_pairs={{0,48},{16,0},{32,16},{48,32},{64,112},{80,64},{96,80},{112,96},{1... | collective-permute-start | bytes 3145736 | tf_op jit(solution)/shard_map/ppermute | solution.py:28
  20.7 33.3 %copy-start.1 = (f32[1024,256]{1,0:T(8,128)}, f32[1024,256]{1,0:T(8,128)S(1)}, u32[]{:S(2)}) copy-start(f32[1024,256]{1,0:T(8,128)S(1)} %pad_maximum_fusion.rest_0_) | copy-start | bytes 3145732
  20.8 28.1 %collective-permute-start.3 = (f32[1024,256]{1,0:T(8,128)S(1)}, f32[1024,256]{1,0:T(8,128)S(1)}, u32[]{:S(2)}, u32[]{:S(2)}) collective-permute-start(f32[1024,256]{1,0:T(8,128)S(1)} %pad_maximum_fusion.rest_0_), channel_id=1, source_target_pairs={{0,64},{16,80},{32,96},{48,112},{64,128},{80,144},{96,160},{112,17... | collective-permute-start | bytes 3145736 | tf_op jit(solution)/shard_map/ppermute | solution.py:27
  21.2 28.5 %collective-permute-start.5 = (f32[1024,256]{1,0:T(8,128)S(1)}, f32[1024,256]{1,0:T(8,128)S(1)}, u32[]{:S(2)}, u32[]{:S(2)}) collective-permute-start(f32[1024,256]{1,0:T(8,128)S(1)} %pad_maximum_fusion.rest_0_), channel_id=1, source_target_pairs={{0,192},{16,208},{32,224},{48,240},{64,0},{80,16},{96,32},{112,48}... | collective-permute-start | bytes 3145736 | tf_op jit(solution)/shard_map/ppermute | solution.py:28
  44.3 9.7 %copy-start.2 = (f32[1024,256]{1,0:T(8,128)}, f32[1024,256]{1,0:T(8,128)S(1)}, u32[]{:S(2)}) copy-start(f32[1024,256]{1,0:T(8,128)S(1)} %collective-permute-done.10.rest_4_) | copy-start | bytes 3145732
  45.2 20.6 %collective-permute-start.11 = (f32[512,256]{1,0:T(8,128)}, f32[512,256]{1,0:T(8,128)S(1)}, u32[]{:S(2)}, u32[]{:S(2)}) collective-permute-start(f32[512,256]{1,0:T(8,128)} %slice.60), channel_id=1, source_target_pairs={{0,16},{16,32},{32,48},{48,0},{64,80},{80,96},{96,112},{112,64},{1... | collective-permute-start | bytes 1572872 | tf_op jit(solution)/shard_map/ppermute | solution.py:36
  45.3 8.8 %copy-start.3 = (f32[1024,256]{1,0:T(8,128)}, f32[1024,256]{1,0:T(8,128)S(1)}, u32[]{:S(2)}) copy-start(f32[1024,256]{1,0:T(8,128)S(1)} %collective-permute-done.12.rest_5_) | copy-start | bytes 3145732
  46.1 19.7 %collective-permute-start.13 = (f32[512,256]{1,0:T(8,128)}, f32[512,256]{1,0:T(8,128)S(1)}, u32[]{:S(2)}, u32[]{:S(2)}) collective-permute-start(f32[512,256]{1,0:T(8,128)} %slice.61), channel_id=1, source_target_pairs={{0,48},{16,0},{32,16},{48,32},{64,112},{80,64},{96,80},{112,96},{1... | collective-permute-start | bytes 1572872 | tf_op jit(solution)/shard_map/ppermute | solution.py:37
  48.8 5.2 %copy-start.4 = (f32[1024,256]{1,0:T(8,128)}, f32[1024,256]{1,0:T(8,128)S(1)}, u32[]{:S(2)}) copy-start(f32[1024,256]{1,0:T(8,128)S(1)} %collective-permute-done.3.rest_1_) | copy-start | bytes 3145732
  49.7 16.2 %collective-permute-start.4 = (f32[512,256]{1,0:T(8,128)}, f32[512,256]{1,0:T(8,128)S(1)}, u32[]{:S(2)}, u32[]{:S(2)}) collective-permute-start(f32[512,256]{1,0:T(8,128)} %slice.57), channel_id=1, source_target_pairs={{0,64},{16,80},{32,96},{48,112},{64,128},{80,144},{96,160},{112,17... | collective-permute-start | bytes 1572872 | tf_op jit(solution)/shard_map/ppermute | solution.py:36
  49.7 4.3 %copy-start.5 = (f32[1024,256]{1,0:T(8,128)}, f32[1024,256]{1,0:T(8,128)S(1)}, u32[]{:S(2)}) copy-start(f32[1024,256]{1,0:T(8,128)S(1)} %collective-permute-done.5.rest_2_) | copy-start | bytes 3145732
  50.7 15.2 %collective-permute-start.6 = (f32[512,256]{1,0:T(8,128)}, f32[512,256]{1,0:T(8,128)}, u32[]{:S(2)}, u32[]{:S(2)}) collective-permute-start(f32[512,256]{1,0:T(8,128)} %slice.58), channel_id=1, source_target_pairs={{0,192},{16,208},{32,224},{48,240},{64,0},{80,16},{96,32},{112,48}... | collective-permute-start | bytes 1572872 | tf_op jit(solution)/shard_map/ppermute | solution.py:37
  65.9 0.8 copy-start.6
  65.9 1.0 copy-start.7
  65.9 1.1 copy-start.8
  76.0 4.1 %collective-permute-start.26 = (f32[256,128]{1,0:T(8,128)}, f32[256,128]{1,0:T(8,128)S(1)}, u32[]{:S(2)}, u32[]{:S(2)}) collective-permute-start(f32[256,128]{1,0:T(8,128)} %get-tuple-element.39), channel_id=1, source_target_pairs={{0,14},{2,0},{4,2},{6,4},{8,6},{10,8},{12,10},{14,12},{1,15},{3,1}... | collective-permute-start | bytes 393224 | tf_op jit(solution)/shard_map/ppermute | solution.py:220
  76.0 7.2 %collective-permute-start.22 = (f32[256,128]{1,0:T(8,128)}, f32[256,128]{1,0:T(8,128)S(1)}, u32[]{:S(2)}, u32[]{:S(2)}) collective-permute-start(f32[256,128]{1,0:T(8,128)} %get-tuple-element.35), channel_id=1, source_target_pairs={{0,2},{2,4},{4,6},{6,8},{8,10},{10,12},{12,14},{14,0},{1,3},{3,5},... | collective-permute-start | bytes 393224 | tf_op jit(solution)/shard_map/ppermute | solution.py:220
  77.5 6.9 %collective-permute-start.18 = (f32[256,128]{1,0:T(8,128)}, f32[256,128]{1,0:T(8,128)S(1)}, u32[]{:S(2)}, u32[]{:S(2)}) collective-permute-start(f32[256,128]{1,0:T(8,128)} %get-tuple-element.30), channel_id=1, source_target_pairs={{0,14},{2,0},{4,2},{6,4},{8,6},{10,8},{12,10},{14,12},{1,15},{3,1}... | collective-permute-start | bytes 393224 | tf_op jit(solution)/shard_map/ppermute | solution.py:220
  79.5 8.7 %collective-permute-start.14 = (f32[256,128]{1,0:T(8,128)}, f32[256,128]{1,0:T(8,128)S(1)}, u32[]{:S(2)}, u32[]{:S(2)}) collective-permute-start(f32[256,128]{1,0:T(8,128)} %get-tuple-element.26), channel_id=1, source_target_pairs={{0,2},{2,4},{4,6},{6,8},{8,10},{10,12},{12,14},{14,0},{1,3},{3,5},... | collective-permute-start | bytes 393224 | tf_op jit(solution)/shard_map/ppermute | solution.py:220
  81.1 8.2 %collective-permute-start.27 = (f32[512,128]{1,0:T(8,128)S(1)}, f32[512,128]{1,0:T(8,128)S(1)}, u32[]{:S(2)}, u32[]{:S(2)}) collective-permute-start(f32[512,128]{1,0:T(8,128)S(1)} %pad_maximum_fusion.5), channel_id=1, source_target_pairs={{0,14},{2,0},{4,2},{6,4},{8,6},{10,8},{12,10},{14,12},{1,15},{3,1}... | collective-permute-start | bytes 786440 | tf_op jit(solution)/shard_map/ppermute | solution.py:220
  84.3 8.7 %collective-permute-start.23 = (f32[512,128]{1,0:T(8,128)S(1)}, f32[512,128]{1,0:T(8,128)S(1)}, u32[]{:S(2)}, u32[]{:S(2)}) collective-permute-start(f32[512,128]{1,0:T(8,128)S(1)} %pad_maximum_fusion.4), channel_id=1, source_target_pairs={{0,2},{2,4},{4,6},{6,8},{8,10},{10,12},{12,14},{14,0},{1,3},{3,5},... | collective-permute-start | bytes 786440 | tf_op jit(solution)/shard_map/ppermute | solution.py:220
  85.4 8.7 %collective-permute-start.19 = (f32[512,128]{1,0:T(8,128)S(1)}, f32[512,128]{1,0:T(8,128)S(1)}, u32[]{:S(2)}, u32[]{:S(2)}) collective-permute-start(f32[512,128]{1,0:T(8,128)S(1)} %pad_maximum_fusion.3), channel_id=1, source_target_pairs={{0,14},{2,0},{4,2},{6,4},{8,6},{10,8},{12,10},{14,12},{1,15},{3,1}... | collective-permute-start | bytes 786440 | tf_op jit(solution)/shard_map/ppermute | solution.py:220
  89.2 8.8 %collective-permute-start.15 = (f32[512,128]{1,0:T(8,128)S(1)}, f32[512,128]{1,0:T(8,128)S(1)}, u32[]{:S(2)}, u32[]{:S(2)}) collective-permute-start(f32[512,128]{1,0:T(8,128)S(1)} %pad_maximum_fusion.2), channel_id=1, source_target_pairs={{0,2},{2,4},{4,6},{6,8},{8,10},{10,12},{12,14},{14,0},{1,3},{3,5},... | collective-permute-start | bytes 786440 | tf_op jit(solution)/shard_map/ppermute | solution.py:220
  90.2 9.3 %collective-permute-start.28 = (f32[512,128]{1,0:T(8,128)S(1)}, f32[512,128]{1,0:T(8,128)S(1)}, u32[]{:S(2)}, u32[]{:S(2)}) collective-permute-start(f32[512,128]{1,0:T(8,128)S(1)} %add.46), channel_id=1, source_target_pairs={{0,14},{2,0},{4,2},{6,4},{8,6},{10,8},{12,10},{14,12},{1,15},{3,1}... | collective-permute-start | bytes 786440 | tf_op jit(solution)/shard_map/ppermute | solution.py:220
  94.0 9.6 %collective-permute-start.24 = (f32[512,128]{1,0:T(8,128)S(1)}, f32[512,128]{1,0:T(8,128)S(1)}, u32[]{:S(2)}, u32[]{:S(2)}) collective-permute-start(f32[512,128]{1,0:T(8,128)S(1)} %add.43), channel_id=1, source_target_pairs={{0,2},{2,4},{4,6},{6,8},{8,10},{10,12},{12,14},{14,0},{1,3},{3,5},... | collective-permute-start | bytes 786440 | tf_op jit(solution)/shard_map/ppermute | solution.py:220
  95.1 10.1 %collective-permute-start.20 = (f32[512,128]{1,0:T(8,128)S(1)}, f32[512,128]{1,0:T(8,128)S(1)}, u32[]{:S(2)}, u32[]{:S(2)}) collective-permute-start(f32[512,128]{1,0:T(8,128)S(1)} %add.40), channel_id=1, source_target_pairs={{0,14},{2,0},{4,2},{6,4},{8,6},{10,8},{12,10},{14,12},{1,15},{3,1}... | collective-permute-start | bytes 786440 | tf_op jit(solution)/shard_map/ppermute | solution.py:220
  99.0 10.0 %collective-permute-start.16 = (f32[512,128]{1,0:T(8,128)S(1)}, f32[512,128]{1,0:T(8,128)S(1)}, u32[]{:S(2)}, u32[]{:S(2)}) collective-permute-start(f32[512,128]{1,0:T(8,128)S(1)} %add.37), channel_id=1, source_target_pairs={{0,2},{2,4},{4,6},{6,8},{8,10},{10,12},{12,14},{14,0},{1,3},{3,5},... | collective-permute-start | bytes 786440 | tf_op jit(solution)/shard_map/ppermute | solution.py:220
  100.6 10.2 %collective-permute-start.29 = (f32[512,128]{1,0:T(8,128)S(1)}, f32[512,128]{1,0:T(8,128)S(1)}, u32[]{:S(2)}, u32[]{:S(2)}) collective-permute-start(f32[512,128]{1,0:T(8,128)S(1)} %add.47), channel_id=1, source_target_pairs={{0,14},{2,0},{4,2},{6,4},{8,6},{10,8},{12,10},{14,12},{1,15},{3,1}... | collective-permute-start | bytes 786440 | tf_op jit(solution)/shard_map/ppermute | solution.py:220
  104.6 10.0 %collective-permute-start.25 = (f32[512,128]{1,0:T(8,128)S(1)}, f32[512,128]{1,0:T(8,128)S(1)}, u32[]{:S(2)}, u32[]{:S(2)}) collective-permute-start(f32[512,128]{1,0:T(8,128)S(1)} %add.44), channel_id=1, source_target_pairs={{0,2},{2,4},{4,6},{6,8},{8,10},{10,12},{12,14},{14,0},{1,3},{3,5},... | collective-permute-start | bytes 786440 | tf_op jit(solution)/shard_map/ppermute | solution.py:220
  106.2 10.2 %collective-permute-start.21 = (f32[512,128]{1,0:T(8,128)S(1)}, f32[512,128]{1,0:T(8,128)S(1)}, u32[]{:S(2)}, u32[]{:S(2)}) collective-permute-start(f32[512,128]{1,0:T(8,128)S(1)} %add.41), channel_id=1, source_target_pairs={{0,14},{2,0},{4,2},{6,4},{8,6},{10,8},{12,10},{14,12},{1,15},{3,1}... | collective-permute-start | bytes 786440 | tf_op jit(solution)/shard_map/ppermute | solution.py:220
  110.0 10.2 %collective-permute-start.17 = (f32[512,128]{1,0:T(8,128)S(1)}, f32[512,128]{1,0:T(8,128)S(1)}, u32[]{:S(2)}, u32[]{:S(2)}) collective-permute-start(f32[512,128]{1,0:T(8,128)S(1)} %add.38), channel_id=1, source_target_pairs={{0,2},{2,4},{4,6},{6,8},{8,10},{10,12},{12,14},{14,0},{1,3},{3,5},... | collective-permute-start | bytes 786440 | tf_op jit(solution)/shard_map/ppermute | solution.py:220
  110.8 9.4 %copy-start.10 = (f32[512,128]{1,0:T(8,128)}, f32[512,128]{1,0:T(8,128)S(1)}, u32[]{:S(2)}) copy-start(f32[512,128]{1,0:T(8,128)S(1)} %collective-permute-done.29.refs_4_) | copy-start | bytes 786436
  114.6 5.6 %copy-start.11 = (f32[512,128]{1,0:T(8,128)}, f32[512,128]{1,0:T(8,128)S(1)}, u32[]{:S(2)}) copy-start(f32[512,128]{1,0:T(8,128)S(1)} %collective-permute-done.25.refs_3_) | copy-start | bytes 786436
  116.4 3.8 %copy-start.12 = (f32[512,128]{1,0:T(8,128)}, f32[512,128]{1,0:T(8,128)S(1)}, u32[]{:S(2)}) copy-start(f32[512,128]{1,0:T(8,128)S(1)} %collective-permute-done.21.refs_1_) | copy-start | bytes 786436
  120.2 0.7 copy-start.13
  149.3 7.7 %collective-permute-start.30 = (f32[128,8,128]{2,1,0:T(8,128)S(1)}, f32[128,8,128]{2,1,0:T(8,128)S(1)}, u32[]{:S(2)}, u32[]{:S(2)}) collective-permute-start(f32[128,8,128]{2,1,0:T(8,128)S(1)} %all_to_all.5), channel_id=1, source_target_pairs={{0,1},{1,0},{2,3},{3,2},{4,5},{5,4},{6,7},{7,6},{8,9},{9,8},{10,11... | collective-permute-start | bytes 1572872 | tf_op jit(solution)/shard_map/ppermute | solution.py:322
  157.1 0.8 copy-start.9

commit v5 on v4

--- a/solution.py
+++ b/solution.py
@@ -189,7 +189,7 @@
     share = total / (2 * SIDE * SIDE * size)
     return pl.pallas_call(
         functools.partial(ladder_kernel, pieces_given=len(pieces), last=len(so_far)),
-        in_specs=[smem] * 3 + [hbm] * (1 + len(pieces) + len(so_far)),
+        in_specs=[smem] * 3 + [pl.BlockSpec(memory_space=pltpu.HBM)] + [hbm] * (len(pieces) + len(so_far)),
         out_specs=[hbm] * len(outs),
         out_shape=[jax.ShapeDtypeStruct(shape, jnp.float32) for shape in outs],
         scratch_shapes=[
@@ -203,7 +203,7 @@
             pltpu.SemaphoreType.DMA((len(outs),)),
             pltpu.SemaphoreType.DMA,
         ],
-        compiler_params=pltpu.CompilerParams(vmem_limit_bytes=56 * 1024 * 1024),
+        compiler_params=pltpu.CompilerParams(vmem_limit_bytes=(14 if so_far else 18) * 1024 * 1024),
         cost_estimate=pl.CostEstimate(
             flops=int(share * slots * 6 * size * size * width),
             bytes_accessed=int(share * slots * size * size * 4)
@@ -275,6 +275,7 @@
             pltpu.VMEM((len(flat), rows, LANES), jnp.float32),
             pltpu.SemaphoreType.DMA((len(flat),)),
         ],
+        compiler_params=pltpu.CompilerParams(vmem_limit_bytes=8 * 1024 * 1024),
         name="merge",
     )(*flat)
 
@@ -303,6 +304,7 @@
             pltpu.VMEM((2, *direct.shape), jnp.float32),
             pltpu.SemaphoreType.DMA((2,)),
         ],
+        compiler_params=pltpu.CompilerParams(vmem_limit_bytes=8 * 1024 * 1024),
         name="finish",
     )(direct, mirror)
 

time: 161 us -> 150 us (0.932)
  other arithmetic: 12.1 us -> 0.54 us
  Pallas kernels: 25.4 us -> 16.3 us
  waiting for transfers between devices: 39 us -> 44.9 us
  starting transfers between devices: 49.1 us -> 54.2 us
    pallas_call x2, Pallas kernels: 20.7 us -> 14.7 us  [ladder(): pl.pallas_call(functools.partial(ladder_kernel, pieces_given=len(pieces),...]
    ppermute x16, waiting for transfers between devices: 12.2 us -> 18.1 us  [shift_line(): lax.ppermute(block, 'cd', [(i, (i + step) % size) for i in range(size)])]
    add x4, other arithmetic: 3.97 us -> 0.11 us  [ring_terms(): down = behind + down]
    add x4, other arithmetic: 3.96 us -> 0.11 us  [ring_terms(): up = ahead + up]
    ppermute x16, starting transfers between devices: 19.9 us -> 23.5 us  [shift_line(): lax.ppermute(block, 'cd', [(i, (i + step) % size) for i in range(size)])]
    unnamed x29 -> x13, local copies, waits for them, and re-layouts: 3.86 us -> 6.98 us
    pallas_call x1, Pallas kernels: 2.37 us -> 0.34 us  [merge(): pl.pallas_call(functools.partial(merge_kernel, terms=[len(terms) for term...]
    slice x2, other arithmetic: 1.99 us -> 0.05 us  [ring_terms(): down = jnp.concatenate([behind[:half], behind[half:] + down], axis=0)]
  transfers between devices with their start and end apart: 31 -> 31, of which waited for: 14 -> 14; matrix products, arithmetic and copies ran while one was open for 10% -> 0% of each run, Pallas kernels for 7% -> 6%
where the time goes in v5:
time: 150 us
  starting transfers between devices  54.2 us (36%)
  waiting for transfers between devices  44.9 us (30%)
  blocking collectives  25.3 us (17%)
  Pallas kernels  16.3 us (11%)
  local copies, waits for them, and re-layouts  7.16 us (5%)
    all_to_all x1, blocking collectives, per_device(): lax.all_to_all(outgoing, ('ab', 'cd'), split_axis=0, concat_axis=0, tiled...  25.3 us
    ppermute x16, starting transfers between devices, shift_line(): lax.ppermute(block, 'cd', [(i, (i + step) % size) for i in range(size)])  23.5 us
    ppermute x4, waiting for transfers between devices, both_ways(): lax.ppermute(block, 'ab', plane_route(dx, dy))  20.8 us
    ppermute x16, waiting for transfers between devices, shift_line(): lax.ppermute(block, 'cd', [(i, (i + step) % size) for i in range(size)])  18.1 us
    pallas_call x2, Pallas kernels, ladder(): pl.pallas_call(functools.partial(ladder_kernel, pieces_given=len(pieces),...  14.7 us
    ppermute x1, starting transfers between devices, per_device(): lax.ppermute(arrived, 'ij', [(0, 1), (1, 0)]).reshape(direct.shape)  7.46 us
    unnamed x13, local copies, waits for them, and re-layouts  6.98 us
    ppermute x4, starting transfers between devices, both_ways(): lax.ppermute(block, 'ab', plane_route(-dx, -dy))  6.74 us
  transfers between devices with their start and end apart: 31, of which 14 were waited for; matrix products, arithmetic and copies ran while one was open for 0% of the time, Pallas kernels for 6%

profile of v5, /device:TPU:1, one launch (start us, length us, event | category | flops | bytes accessed | tf_op | source)
XLA Modules:
  0.0 149.6 jit_solution(12210613613744148773)
XLA Ops:
  0.0 1.2 copy.6
  1.3 2.2 %collective-permute-start.7 = (f32[256,256]{1,0:T(8,128)S(1)}, f32[256,256]{1,0:T(8,128)S(1)}, u32[]{:S(2)}, u32[]{:S(2)}) collective-permute-start(f32[256,256]{1,0:T(8,128)S(1)} %get-tuple-element.41), channel_id=1, source_target_pairs={{0,64},{16,80},{32,96},{48,112},{64,128},{80,144},{96,160},{112,17... | collective-permute-start | bytes 786440 | tf_op jit(solution)/shard_map/ppermute | solution.py:27
  3.5 1.5 %collective-permute-start.8 = (f32[256,256]{1,0:T(8,128)S(1)}, f32[256,256]{1,0:T(8,128)S(1)}, u32[]{:S(2)}, u32[]{:S(2)}) collective-permute-start(f32[256,256]{1,0:T(8,128)S(1)} %get-tuple-element.41), channel_id=1, source_target_pairs={{0,192},{16,208},{32,224},{48,240},{64,0},{80,16},{96,32},{112,48}... | collective-permute-start | bytes 786440 | tf_op jit(solution)/shard_map/ppermute | solution.py:28
  5.0 1.6 %collective-permute-start.9 = (f32[256,256]{1,0:T(8,128)S(1)}, f32[256,256]{1,0:T(8,128)S(1)}, u32[]{:S(2)}, u32[]{:S(2)}) collective-permute-start(f32[256,256]{1,0:T(8,128)S(1)} %get-tuple-element.41), channel_id=1, source_target_pairs={{0,128},{16,144},{32,160},{48,176},{64,192},{80,208},{96,224},{112... | collective-permute-start | bytes 786440 | tf_op jit(solution)/shard_map/ppermute | solution.py:42
  6.6 1.2 collective-permute-start
  7.8 1.5 collective-permute-start.1
  9.3 4.2 %collective-permute-start.2 = (f32[256,256]{1,0:T(8,128)S(1)}, f32[256,256]{1,0:T(8,128)S(1)}, u32[]{:S(2)}, u32[]{:S(2)}) collective-permute-start(f32[256,256]{1,0:T(8,128)S(1)} %get-tuple-element.42), channel_id=1, source_target_pairs={{0,32},{16,48},{32,0},{48,16},{64,96},{80,112},{96,64},{112,80},{1... | collective-permute-start | bytes 786440 | tf_op jit(solution)/shard_map/ppermute | solution.py:42
  13.5 4.0 %collective-permute-done.9 = f32[256,256]{1,0:T(8,128)S(1)} collective-permute-done((f32[256,256]{1,0:T(8,128)S(1)}, f32[256,256]{1,0:T(8,128)S(1)}, u32[]{:S(2)}, u32[]{:S(2)}) %collective-permute-start.9) | collective-permute-done | bytes 262176 | tf_op jit(solution)/shard_map/ppermute | solution.py:42
  17.5 1.3 collective-permute-start.10
  18.8 1.5 collective-permute-start.12
  20.3 0.4 collective-permute-done.2
  20.7 0.5 collective-permute-start.3
  21.2 2.3 %collective-permute-start.5 = (f32[1024,256]{1,0:T(8,128)S(1)}, f32[1024,256]{1,0:T(8,128)S(1)}, u32[]{:S(2)}, u32[]{:S(2)}) collective-permute-start(f32[1024,256]{1,0:T(8,128)S(1)} %pad_maximum_fusion.rest_0_), channel_id=1, source_target_pairs={{0,192},{16,208},{32,224},{48,240},{64,0},{80,16},{96,32},{112,48}... | collective-permute-start | bytes 3145736 | tf_op jit(solution)/shard_map/ppermute | solution.py:28
  23.5 20.8 %collective-permute-done.10.rest_4_ = f32[1024,256]{1,0:T(8,128)S(1)} collective-permute-done((f32[1024,256]{1,0:T(8,128)S(1)}, f32[1024,256]{1,0:T(8,128)S(1)}, u32[]{:S(2)}, u32[]{:S(2)}) %collective-permute-start.10) | collective-permute-done | bytes 1048608 | tf_op jit(solution)/shard_map/ppermute | solution.py:27
  44.5 2.7 %collective-permute-start.13 = (f32[512,256]{1,0:T(8,128)S(1)}, f32[512,256]{1,0:T(8,128)S(1)}, u32[]{:S(2)}, u32[]{:S(2)}) collective-permute-start(f32[512,256]{1,0:T(8,128)S(1)} %slice.61), channel_id=1, source_target_pairs={{0,48},{16,0},{32,16},{48,32},{64,112},{80,64},{96,80},{112,96},{1... | collective-permute-start | bytes 1572872 | tf_op jit(solution)/shard_map/ppermute | solution.py:37
  47.4 2.7 %collective-permute-start.6 = (f32[512,256]{1,0:T(8,128)S(1)}, f32[512,256]{1,0:T(8,128)S(1)}, u32[]{:S(2)}, u32[]{:S(2)}) collective-permute-start(f32[512,256]{1,0:T(8,128)S(1)} %slice.58), channel_id=1, source_target_pairs={{0,192},{16,208},{32,224},{48,240},{64,0},{80,16},{96,32},{112,48}... | collective-permute-start | bytes 1572872 | tf_op jit(solution)/shard_map/ppermute | solution.py:37
  50.8 4.4 %copy-done = f32[46,256,256]{2,1,0:T(8,128)S(1)} copy-done((f32[46,256,256]{2,1,0:T(8,128)S(1)}, f32[46,256,256]{2,1,0:T(8,128)}, u32[]{:S(2)}) %copy-start) | copy-done | bytes 12058648
  55.2 0.7 copy-done.1
  55.9 0.7 copy-done.2
  56.5 9.5 %ladder.1.rest_4_ = f32[2,8,512,128]{3,2,1,0:T(8,128)S(1)} custom-call(s32[46]{0:T(128)S(1)} %copy-done.1, s32[46]{0:T(128)S(1)} %copy-done.2, s32[1]{0:T(128)S(6)} %copy.8.count_ref, f32[46,256,256]{2,1,0:T(8,128)S(1)} %copy-done, f32[1024,256]{1,0:T(8,128)S(1)} %pad_maximum_fusion.rest_0_, f32[1024,256]{1,0:T(8,128)S(1)} %collective-permute-done.3.rest_1_, ...), custom_call_target="tpu_custom_call" | custom-call | flops 3472883712 | bytes 19529728 | tf_op jit(solution)/shard_map/ladder/pallas_call | solution.py:190
  66.1 5.2 %ladder_last.1 = (f32[256,128]{1,0:T(8,128)S(1)}, f32[256,128]{1,0:T(8,128)S(1)}, f32[512,128]{1,0:T(8,128)S(1)}, f32[512,128]{1,0:T(8,128)S(1)}, f32[512,128]{1...) custom-call(s32[46]{0:T(128)S(1)} %copy-done.1, ...), custom_call_target="tpu_custom_call" | custom-call | flops 1157627904 | bytes 13500416 | tf_op jit(solution)/shard_map/ladder_last/pallas_call | solution.py:190
  71.4 0.1 collective-permute-start.26
  71.5 1.5 collective-permute-start.22
  72.9 2.1 %collective-permute-start.18 = (f32[256,128]{1,0:T(8,128)S(1)}, f32[256,128]{1,0:T(8,128)S(1)}, u32[]{:S(2)}, u32[]{:S(2)}) collective-permute-start(f32[256,128]{1,0:T(8,128)S(1)} %get-tuple-element.30), channel_id=1, source_target_pairs={{0,14},{2,0},{4,2},{6,4},{8,6},{10,8},{12,10},{14,12},{1,15},{3,1}... | collective-permute-start | bytes 393224 | tf_op jit(solution)/shard_map/ppermute | solution.py:220
  75.0 0.3 collective-permute-done.26
  75.3 2.5 %collective-permute-start.27 = (f32[512,128]{1,0:T(8,128)S(1)}, f32[512,128]{1,0:T(8,128)S(1)}, u32[]{:S(2)}, u32[]{:S(2)}) collective-permute-start(f32[512,128]{1,0:T(8,128)S(1)} %pad_maximum_fusion.5), channel_id=1, source_target_pairs={{0,14},{2,0},{4,2},{6,4},{8,6},{10,8},{12,10},{14,12},{1,15},{3,1}... | collective-permute-start | bytes 786440 | tf_op jit(solution)/shard_map/ppermute | solution.py:220
  77.9 0.1 collective-permute-start.23
  78.0 2.7 %collective-permute-start.19 = (f32[512,128]{1,0:T(8,128)S(1)}, f32[512,128]{1,0:T(8,128)S(1)}, u32[]{:S(2)}, u32[]{:S(2)}) collective-permute-start(f32[512,128]{1,0:T(8,128)S(1)} %pad_maximum_fusion.3), channel_id=1, source_target_pairs={{0,14},{2,0},{4,2},{6,4},{8,6},{10,8},{12,10},{14,12},{1,15},{3,1}... | collective-permute-start | bytes 786440 | tf_op jit(solution)/shard_map/ppermute | solution.py:220
  80.7 0.8 collective-permute-done.14
  81.6 0.1 collective-permute-start.15
  81.7 1.3 collective-permute-done.27
  83.0 3.5 %collective-permute-start.28 = (f32[512,128]{1,0:T(8,128)S(1)}, f32[512,128]{1,0:T(8,128)S(1)}, u32[]{:S(2)}, u32[]{:S(2)}) collective-permute-start(f32[512,128]{1,0:T(8,128)S(1)} %add.46), channel_id=1, source_target_pairs={{0,14},{2,0},{4,2},{6,4},{8,6},{10,8},{12,10},{14,12},{1,15},{3,1}... | collective-permute-start | bytes 786440 | tf_op jit(solution)/shard_map/ppermute | solution.py:220
  86.6 2.0 %collective-permute-done.19 = f32[512,128]{1,0:T(8,128)S(1)} collective-permute-done((f32[512,128]{1,0:T(8,128)S(1)}, f32[512,128]{1,0:T(8,128)S(1)}, u32[]{:S(2)}, u32[]{:S(2)}) %collective-permute-start.19) | collective-permute-done | bytes 262176 | tf_op jit(solution)/shard_map/ppermute | solution.py:220
  88.6 3.5 %collective-permute-start.20 = (f32[512,128]{1,0:T(8,128)S(1)}, f32[512,128]{1,0:T(8,128)S(1)}, u32[]{:S(2)}, u32[]{:S(2)}) collective-permute-start(f32[512,128]{1,0:T(8,128)S(1)} %add.40), channel_id=1, source_target_pairs={{0,14},{2,0},{4,2},{6,4},{8,6},{10,8},{12,10},{14,12},{1,15},{3,1}... | collective-permute-start | bytes 786440 | tf_op jit(solution)/shard_map/ppermute | solution.py:220
  92.2 2.0 %collective-permute-done.28 = f32[512,128]{1,0:T(8,128)S(1)} collective-permute-done((f32[512,128]{1,0:T(8,128)S(1)}, f32[512,128]{1,0:T(8,128)S(1)}, u32[]{:S(2)}, u32[]{:S(2)}) %collective-permute-start.28) | collective-permute-done | bytes 262176 | tf_op jit(solution)/shard_map/ppermute | solution.py:220
  94.2 3.5 %collective-permute-start.29 = (f32[512,128]{1,0:T(8,128)S(1)}, f32[512,128]{1,0:T(8,128)S(1)}, u32[]{:S(2)}, u32[]{:S(2)}) collective-permute-start(f32[512,128]{1,0:T(8,128)S(1)} %add.47), channel_id=1, source_target_pairs={{0,14},{2,0},{4,2},{6,4},{8,6},{10,8},{12,10},{14,12},{1,15},{3,1}... | collective-permute-start | bytes 786440 | tf_op jit(solution)/shard_map/ppermute | solution.py:220
  97.8 0.3 collective-permute-start.25
  98.1 1.7 %collective-permute-done.20 = f32[512,128]{1,0:T(8,128)S(1)} collective-permute-done((f32[512,128]{1,0:T(8,128)S(1)}, f32[512,128]{1,0:T(8,128)S(1)}, u32[]{:S(2)}, u32[]{:S(2)}) %collective-permute-start.20) | collective-permute-done | bytes 262176 | tf_op jit(solution)/shard_map/ppermute | solution.py:220
  99.9 3.5 %collective-permute-start.21 = (f32[512,128]{1,0:T(8,128)S(1)}, f32[512,128]{1,0:T(8,128)S(1)}, u32[]{:S(2)}, u32[]{:S(2)}) collective-permute-start(f32[512,128]{1,0:T(8,128)S(1)} %add.41), channel_id=1, source_target_pairs={{0,14},{2,0},{4,2},{6,4},{8,6},{10,8},{12,10},{14,12},{1,15},{3,1}... | collective-permute-start | bytes 786440 | tf_op jit(solution)/shard_map/ppermute | solution.py:220
  103.5 2.0 %collective-permute-done.29.refs_4_ = f32[512,128]{1,0:T(8,128)S(1)} collective-permute-done((f32[512,128]{1,0:T(8,128)S(1)}, f32[512,128]{1,0:T(8,128)S(1)}, u32[]{:S(2)}, u32[]{:S(2)}) %collective-permute-start.29) | collective-permute-done | bytes 262176 | tf_op jit(solution)/shard_map/ppermute | solution.py:220
  105.5 2.5 %collective-permute-done.25.refs_3_ = f32[512,128]{1,0:T(8,128)S(1)} collective-permute-done((f32[512,128]{1,0:T(8,128)S(1)}, f32[512,128]{1,0:T(8,128)S(1)}, u32[]{:S(2)}, u32[]{:S(2)}) %collective-permute-start.25) | collective-permute-done | bytes 262176 | tf_op jit(solution)/shard_map/ppermute | solution.py:220
  107.9 3.2 %collective-permute-done.21.refs_1_ = f32[512,128]{1,0:T(8,128)S(1)} collective-permute-done((f32[512,128]{1,0:T(8,128)S(1)}, f32[512,128]{1,0:T(8,128)S(1)}, u32[]{:S(2)}, u32[]{:S(2)}) %collective-permute-start.21) | collective-permute-done | bytes 262176 | tf_op jit(solution)/shard_map/ppermute | solution.py:220
  111.1 2.5 %collective-permute-done.17.refs_0_ = f32[512,128]{1,0:T(8,128)S(1)} collective-permute-done((f32[512,128]{1,0:T(8,128)S(1)}, f32[512,128]{1,0:T(8,128)S(1)}, u32[]{:S(2)}, u32[]{:S(2)}) %collective-permute-start.17) | collective-permute-done | bytes 262176 | tf_op jit(solution)/shard_map/ppermute | solution.py:220
  113.5 0.3 merge.1.direct_any
  113.9 25.3 %all_to_all.5 = f32[128,8,128]{2,1,0:T(8,128)S(1)} all-to-all(f32[128,8,128]{2,1,0:T(8,128)S(1)} %bitcast.8), channel_id=1, replica_groups=mesh['ab'=16,'cd'=8,'ij'=2] {'ab','cd'}, dimensions={0} | all-to-all | bytes 1048576 | tf_op jit(solution)/shard_map/all_to_all | solution.py:323
  139.2 7.5 %collective-permute-start.30 = (f32[128,8,128]{2,1,0:T(8,128)S(1)}, f32[128,8,128]{2,1,0:T(8,128)S(1)}, u32[]{:S(2)}, u32[]{:S(2)}) collective-permute-start(f32[128,8,128]{2,1,0:T(8,128)S(1)} %all_to_all.5), channel_id=1, source_target_pairs={{0,1},{1,0},{2,3},{3,2},{4,5},{5,4},{6,7},{7,6},{8,9},{9,8},{10,11... | collective-permute-start | bytes 1572872 | tf_op jit(solution)/shard_map/ppermute | solution.py:324
  146.7 1.5 %collective-permute-done.30 = f32[128,8,128]{2,1,0:T(8,128)S(1)} collective-permute-done((f32[128,8,128]{2,1,0:T(8,128)S(1)}, f32[128,8,128]{2,1,0:T(8,128)S(1)}, u32[]{:S(2)}, u32[]{:S(2)}) %collective-permute-start.30) | collective-permute-done | bytes 524320 | tf_op jit(solution)/shard_map/ppermute | solution.py:324
  148.2 1.2 finish.1
  (56 shorter events, 1.2 us)
Async XLA Ops:
  1.3 8.0 %collective-permute-start.7 = (f32[256,256]{1,0:T(8,128)S(1)}, f32[256,256]{1,0:T(8,128)S(1)}, u32[]{:S(2)}, u32[]{:S(2)}) collective-permute-start(f32[256,256]{1,0:T(8,128)S(1)} %get-tuple-element.41), channel_id=1, source_target_pairs={{0,64},{16,80},{32,96},{48,112},{64,128},{80,144},{96,160},{112,17... | collective-permute-start | bytes 786440 | tf_op jit(solution)/shard_map/ppermute | solution.py:27
  3.5 10.0 %collective-permute-start.8 = (f32[256,256]{1,0:T(8,128)S(1)}, f32[256,256]{1,0:T(8,128)S(1)}, u32[]{:S(2)}, u32[]{:S(2)}) collective-permute-start(f32[256,256]{1,0:T(8,128)S(1)} %get-tuple-element.41), channel_id=1, source_target_pairs={{0,192},{16,208},{32,224},{48,240},{64,0},{80,16},{96,32},{112,48}... | collective-permute-start | bytes 786440 | tf_op jit(solution)/shard_map/ppermute | solution.py:28
  5.0 12.4 %collective-permute-start.9 = (f32[256,256]{1,0:T(8,128)S(1)}, f32[256,256]{1,0:T(8,128)S(1)}, u32[]{:S(2)}, u32[]{:S(2)}) collective-permute-start(f32[256,256]{1,0:T(8,128)S(1)} %get-tuple-element.41), channel_id=1, source_target_pairs={{0,128},{16,144},{32,160},{48,176},{64,192},{80,208},{96,224},{112... | collective-permute-start | bytes 786440 | tf_op jit(solution)/shard_map/ppermute | solution.py:42
  6.6 13.7 %collective-permute-start = (f32[256,256]{1,0:T(8,128)S(1)}, f32[256,256]{1,0:T(8,128)S(1)}, u32[]{:S(2)}, u32[]{:S(2)}) collective-permute-start(f32[256,256]{1,0:T(8,128)S(1)} %get-tuple-element.42), channel_id=1, source_target_pairs={{0,16},{16,32},{32,48},{48,0},{64,80},{80,96},{96,112},{112,64},{1... | collective-permute-start | bytes 786440 | tf_op jit(solution)/shard_map/ppermute | solution.py:27
  7.8 12.5 %collective-permute-start.1 = (f32[256,256]{1,0:T(8,128)S(1)}, f32[256,256]{1,0:T(8,128)S(1)}, u32[]{:S(2)}, u32[]{:S(2)}) collective-permute-start(f32[256,256]{1,0:T(8,128)S(1)} %get-tuple-element.42), channel_id=1, source_target_pairs={{0,48},{16,0},{32,16},{48,32},{64,112},{80,64},{96,80},{112,96},{1... | collective-permute-start | bytes 786440 | tf_op jit(solution)/shard_map/ppermute | solution.py:28
  9.3 11.4 %collective-permute-start.2 = (f32[256,256]{1,0:T(8,128)S(1)}, f32[256,256]{1,0:T(8,128)S(1)}, u32[]{:S(2)}, u32[]{:S(2)}) collective-permute-start(f32[256,256]{1,0:T(8,128)S(1)} %get-tuple-element.42), channel_id=1, source_target_pairs={{0,32},{16,48},{32,0},{48,16},{64,96},{80,112},{96,64},{112,80},{1... | collective-permute-start | bytes 786440 | tf_op jit(solution)/shard_map/ppermute | solution.py:42
  17.4 48.7 %slice-start = ((s8[12058624]{0:T(1024)(128)(4,1)}), s8[4194304]{0:T(1024)(128)(4,1)S(1)}, s32[]{:S(2)}) async-start(s8[12058624]{0:T(1024)(128)(4,1)} %bitcast.6), calls=%async_computation.1 | async-start | bytes 8388608
  17.5 26.8 %collective-permute-start.10 = (f32[1024,256]{1,0:T(8,128)S(1)}, f32[1024,256]{1,0:T(8,128)S(1)}, u32[]{:S(2)}, u32[]{:S(2)}) collective-permute-start(f32[1024,256]{1,0:T(8,128)S(1)} %pad_maximum_fusion.1.rest_3_), channel_id=1, source_target_pairs={{0,16},{16,32},{32,48},{48,0},{64,80},{80,96},{96,112},{112,64},{1... | collective-permute-start | bytes 3145736 | tf_op jit(solution)/shard_map/ppermute | solution.py:27
  18.8 25.7 %collective-permute-start.12 = (f32[1024,256]{1,0:T(8,128)S(1)}, f32[1024,256]{1,0:T(8,128)S(1)}, u32[]{:S(2)}, u32[]{:S(2)}) collective-permute-start(f32[1024,256]{1,0:T(8,128)S(1)} %pad_maximum_fusion.1.rest_3_), channel_id=1, source_target_pairs={{0,48},{16,0},{32,16},{48,32},{64,112},{80,64},{96,80},{112,96},{1... | collective-permute-start | bytes 3145736 | tf_op jit(solution)/shard_map/ppermute | solution.py:28
  20.7 26.5 %collective-permute-start.3 = (f32[1024,256]{1,0:T(8,128)S(1)}, f32[1024,256]{1,0:T(8,128)S(1)}, u32[]{:S(2)}, u32[]{:S(2)}) collective-permute-start(f32[1024,256]{1,0:T(8,128)S(1)} %pad_maximum_fusion.rest_0_), channel_id=1, source_target_pairs={{0,64},{16,80},{32,96},{48,112},{64,128},{80,144},{96,160},{112,17... | collective-permute-start | bytes 3145736 | tf_op jit(solution)/shard_map/ppermute | solution.py:27
  21.2 26.2 %collective-permute-start.5 = (f32[1024,256]{1,0:T(8,128)S(1)}, f32[1024,256]{1,0:T(8,128)S(1)}, u32[]{:S(2)}, u32[]{:S(2)}) collective-permute-start(f32[1024,256]{1,0:T(8,128)S(1)} %pad_maximum_fusion.rest_0_), channel_id=1, source_target_pairs={{0,192},{16,208},{32,224},{48,240},{64,0},{80,16},{96,32},{112,48}... | collective-permute-start | bytes 3145736 | tf_op jit(solution)/shard_map/ppermute | solution.py:28
  44.4 21.7 %collective-permute-start.11 = (f32[512,256]{1,0:T(8,128)S(1)}, f32[512,256]{1,0:T(8,128)S(1)}, u32[]{:S(2)}, u32[]{:S(2)}) collective-permute-start(f32[512,256]{1,0:T(8,128)S(1)} %slice.60), channel_id=1, source_target_pairs={{0,16},{16,32},{32,48},{48,0},{64,80},{80,96},{96,112},{112,64},{1... | collective-permute-start | bytes 1572872 | tf_op jit(solution)/shard_map/ppermute | solution.py:36
  44.5 21.6 %collective-permute-start.13 = (f32[512,256]{1,0:T(8,128)S(1)}, f32[512,256]{1,0:T(8,128)S(1)}, u32[]{:S(2)}, u32[]{:S(2)}) collective-permute-start(f32[512,256]{1,0:T(8,128)S(1)} %slice.61), channel_id=1, source_target_pairs={{0,48},{16,0},{32,16},{48,32},{64,112},{80,64},{96,80},{112,96},{1... | collective-permute-start | bytes 1572872 | tf_op jit(solution)/shard_map/ppermute | solution.py:37
  47.3 18.8 %collective-permute-start.4 = (f32[512,256]{1,0:T(8,128)S(1)}, f32[512,256]{1,0:T(8,128)S(1)}, u32[]{:S(2)}, u32[]{:S(2)}) collective-permute-start(f32[512,256]{1,0:T(8,128)S(1)} %slice.57), channel_id=1, source_target_pairs={{0,64},{16,80},{32,96},{48,112},{64,128},{80,144},{96,160},{112,17... | collective-permute-start | bytes 1572872 | tf_op jit(solution)/shard_map/ppermute | solution.py:36
  47.4 18.7 %collective-permute-start.6 = (f32[512,256]{1,0:T(8,128)S(1)}, f32[512,256]{1,0:T(8,128)S(1)}, u32[]{:S(2)}, u32[]{:S(2)}) collective-permute-start(f32[512,256]{1,0:T(8,128)S(1)} %slice.58), channel_id=1, source_target_pairs={{0,192},{16,208},{32,224},{48,240},{64,0},{80,16},{96,32},{112,48}... | collective-permute-start | bytes 1572872 | tf_op jit(solution)/shard_map/ppermute | solution.py:37
  50.8 4.4 %copy-start = (f32[46,256,256]{2,1,0:T(8,128)S(1)}, f32[46,256,256]{2,1,0:T(8,128)}, u32[]{:S(2)}) copy-start(f32[46,256,256]{2,1,0:T(8,128)} %tiles_ref.3) | copy-start | bytes 36175876
  55.2 0.7 copy-start.1
  55.9 0.7 copy-start.2
  56.5 9.6 %slice-start.1 = ((s8[12058624]{0:T(1024)(128)(4,1)}), s8[4194304]{0:T(1024)(128)(4,1)S(1)}, s32[]{:S(2)}) async-start(s8[12058624]{0:T(1024)(128)(4,1)} %bitcast.6), calls=%async_computation.2 | async-start | bytes 8388608
  56.5 9.6 %slice-start.2 = ((s8[12058624]{0:T(1024)(128)(4,1)}), s8[3670016]{0:T(1024)(128)(4,1)S(1)}, s32[]{:S(2)}) async-start(s8[12058624]{0:T(1024)(128)(4,1)} %bitcast.6), calls=%async_computation.3 | async-start | bytes 7340032
  71.4 3.9 %collective-permute-start.26 = (f32[256,128]{1,0:T(8,128)S(1)}, f32[256,128]{1,0:T(8,128)S(1)}, u32[]{:S(2)}, u32[]{:S(2)}) collective-permute-start(f32[256,128]{1,0:T(8,128)S(1)} %get-tuple-element.39), channel_id=1, source_target_pairs={{0,14},{2,0},{4,2},{6,4},{8,6},{10,8},{12,10},{14,12},{1,15},{3,1}... | collective-permute-start | bytes 393224 | tf_op jit(solution)/shard_map/ppermute | solution.py:220
  71.5 6.3 %collective-permute-start.22 = (f32[256,128]{1,0:T(8,128)S(1)}, f32[256,128]{1,0:T(8,128)S(1)}, u32[]{:S(2)}, u32[]{:S(2)}) collective-permute-start(f32[256,128]{1,0:T(8,128)S(1)} %get-tuple-element.35), channel_id=1, source_target_pairs={{0,2},{2,4},{4,6},{6,8},{8,10},{10,12},{12,14},{14,0},{1,3},{3,5},... | collective-permute-start | bytes 393224 | tf_op jit(solution)/shard_map/ppermute | solution.py:220
  72.9 5.0 %collective-permute-start.18 = (f32[256,128]{1,0:T(8,128)S(1)}, f32[256,128]{1,0:T(8,128)S(1)}, u32[]{:S(2)}, u32[]{:S(2)}) collective-permute-start(f32[256,128]{1,0:T(8,128)S(1)} %get-tuple-element.30), channel_id=1, source_target_pairs={{0,14},{2,0},{4,2},{6,4},{8,6},{10,8},{12,10},{14,12},{1,15},{3,1}... | collective-permute-start | bytes 393224 | tf_op jit(solution)/shard_map/ppermute | solution.py:220
  75.0 6.6 %collective-permute-start.14 = (f32[256,128]{1,0:T(8,128)S(1)}, f32[256,128]{1,0:T(8,128)S(1)}, u32[]{:S(2)}, u32[]{:S(2)}) collective-permute-start(f32[256,128]{1,0:T(8,128)S(1)} %get-tuple-element.26), channel_id=1, source_target_pairs={{0,2},{2,4},{4,6},{6,8},{8,10},{10,12},{12,14},{14,0},{1,3},{3,5},... | collective-permute-start | bytes 393224 | tf_op jit(solution)/shard_map/ppermute | solution.py:220
  75.3 7.6 %collective-permute-start.27 = (f32[512,128]{1,0:T(8,128)S(1)}, f32[512,128]{1,0:T(8,128)S(1)}, u32[]{:S(2)}, u32[]{:S(2)}) collective-permute-start(f32[512,128]{1,0:T(8,128)S(1)} %pad_maximum_fusion.5), channel_id=1, source_target_pairs={{0,14},{2,0},{4,2},{6,4},{8,6},{10,8},{12,10},{14,12},{1,15},{3,1}... | collective-permute-start | bytes 786440 | tf_op jit(solution)/shard_map/ppermute | solution.py:220
  77.9 8.6 %collective-permute-start.23 = (f32[512,128]{1,0:T(8,128)S(1)}, f32[512,128]{1,0:T(8,128)S(1)}, u32[]{:S(2)}, u32[]{:S(2)}) collective-permute-start(f32[512,128]{1,0:T(8,128)S(1)} %pad_maximum_fusion.4), channel_id=1, source_target_pairs={{0,2},{2,4},{4,6},{6,8},{8,10},{10,12},{12,14},{14,0},{1,3},{3,5},... | collective-permute-start | bytes 786440 | tf_op jit(solution)/shard_map/ppermute | solution.py:220
  78.0 10.6 %collective-permute-start.19 = (f32[512,128]{1,0:T(8,128)S(1)}, f32[512,128]{1,0:T(8,128)S(1)}, u32[]{:S(2)}, u32[]{:S(2)}) collective-permute-start(f32[512,128]{1,0:T(8,128)S(1)} %pad_maximum_fusion.3), channel_id=1, source_target_pairs={{0,14},{2,0},{4,2},{6,4},{8,6},{10,8},{12,10},{14,12},{1,15},{3,1}... | collective-permute-start | bytes 786440 | tf_op jit(solution)/shard_map/ppermute | solution.py:220
  81.6 10.5 %collective-permute-start.15 = (f32[512,128]{1,0:T(8,128)S(1)}, f32[512,128]{1,0:T(8,128)S(1)}, u32[]{:S(2)}, u32[]{:S(2)}) collective-permute-start(f32[512,128]{1,0:T(8,128)S(1)} %pad_maximum_fusion.2), channel_id=1, source_target_pairs={{0,2},{2,4},{4,6},{6,8},{8,10},{10,12},{12,14},{14,0},{1,3},{3,5},... | collective-permute-start | bytes 786440 | tf_op jit(solution)/shard_map/ppermute | solution.py:220
  83.0 11.2 %collective-permute-start.28 = (f32[512,128]{1,0:T(8,128)S(1)}, f32[512,128]{1,0:T(8,128)S(1)}, u32[]{:S(2)}, u32[]{:S(2)}) collective-permute-start(f32[512,128]{1,0:T(8,128)S(1)} %add.46), channel_id=1, source_target_pairs={{0,14},{2,0},{4,2},{6,4},{8,6},{10,8},{12,10},{14,12},{1,15},{3,1}... | collective-permute-start | bytes 786440 | tf_op jit(solution)/shard_map/ppermute | solution.py:220
  86.5 11.2 %collective-permute-start.24 = (f32[512,128]{1,0:T(8,128)S(1)}, f32[512,128]{1,0:T(8,128)S(1)}, u32[]{:S(2)}, u32[]{:S(2)}) collective-permute-start(f32[512,128]{1,0:T(8,128)S(1)} %add.43), channel_id=1, source_target_pairs={{0,2},{2,4},{4,6},{6,8},{8,10},{10,12},{12,14},{14,0},{1,3},{3,5},... | collective-permute-start | bytes 786440 | tf_op jit(solution)/shard_map/ppermute | solution.py:220
  88.6 11.2 %collective-permute-start.20 = (f32[512,128]{1,0:T(8,128)S(1)}, f32[512,128]{1,0:T(8,128)S(1)}, u32[]{:S(2)}, u32[]{:S(2)}) collective-permute-start(f32[512,128]{1,0:T(8,128)S(1)} %add.40), channel_id=1, source_target_pairs={{0,14},{2,0},{4,2},{6,4},{8,6},{10,8},{12,10},{14,12},{1,15},{3,1}... | collective-permute-start | bytes 786440 | tf_op jit(solution)/shard_map/ppermute | solution.py:220
  92.2 11.2 %collective-permute-start.16 = (f32[512,128]{1,0:T(8,128)S(1)}, f32[512,128]{1,0:T(8,128)S(1)}, u32[]{:S(2)}, u32[]{:S(2)}) collective-permute-start(f32[512,128]{1,0:T(8,128)S(1)} %add.37), channel_id=1, source_target_pairs={{0,2},{2,4},{4,6},{6,8},{8,10},{10,12},{12,14},{14,0},{1,3},{3,5},... | collective-permute-start | bytes 786440 | tf_op jit(solution)/shard_map/ppermute | solution.py:220
  94.2 11.2 %collective-permute-start.29 = (f32[512,128]{1,0:T(8,128)S(1)}, f32[512,128]{1,0:T(8,128)S(1)}, u32[]{:S(2)}, u32[]{:S(2)}) collective-permute-start(f32[512,128]{1,0:T(8,128)S(1)} %add.47), channel_id=1, source_target_pairs={{0,14},{2,0},{4,2},{6,4},{8,6},{10,8},{12,10},{14,12},{1,15},{3,1}... | collective-permute-start | bytes 786440 | tf_op jit(solution)/shard_map/ppermute | solution.py:220
  97.8 10.1 %collective-permute-start.25 = (f32[512,128]{1,0:T(8,128)S(1)}, f32[512,128]{1,0:T(8,128)S(1)}, u32[]{:S(2)}, u32[]{:S(2)}) collective-permute-start(f32[512,128]{1,0:T(8,128)S(1)} %add.44), channel_id=1, source_target_pairs={{0,2},{2,4},{4,6},{6,8},{8,10},{10,12},{12,14},{14,0},{1,3},{3,5},... | collective-permute-start | bytes 786440 | tf_op jit(solution)/shard_map/ppermute | solution.py:220
  99.9 11.2 %collective-permute-start.21 = (f32[512,128]{1,0:T(8,128)S(1)}, f32[512,128]{1,0:T(8,128)S(1)}, u32[]{:S(2)}, u32[]{:S(2)}) collective-permute-start(f32[512,128]{1,0:T(8,128)S(1)} %add.41), channel_id=1, source_target_pairs={{0,14},{2,0},{4,2},{6,4},{8,6},{10,8},{12,10},{14,12},{1,15},{3,1}... | collective-permute-start | bytes 786440 | tf_op jit(solution)/shard_map/ppermute | solution.py:220
  103.4 10.1 %collective-permute-start.17 = (f32[512,128]{1,0:T(8,128)S(1)}, f32[512,128]{1,0:T(8,128)S(1)}, u32[]{:S(2)}, u32[]{:S(2)}) collective-permute-start(f32[512,128]{1,0:T(8,128)S(1)} %add.38), channel_id=1, source_target_pairs={{0,2},{2,4},{4,6},{6,8},{8,10},{10,12},{12,14},{14,0},{1,3},{3,5},... | collective-permute-start | bytes 786440 | tf_op jit(solution)/shard_map/ppermute | solution.py:220
  139.2 9.0 %collective-permute-start.30 = (f32[128,8,128]{2,1,0:T(8,128)S(1)}, f32[128,8,128]{2,1,0:T(8,128)S(1)}, u32[]{:S(2)}, u32[]{:S(2)}) collective-permute-start(f32[128,8,128]{2,1,0:T(8,128)S(1)} %all_to_all.5), channel_id=1, source_target_pairs={{0,1},{1,0},{2,3},{3,2},{4,5},{5,4},{6,7},{7,6},{8,9},{9,8},{10,11... | collective-permute-start | bytes 1572872 | tf_op jit(solution)/shard_map/ppermute | solution.py:324

commit v6 on v5

--- a/solution.py
+++ b/solution.py
@@ -11,7 +11,7 @@
 SIDE = 4
 CHUNKS = 2
 HELD = 16
-GROUP = 2
+GROUP = 4
 
 
 def plane_route(dx, dy):

time: 150 us -> 147 us (0.980)
  starting transfers between devices: 54.2 us -> 61.6 us
  Pallas kernels: 16.3 us -> 10.3 us
  blocking collectives: 25.3 us -> 22.1 us
    ppermute x16, starting transfers between devices: 23.5 us -> 32.1 us  [shift_line(): lax.ppermute(block, 'cd', [(i, (i + step) % size) for i in range(size)])]
    pallas_call x2, Pallas kernels: 14.7 us -> 8.69 us  [ladder(): pl.pallas_call(functools.partial(ladder_kernel, pieces_given=len(pieces),...]
    all_to_all x1, blocking collectives: 25.3 us -> 22.1 us  [per_device(): lax.all_to_all(outgoing, ('ab', 'cd'), split_axis=0, concat_axis=0, tiled...]
  transfers between devices with their start and end apart: 31 -> 31, of which waited for: 14 -> 13; matrix products, arithmetic and copies ran while one was open for 0% -> 0% of each run, Pallas kernels for 6% -> 4%
where the time goes in v6:
time: 147 us
  starting transfers between devices  61.6 us (42%)
  waiting for transfers between devices  44.5 us (30%)
  blocking collectives  22.1 us (15%)
  Pallas kernels  10.3 us (7%)
  local copies, waits for them, and re-layouts  7.16 us (5%)
    ppermute x16, starting transfers between devices, shift_line(): lax.ppermute(block, 'cd', [(i, (i + step) % size) for i in range(size)])  32.1 us
    all_to_all x1, blocking collectives, per_device(): lax.all_to_all(outgoing, ('ab', 'cd'), split_axis=0, concat_axis=0, tiled...  22.1 us
    ppermute x4, waiting for transfers between devices, both_ways(): lax.ppermute(block, 'ab', plane_route(dx, dy))  20.8 us
    ppermute x16, waiting for transfers between devices, shift_line(): lax.ppermute(block, 'cd', [(i, (i + step) % size) for i in range(size)])  17.8 us
    pallas_call x2, Pallas kernels, ladder(): pl.pallas_call(functools.partial(ladder_kernel, pieces_given=len(pieces),...  8.69 us
    unnamed x13, local copies, waits for them, and re-layouts  6.98 us
    ppermute x4, starting transfers between devices, both_ways(): lax.ppermute(block, 'ab', plane_route(-dx, -dy))  6.74 us
    ppermute x1, starting transfers between devices, per_device(): lax.ppermute(arrived, 'ij', [(0, 1), (1, 0)]).reshape(direct.shape)  6.23 us
  transfers between devices with their start and end apart: 31, of which 13 were waited for; matrix products, arithmetic and copies ran while one was open for 0% of the time, Pallas kernels for 4%

profile of v6, /device:TPU:1, one launch (start us, length us, event | category | flops | bytes accessed | tf_op | source)
XLA Modules:
  0.0 147.3 jit_solution(11394692617025135940)
XLA Ops:
  0.0 1.2 copy.6
  1.3 2.2 %collective-permute-start.7 = (f32[256,256]{1,0:T(8,128)S(1)}, f32[256,256]{1,0:T(8,128)S(1)}, u32[]{:S(2)}, u32[]{:S(2)}) collective-permute-start(f32[256,256]{1,0:T(8,128)S(1)} %get-tuple-element.41), channel_id=1, source_target_pairs={{0,64},{16,80},{32,96},{48,112},{64,128},{80,144},{96,160},{112,17... | collective-permute-start | bytes 786440 | tf_op jit(solution)/shard_map/ppermute | solution.py:27
  3.5 1.5 %collective-permute-start.8 = (f32[256,256]{1,0:T(8,128)S(1)}, f32[256,256]{1,0:T(8,128)S(1)}, u32[]{:S(2)}, u32[]{:S(2)}) collective-permute-start(f32[256,256]{1,0:T(8,128)S(1)} %get-tuple-element.41), channel_id=1, source_target_pairs={{0,192},{16,208},{32,224},{48,240},{64,0},{80,16},{96,32},{112,48}... | collective-permute-start | bytes 786440 | tf_op jit(solution)/shard_map/ppermute | solution.py:28
  5.0 1.6 %collective-permute-start.9 = (f32[256,256]{1,0:T(8,128)S(1)}, f32[256,256]{1,0:T(8,128)S(1)}, u32[]{:S(2)}, u32[]{:S(2)}) collective-permute-start(f32[256,256]{1,0:T(8,128)S(1)} %get-tuple-element.41), channel_id=1, source_target_pairs={{0,128},{16,144},{32,160},{48,176},{64,192},{80,208},{96,224},{112... | collective-permute-start | bytes 786440 | tf_op jit(solution)/shard_map/ppermute | solution.py:42
  6.6 1.2 collective-permute-start
  7.8 1.5 collective-permute-start.1
  9.3 4.2 %collective-permute-start.2 = (f32[256,256]{1,0:T(8,128)S(1)}, f32[256,256]{1,0:T(8,128)S(1)}, u32[]{:S(2)}, u32[]{:S(2)}) collective-permute-start(f32[256,256]{1,0:T(8,128)S(1)} %get-tuple-element.42), channel_id=1, source_target_pairs={{0,32},{16,48},{32,0},{48,16},{64,96},{80,112},{96,64},{112,80},{1... | collective-permute-start | bytes 786440 | tf_op jit(solution)/shard_map/ppermute | solution.py:42
  13.5 4.0 %collective-permute-done.9 = f32[256,256]{1,0:T(8,128)S(1)} collective-permute-done((f32[256,256]{1,0:T(8,128)S(1)}, f32[256,256]{1,0:T(8,128)S(1)}, u32[]{:S(2)}, u32[]{:S(2)}) %collective-permute-start.9) | collective-permute-done | bytes 262176 | tf_op jit(solution)/shard_map/ppermute | solution.py:42
  17.5 1.3 collective-permute-start.10
  18.8 1.5 collective-permute-start.12
  20.3 0.4 collective-permute-done.2
  20.7 0.5 collective-permute-start.3
  21.2 2.3 %collective-permute-start.5 = (f32[1024,256]{1,0:T(8,128)S(1)}, f32[1024,256]{1,0:T(8,128)S(1)}, u32[]{:S(2)}, u32[]{:S(2)}) collective-permute-start(f32[1024,256]{1,0:T(8,128)S(1)} %pad_maximum_fusion.rest_0_), channel_id=1, source_target_pairs={{0,192},{16,208},{32,224},{48,240},{64,0},{80,16},{96,32},{112,48}... | collective-permute-start | bytes 3145736 | tf_op jit(solution)/shard_map/ppermute | solution.py:28
  23.5 20.8 %collective-permute-done.10.rest_4_ = f32[1024,256]{1,0:T(8,128)S(1)} collective-permute-done((f32[1024,256]{1,0:T(8,128)S(1)}, f32[1024,256]{1,0:T(8,128)S(1)}, u32[]{:S(2)}, u32[]{:S(2)}) %collective-permute-start.10) | collective-permute-done | bytes 1048608 | tf_op jit(solution)/shard_map/ppermute | solution.py:27
  44.5 2.7 %collective-permute-start.13 = (f32[512,256]{1,0:T(8,128)S(1)}, f32[512,256]{1,0:T(8,128)S(1)}, u32[]{:S(2)}, u32[]{:S(2)}) collective-permute-start(f32[512,256]{1,0:T(8,128)S(1)} %slice.61), channel_id=1, source_target_pairs={{0,48},{16,0},{32,16},{48,32},{64,112},{80,64},{96,80},{112,96},{1... | collective-permute-start | bytes 1572872 | tf_op jit(solution)/shard_map/ppermute | solution.py:37
  47.4 2.7 %collective-permute-start.6 = (f32[512,256]{1,0:T(8,128)S(1)}, f32[512,256]{1,0:T(8,128)S(1)}, u32[]{:S(2)}, u32[]{:S(2)}) collective-permute-start(f32[512,256]{1,0:T(8,128)S(1)} %slice.58), channel_id=1, source_target_pairs={{0,192},{16,208},{32,224},{48,240},{64,0},{80,16},{96,32},{112,48}... | collective-permute-start | bytes 1572872 | tf_op jit(solution)/shard_map/ppermute | solution.py:37
  50.8 4.4 %copy-done = f32[46,256,256]{2,1,0:T(8,128)S(1)} copy-done((f32[46,256,256]{2,1,0:T(8,128)S(1)}, f32[46,256,256]{2,1,0:T(8,128)}, u32[]{:S(2)}) %copy-start) | copy-done | bytes 12058648
  55.2 0.7 copy-done.1
  55.9 0.7 copy-done.2
  56.5 5.2 %ladder.1.rest_4_ = f32[2,8,512,128]{3,2,1,0:T(8,128)S(1)} custom-call(s32[46]{0:T(128)S(1)} %copy-done.1, s32[46]{0:T(128)S(1)} %copy-done.2, s32[1]{0:T(128)S(6)} %copy.8.count_ref, f32[46,256,256]{2,1,0:T(8,128)S(1)} %copy-done, f32[1024,256]{1,0:T(8,128)S(1)} %pad_maximum_fusion.rest_0_, f32[1024,256]{1,0:T(8,128)S(1)} %collective-permute-done.3.rest_1_, ...), custom_call_target="tpu_custom_call" | custom-call | flops 3472883712 | bytes 19529728 | tf_op jit(solution)/shard_map/ladder/pallas_call | solution.py:190
  61.8 3.5 %ladder_last.1 = (f32[256,128]{1,0:T(8,128)S(1)}, f32[256,128]{1,0:T(8,128)S(1)}, f32[512,128]{1,0:T(8,128)S(1)}, f32[512,128]{1,0:T(8,128)S(1)}, f32[512,128]{1...) custom-call(s32[46]{0:T(128)S(1)} %copy-done.1, ...), custom_call_target="tpu_custom_call" | custom-call | flops 1157627904 | bytes 13500416 | tf_op jit(solution)/shard_map/ladder_last/pallas_call | solution.py:190
  65.3 9.6 %collective-permute-start.26 = (f32[256,128]{1,0:T(8,128)S(1)}, f32[256,128]{1,0:T(8,128)S(1)}, u32[]{:S(2)}, u32[]{:S(2)}) collective-permute-start(f32[256,128]{1,0:T(8,128)S(1)} %get-tuple-element.39), channel_id=1, source_target_pairs={{0,14},{2,0},{4,2},{6,4},{8,6},{10,8},{12,10},{14,12},{1,15},{3,1}... | collective-permute-start | bytes 393224 | tf_op jit(solution)/shard_map/ppermute | solution.py:220
  74.9 2.7 %collective-permute-start.18 = (f32[256,128]{1,0:T(8,128)S(1)}, f32[256,128]{1,0:T(8,128)S(1)}, u32[]{:S(2)}, u32[]{:S(2)}) collective-permute-start(f32[256,128]{1,0:T(8,128)S(1)} %get-tuple-element.30), channel_id=1, source_target_pairs={{0,14},{2,0},{4,2},{6,4},{8,6},{10,8},{12,10},{14,12},{1,15},{3,1}... | collective-permute-start | bytes 393224 | tf_op jit(solution)/shard_map/ppermute | solution.py:220
  77.7 2.7 %collective-permute-start.27 = (f32[512,128]{1,0:T(8,128)S(1)}, f32[512,128]{1,0:T(8,128)S(1)}, u32[]{:S(2)}, u32[]{:S(2)}) collective-permute-start(f32[512,128]{1,0:T(8,128)S(1)} %pad_maximum_fusion.5), channel_id=1, source_target_pairs={{0,14},{2,0},{4,2},{6,4},{8,6},{10,8},{12,10},{14,12},{1,15},{3,1}... | collective-permute-start | bytes 786440 | tf_op jit(solution)/shard_map/ppermute | solution.py:220
  80.5 0.1 collective-permute-start.23
  80.6 0.2 collective-permute-done.18
  80.8 3.5 %collective-permute-start.19 = (f32[512,128]{1,0:T(8,128)S(1)}, f32[512,128]{1,0:T(8,128)S(1)}, u32[]{:S(2)}, u32[]{:S(2)}) collective-permute-start(f32[512,128]{1,0:T(8,128)S(1)} %pad_maximum_fusion.3), channel_id=1, source_target_pairs={{0,14},{2,0},{4,2},{6,4},{8,6},{10,8},{12,10},{14,12},{1,15},{3,1}... | collective-permute-start | bytes 786440 | tf_op jit(solution)/shard_map/ppermute | solution.py:220
  84.4 0.1 collective-permute-start.15
  84.5 0.7 collective-permute-done.27
  85.2 3.2 %collective-permute-start.28 = (f32[512,128]{1,0:T(8,128)S(1)}, f32[512,128]{1,0:T(8,128)S(1)}, u32[]{:S(2)}, u32[]{:S(2)}) collective-permute-start(f32[512,128]{1,0:T(8,128)S(1)} %add.46), channel_id=1, source_target_pairs={{0,14},{2,0},{4,2},{6,4},{8,6},{10,8},{12,10},{14,12},{1,15},{3,1}... | collective-permute-start | bytes 786440 | tf_op jit(solution)/shard_map/ppermute | solution.py:220
  88.4 0.1 collective-permute-start.24
  88.5 1.8 %collective-permute-done.19 = f32[512,128]{1,0:T(8,128)S(1)} collective-permute-done((f32[512,128]{1,0:T(8,128)S(1)}, f32[512,128]{1,0:T(8,128)S(1)}, u32[]{:S(2)}, u32[]{:S(2)}) %collective-permute-start.19) | collective-permute-done | bytes 262176 | tf_op jit(solution)/shard_map/ppermute | solution.py:220
  90.3 3.2 %collective-permute-start.20 = (f32[512,128]{1,0:T(8,128)S(1)}, f32[512,128]{1,0:T(8,128)S(1)}, u32[]{:S(2)}, u32[]{:S(2)}) collective-permute-start(f32[512,128]{1,0:T(8,128)S(1)} %add.40), channel_id=1, source_target_pairs={{0,14},{2,0},{4,2},{6,4},{8,6},{10,8},{12,10},{14,12},{1,15},{3,1}... | collective-permute-start | bytes 786440 | tf_op jit(solution)/shard_map/ppermute | solution.py:220
  93.6 0.3 collective-permute-start.16
  93.9 2.0 %collective-permute-done.28 = f32[512,128]{1,0:T(8,128)S(1)} collective-permute-done((f32[512,128]{1,0:T(8,128)S(1)}, f32[512,128]{1,0:T(8,128)S(1)}, u32[]{:S(2)}, u32[]{:S(2)}) %collective-permute-start.28) | collective-permute-done | bytes 262176 | tf_op jit(solution)/shard_map/ppermute | solution.py:220
  95.9 3.2 %collective-permute-start.29 = (f32[512,128]{1,0:T(8,128)S(1)}, f32[512,128]{1,0:T(8,128)S(1)}, u32[]{:S(2)}, u32[]{:S(2)}) collective-permute-start(f32[512,128]{1,0:T(8,128)S(1)} %add.47), channel_id=1, source_target_pairs={{0,14},{2,0},{4,2},{6,4},{8,6},{10,8},{12,10},{14,12},{1,15},{3,1}... | collective-permute-start | bytes 786440 | tf_op jit(solution)/shard_map/ppermute | solution.py:220
  99.2 0.1 collective-permute-start.25
  99.3 2.2 %collective-permute-done.20 = f32[512,128]{1,0:T(8,128)S(1)} collective-permute-done((f32[512,128]{1,0:T(8,128)S(1)}, f32[512,128]{1,0:T(8,128)S(1)}, u32[]{:S(2)}, u32[]{:S(2)}) %collective-permute-start.20) | collective-permute-done | bytes 262176 | tf_op jit(solution)/shard_map/ppermute | solution.py:220
  101.5 3.2 %collective-permute-start.21 = (f32[512,128]{1,0:T(8,128)S(1)}, f32[512,128]{1,0:T(8,128)S(1)}, u32[]{:S(2)}, u32[]{:S(2)}) collective-permute-start(f32[512,128]{1,0:T(8,128)S(1)} %add.41), channel_id=1, source_target_pairs={{0,14},{2,0},{4,2},{6,4},{8,6},{10,8},{12,10},{14,12},{1,15},{3,1}... | collective-permute-start | bytes 786440 | tf_op jit(solution)/shard_map/ppermute | solution.py:220
  104.9 2.2 %collective-permute-done.29.refs_4_ = f32[512,128]{1,0:T(8,128)S(1)} collective-permute-done((f32[512,128]{1,0:T(8,128)S(1)}, f32[512,128]{1,0:T(8,128)S(1)}, u32[]{:S(2)}, u32[]{:S(2)}) %collective-permute-start.29) | collective-permute-done | bytes 262176 | tf_op jit(solution)/shard_map/ppermute | solution.py:220
  107.1 3.0 %collective-permute-done.25.refs_3_ = f32[512,128]{1,0:T(8,128)S(1)} collective-permute-done((f32[512,128]{1,0:T(8,128)S(1)}, f32[512,128]{1,0:T(8,128)S(1)}, u32[]{:S(2)}, u32[]{:S(2)}) %collective-permute-start.25) | collective-permute-done | bytes 262176 | tf_op jit(solution)/shard_map/ppermute | solution.py:220
  110.1 2.6 %collective-permute-done.21.refs_1_ = f32[512,128]{1,0:T(8,128)S(1)} collective-permute-done((f32[512,128]{1,0:T(8,128)S(1)}, f32[512,128]{1,0:T(8,128)S(1)}, u32[]{:S(2)}, u32[]{:S(2)}) %collective-permute-start.21) | collective-permute-done | bytes 262176 | tf_op jit(solution)/shard_map/ppermute | solution.py:220
  112.8 3.0 %collective-permute-done.17.refs_0_ = f32[512,128]{1,0:T(8,128)S(1)} collective-permute-done((f32[512,128]{1,0:T(8,128)S(1)}, f32[512,128]{1,0:T(8,128)S(1)}, u32[]{:S(2)}, u32[]{:S(2)}) %collective-permute-start.17) | collective-permute-done | bytes 262176 | tf_op jit(solution)/shard_map/ppermute | solution.py:220
  115.7 0.3 merge.1.direct_any
  116.1 22.1 %all_to_all.5 = f32[128,8,128]{2,1,0:T(8,128)S(1)} all-to-all(f32[128,8,128]{2,1,0:T(8,128)S(1)} %bitcast.8), channel_id=1, replica_groups=mesh['ab'=16,'cd'=8,'ij'=2] {'ab','cd'}, dimensions={0} | all-to-all | bytes 1048576 | tf_op jit(solution)/shard_map/all_to_all | solution.py:323
  138.2 6.2 %collective-permute-start.30 = (f32[128,8,128]{2,1,0:T(8,128)S(1)}, f32[128,8,128]{2,1,0:T(8,128)S(1)}, u32[]{:S(2)}, u32[]{:S(2)}) collective-permute-start(f32[128,8,128]{2,1,0:T(8,128)S(1)} %all_to_all.5), channel_id=1, source_target_pairs={{0,1},{1,0},{2,3},{3,2},{4,5},{5,4},{6,7},{7,6},{8,9},{9,8},{10,11... | collective-permute-start | bytes 1572872 | tf_op jit(solution)/shard_map/ppermute | solution.py:324
  144.4 1.5 %collective-permute-done.30 = f32[128,8,128]{2,1,0:T(8,128)S(1)} collective-permute-done((f32[128,8,128]{2,1,0:T(8,128)S(1)}, f32[128,8,128]{2,1,0:T(8,128)S(1)}, u32[]{:S(2)}, u32[]{:S(2)}) %collective-permute-start.30) | collective-permute-done | bytes 524320 | tf_op jit(solution)/shard_map/ppermute | solution.py:324
  145.9 1.2 finish.1
  (56 shorter events, 1.1 us)
Async XLA Ops:
  1.3 8.0 %collective-permute-start.7 = (f32[256,256]{1,0:T(8,128)S(1)}, f32[256,256]{1,0:T(8,128)S(1)}, u32[]{:S(2)}, u32[]{:S(2)}) collective-permute-start(f32[256,256]{1,0:T(8,128)S(1)} %get-tuple-element.41), channel_id=1, source_target_pairs={{0,64},{16,80},{32,96},{48,112},{64,128},{80,144},{96,160},{112,17... | collective-permute-start | bytes 786440 | tf_op jit(solution)/shard_map/ppermute | solution.py:27
  3.5 10.0 %collective-permute-start.8 = (f32[256,256]{1,0:T(8,128)S(1)}, f32[256,256]{1,0:T(8,128)S(1)}, u32[]{:S(2)}, u32[]{:S(2)}) collective-permute-start(f32[256,256]{1,0:T(8,128)S(1)} %get-tuple-element.41), channel_id=1, source_target_pairs={{0,192},{16,208},{32,224},{48,240},{64,0},{80,16},{96,32},{112,48}... | collective-permute-start | bytes 786440 | tf_op jit(solution)/shard_map/ppermute | solution.py:28
  5.0 12.4 %collective-permute-start.9 = (f32[256,256]{1,0:T(8,128)S(1)}, f32[256,256]{1,0:T(8,128)S(1)}, u32[]{:S(2)}, u32[]{:S(2)}) collective-permute-start(f32[256,256]{1,0:T(8,128)S(1)} %get-tuple-element.41), channel_id=1, source_target_pairs={{0,128},{16,144},{32,160},{48,176},{64,192},{80,208},{96,224},{112... | collective-permute-start | bytes 786440 | tf_op jit(solution)/shard_map/ppermute | solution.py:42
  6.6 13.7 %collective-permute-start = (f32[256,256]{1,0:T(8,128)S(1)}, f32[256,256]{1,0:T(8,128)S(1)}, u32[]{:S(2)}, u32[]{:S(2)}) collective-permute-start(f32[256,256]{1,0:T(8,128)S(1)} %get-tuple-element.42), channel_id=1, source_target_pairs={{0,16},{16,32},{32,48},{48,0},{64,80},{80,96},{96,112},{112,64},{1... | collective-permute-start | bytes 786440 | tf_op jit(solution)/shard_map/ppermute | solution.py:27
  7.8 12.5 %collective-permute-start.1 = (f32[256,256]{1,0:T(8,128)S(1)}, f32[256,256]{1,0:T(8,128)S(1)}, u32[]{:S(2)}, u32[]{:S(2)}) collective-permute-start(f32[256,256]{1,0:T(8,128)S(1)} %get-tuple-element.42), channel_id=1, source_target_pairs={{0,48},{16,0},{32,16},{48,32},{64,112},{80,64},{96,80},{112,96},{1... | collective-permute-start | bytes 786440 | tf_op jit(solution)/shard_map/ppermute | solution.py:28
  9.3 11.4 %collective-permute-start.2 = (f32[256,256]{1,0:T(8,128)S(1)}, f32[256,256]{1,0:T(8,128)S(1)}, u32[]{:S(2)}, u32[]{:S(2)}) collective-permute-start(f32[256,256]{1,0:T(8,128)S(1)} %get-tuple-element.42), channel_id=1, source_target_pairs={{0,32},{16,48},{32,0},{48,16},{64,96},{80,112},{96,64},{112,80},{1... | collective-permute-start | bytes 786440 | tf_op jit(solution)/shard_map/ppermute | solution.py:42
  17.4 44.3 %slice-start = ((s8[12058624]{0:T(1024)(128)(4,1)}), s8[4194304]{0:T(1024)(128)(4,1)S(1)}, s32[]{:S(2)}) async-start(s8[12058624]{0:T(1024)(128)(4,1)} %bitcast.6), calls=%async_computation.1 | async-start | bytes 8388608
  17.5 26.8 %collective-permute-start.10 = (f32[1024,256]{1,0:T(8,128)S(1)}, f32[1024,256]{1,0:T(8,128)S(1)}, u32[]{:S(2)}, u32[]{:S(2)}) collective-permute-start(f32[1024,256]{1,0:T(8,128)S(1)} %pad_maximum_fusion.1.rest_3_), channel_id=1, source_target_pairs={{0,16},{16,32},{32,48},{48,0},{64,80},{80,96},{96,112},{112,64},{1... | collective-permute-start | bytes 3145736 | tf_op jit(solution)/shard_map/ppermute | solution.py:27
  18.8 25.7 %collective-permute-start.12 = (f32[1024,256]{1,0:T(8,128)S(1)}, f32[1024,256]{1,0:T(8,128)S(1)}, u32[]{:S(2)}, u32[]{:S(2)}) collective-permute-start(f32[1024,256]{1,0:T(8,128)S(1)} %pad_maximum_fusion.1.rest_3_), channel_id=1, source_target_pairs={{0,48},{16,0},{32,16},{48,32},{64,112},{80,64},{96,80},{112,96},{1... | collective-permute-start | bytes 3145736 | tf_op jit(solution)/shard_map/ppermute | solution.py:28
  20.7 26.5 %collective-permute-start.3 = (f32[1024,256]{1,0:T(8,128)S(1)}, f32[1024,256]{1,0:T(8,128)S(1)}, u32[]{:S(2)}, u32[]{:S(2)}) collective-permute-start(f32[1024,256]{1,0:T(8,128)S(1)} %pad_maximum_fusion.rest_0_), channel_id=1, source_target_pairs={{0,64},{16,80},{32,96},{48,112},{64,128},{80,144},{96,160},{112,17... | collective-permute-start | bytes 3145736 | tf_op jit(solution)/shard_map/ppermute | solution.py:27
  21.2 26.2 %collective-permute-start.5 = (f32[1024,256]{1,0:T(8,128)S(1)}, f32[1024,256]{1,0:T(8,128)S(1)}, u32[]{:S(2)}, u32[]{:S(2)}) collective-permute-start(f32[1024,256]{1,0:T(8,128)S(1)} %pad_maximum_fusion.rest_0_), channel_id=1, source_target_pairs={{0,192},{16,208},{32,224},{48,240},{64,0},{80,16},{96,32},{112,48}... | collective-permute-start | bytes 3145736 | tf_op jit(solution)/shard_map/ppermute | solution.py:28
  44.4 17.4 %collective-permute-start.11 = (f32[512,256]{1,0:T(8,128)S(1)}, f32[512,256]{1,0:T(8,128)S(1)}, u32[]{:S(2)}, u32[]{:S(2)}) collective-permute-start(f32[512,256]{1,0:T(8,128)S(1)} %slice.60), channel_id=1, source_target_pairs={{0,16},{16,32},{32,48},{48,0},{64,80},{80,96},{96,112},{112,64},{1... | collective-permute-start | bytes 1572872 | tf_op jit(solution)/shard_map/ppermute | solution.py:36
  44.5 17.2 %collective-permute-start.13 = (f32[512,256]{1,0:T(8,128)S(1)}, f32[512,256]{1,0:T(8,128)S(1)}, u32[]{:S(2)}, u32[]{:S(2)}) collective-permute-start(f32[512,256]{1,0:T(8,128)S(1)} %slice.61), channel_id=1, source_target_pairs={{0,48},{16,0},{32,16},{48,32},{64,112},{80,64},{96,80},{112,96},{1... | collective-permute-start | bytes 1572872 | tf_op jit(solution)/shard_map/ppermute | solution.py:37
  47.3 14.5 %collective-permute-start.4 = (f32[512,256]{1,0:T(8,128)S(1)}, f32[512,256]{1,0:T(8,128)S(1)}, u32[]{:S(2)}, u32[]{:S(2)}) collective-permute-start(f32[512,256]{1,0:T(8,128)S(1)} %slice.57), channel_id=1, source_target_pairs={{0,64},{16,80},{32,96},{48,112},{64,128},{80,144},{96,160},{112,17... | collective-permute-start | bytes 1572872 | tf_op jit(solution)/shard_map/ppermute | solution.py:36
  47.4 14.3 %collective-permute-start.6 = (f32[512,256]{1,0:T(8,128)S(1)}, f32[512,256]{1,0:T(8,128)S(1)}, u32[]{:S(2)}, u32[]{:S(2)}) collective-permute-start(f32[512,256]{1,0:T(8,128)S(1)} %slice.58), channel_id=1, source_target_pairs={{0,192},{16,208},{32,224},{48,240},{64,0},{80,16},{96,32},{112,48}... | collective-permute-start | bytes 1572872 | tf_op jit(solution)/shard_map/ppermute | solution.py:37
  50.8 4.4 %copy-start = (f32[46,256,256]{2,1,0:T(8,128)S(1)}, f32[46,256,256]{2,1,0:T(8,128)}, u32[]{:S(2)}) copy-start(f32[46,256,256]{2,1,0:T(8,128)} %tiles_ref.3) | copy-start | bytes 36175876
  55.2 0.7 copy-start.1
  55.9 0.7 copy-start.2
  56.5 5.2 %slice-start.1 = ((s8[12058624]{0:T(1024)(128)(4,1)}), s8[4194304]{0:T(1024)(128)(4,1)S(1)}, s32[]{:S(2)}) async-start(s8[12058624]{0:T(1024)(128)(4,1)} %bitcast.6), calls=%async_computation.2 | async-start | bytes 8388608
  56.5 5.3 %slice-start.2 = ((s8[12058624]{0:T(1024)(128)(4,1)}), s8[3670016]{0:T(1024)(128)(4,1)S(1)}, s32[]{:S(2)}) async-start(s8[12058624]{0:T(1024)(128)(4,1)} %bitcast.6), calls=%async_computation.3 | async-start | bytes 7340032
  65.3 12.3 %collective-permute-start.26 = (f32[256,128]{1,0:T(8,128)S(1)}, f32[256,128]{1,0:T(8,128)S(1)}, u32[]{:S(2)}, u32[]{:S(2)}) collective-permute-start(f32[256,128]{1,0:T(8,128)S(1)} %get-tuple-element.39), channel_id=1, source_target_pairs={{0,14},{2,0},{4,2},{6,4},{8,6},{10,8},{12,10},{14,12},{1,15},{3,1}... | collective-permute-start | bytes 393224 | tf_op jit(solution)/shard_map/ppermute | solution.py:220
  74.9 5.5 %collective-permute-start.22 = (f32[256,128]{1,0:T(8,128)S(1)}, f32[256,128]{1,0:T(8,128)S(1)}, u32[]{:S(2)}, u32[]{:S(2)}) collective-permute-start(f32[256,128]{1,0:T(8,128)S(1)} %get-tuple-element.35), channel_id=1, source_target_pairs={{0,2},{2,4},{4,6},{6,8},{8,10},{10,12},{12,14},{14,0},{1,3},{3,5},... | collective-permute-start | bytes 393224 | tf_op jit(solution)/shard_map/ppermute | solution.py:220
  74.9 5.8 %collective-permute-start.18 = (f32[256,128]{1,0:T(8,128)S(1)}, f32[256,128]{1,0:T(8,128)S(1)}, u32[]{:S(2)}, u32[]{:S(2)}) collective-permute-start(f32[256,128]{1,0:T(8,128)S(1)} %get-tuple-element.30), channel_id=1, source_target_pairs={{0,14},{2,0},{4,2},{6,4},{8,6},{10,8},{12,10},{14,12},{1,15},{3,1}... | collective-permute-start | bytes 393224 | tf_op jit(solution)/shard_map/ppermute | solution.py:220
  77.6 6.7 %collective-permute-start.14 = (f32[256,128]{1,0:T(8,128)S(1)}, f32[256,128]{1,0:T(8,128)S(1)}, u32[]{:S(2)}, u32[]{:S(2)}) collective-permute-start(f32[256,128]{1,0:T(8,128)S(1)} %get-tuple-element.26), channel_id=1, source_target_pairs={{0,2},{2,4},{4,6},{6,8},{8,10},{10,12},{12,14},{14,0},{1,3},{3,5},... | collective-permute-start | bytes 393224 | tf_op jit(solution)/shard_map/ppermute | solution.py:220
  77.7 7.5 %collective-permute-start.27 = (f32[512,128]{1,0:T(8,128)S(1)}, f32[512,128]{1,0:T(8,128)S(1)}, u32[]{:S(2)}, u32[]{:S(2)}) collective-permute-start(f32[512,128]{1,0:T(8,128)S(1)} %pad_maximum_fusion.5), channel_id=1, source_target_pairs={{0,14},{2,0},{4,2},{6,4},{8,6},{10,8},{12,10},{14,12},{1,15},{3,1}... | collective-permute-start | bytes 786440 | tf_op jit(solution)/shard_map/ppermute | solution.py:220
  80.5 7.9 %collective-permute-start.23 = (f32[512,128]{1,0:T(8,128)S(1)}, f32[512,128]{1,0:T(8,128)S(1)}, u32[]{:S(2)}, u32[]{:S(2)}) collective-permute-start(f32[512,128]{1,0:T(8,128)S(1)} %pad_maximum_fusion.4), channel_id=1, source_target_pairs={{0,2},{2,4},{4,6},{6,8},{8,10},{10,12},{12,14},{14,0},{1,3},{3,5},... | collective-permute-start | bytes 786440 | tf_op jit(solution)/shard_map/ppermute | solution.py:220
  80.8 9.5 %collective-permute-start.19 = (f32[512,128]{1,0:T(8,128)S(1)}, f32[512,128]{1,0:T(8,128)S(1)}, u32[]{:S(2)}, u32[]{:S(2)}) collective-permute-start(f32[512,128]{1,0:T(8,128)S(1)} %pad_maximum_fusion.3), channel_id=1, source_target_pairs={{0,14},{2,0},{4,2},{6,4},{8,6},{10,8},{12,10},{14,12},{1,15},{3,1}... | collective-permute-start | bytes 786440 | tf_op jit(solution)/shard_map/ppermute | solution.py:220
  84.4 9.2 %collective-permute-start.15 = (f32[512,128]{1,0:T(8,128)S(1)}, f32[512,128]{1,0:T(8,128)S(1)}, u32[]{:S(2)}, u32[]{:S(2)}) collective-permute-start(f32[512,128]{1,0:T(8,128)S(1)} %pad_maximum_fusion.2), channel_id=1, source_target_pairs={{0,2},{2,4},{4,6},{6,8},{8,10},{10,12},{12,14},{14,0},{1,3},{3,5},... | collective-permute-start | bytes 786440 | tf_op jit(solution)/shard_map/ppermute | solution.py:220
  85.2 10.7 %collective-permute-start.28 = (f32[512,128]{1,0:T(8,128)S(1)}, f32[512,128]{1,0:T(8,128)S(1)}, u32[]{:S(2)}, u32[]{:S(2)}) collective-permute-start(f32[512,128]{1,0:T(8,128)S(1)} %add.46), channel_id=1, source_target_pairs={{0,14},{2,0},{4,2},{6,4},{8,6},{10,8},{12,10},{14,12},{1,15},{3,1}... | collective-permute-start | bytes 786440 | tf_op jit(solution)/shard_map/ppermute | solution.py:220
  88.4 10.7 %collective-permute-start.24 = (f32[512,128]{1,0:T(8,128)S(1)}, f32[512,128]{1,0:T(8,128)S(1)}, u32[]{:S(2)}, u32[]{:S(2)}) collective-permute-start(f32[512,128]{1,0:T(8,128)S(1)} %add.43), channel_id=1, source_target_pairs={{0,2},{2,4},{4,6},{6,8},{8,10},{10,12},{12,14},{14,0},{1,3},{3,5},... | collective-permute-start | bytes 786440 | tf_op jit(solution)/shard_map/ppermute | solution.py:220
  90.3 11.2 %collective-permute-start.20 = (f32[512,128]{1,0:T(8,128)S(1)}, f32[512,128]{1,0:T(8,128)S(1)}, u32[]{:S(2)}, u32[]{:S(2)}) collective-permute-start(f32[512,128]{1,0:T(8,128)S(1)} %add.40), channel_id=1, source_target_pairs={{0,14},{2,0},{4,2},{6,4},{8,6},{10,8},{12,10},{14,12},{1,15},{3,1}... | collective-permute-start | bytes 786440 | tf_op jit(solution)/shard_map/ppermute | solution.py:220
  93.6 11.2 %collective-permute-start.16 = (f32[512,128]{1,0:T(8,128)S(1)}, f32[512,128]{1,0:T(8,128)S(1)}, u32[]{:S(2)}, u32[]{:S(2)}) collective-permute-start(f32[512,128]{1,0:T(8,128)S(1)} %add.37), channel_id=1, source_target_pairs={{0,2},{2,4},{4,6},{6,8},{8,10},{10,12},{12,14},{14,0},{1,3},{3,5},... | collective-permute-start | bytes 786440 | tf_op jit(solution)/shard_map/ppermute | solution.py:220
  95.9 11.2 %collective-permute-start.29 = (f32[512,128]{1,0:T(8,128)S(1)}, f32[512,128]{1,0:T(8,128)S(1)}, u32[]{:S(2)}, u32[]{:S(2)}) collective-permute-start(f32[512,128]{1,0:T(8,128)S(1)} %add.47), channel_id=1, source_target_pairs={{0,14},{2,0},{4,2},{6,4},{8,6},{10,8},{12,10},{14,12},{1,15},{3,1}... | collective-permute-start | bytes 786440 | tf_op jit(solution)/shard_map/ppermute | solution.py:220
  99.2 10.9 %collective-permute-start.25 = (f32[512,128]{1,0:T(8,128)S(1)}, f32[512,128]{1,0:T(8,128)S(1)}, u32[]{:S(2)}, u32[]{:S(2)}) collective-permute-start(f32[512,128]{1,0:T(8,128)S(1)} %add.44), channel_id=1, source_target_pairs={{0,2},{2,4},{4,6},{6,8},{8,10},{10,12},{12,14},{14,0},{1,3},{3,5},... | collective-permute-start | bytes 786440 | tf_op jit(solution)/shard_map/ppermute | solution.py:220
  101.5 11.2 %collective-permute-start.21 = (f32[512,128]{1,0:T(8,128)S(1)}, f32[512,128]{1,0:T(8,128)S(1)}, u32[]{:S(2)}, u32[]{:S(2)}) collective-permute-start(f32[512,128]{1,0:T(8,128)S(1)} %add.41), channel_id=1, source_target_pairs={{0,14},{2,0},{4,2},{6,4},{8,6},{10,8},{12,10},{14,12},{1,15},{3,1}... | collective-permute-start | bytes 786440 | tf_op jit(solution)/shard_map/ppermute | solution.py:220
  104.8 10.9 %collective-permute-start.17 = (f32[512,128]{1,0:T(8,128)S(1)}, f32[512,128]{1,0:T(8,128)S(1)}, u32[]{:S(2)}, u32[]{:S(2)}) collective-permute-start(f32[512,128]{1,0:T(8,128)S(1)} %add.38), channel_id=1, source_target_pairs={{0,2},{2,4},{4,6},{6,8},{8,10},{10,12},{12,14},{14,0},{1,3},{3,5},... | collective-permute-start | bytes 786440 | tf_op jit(solution)/shard_map/ppermute | solution.py:220
  138.2 7.8 %collective-permute-start.30 = (f32[128,8,128]{2,1,0:T(8,128)S(1)}, f32[128,8,128]{2,1,0:T(8,128)S(1)}, u32[]{:S(2)}, u32[]{:S(2)}) collective-permute-start(f32[128,8,128]{2,1,0:T(8,128)S(1)} %all_to_all.5), channel_id=1, source_target_pairs={{0,1},{1,0},{2,3},{3,2},{4,5},{5,4},{6,7},{7,6},{8,9},{9,8},{10,11... | collective-permute-start | bytes 1572872 | tf_op jit(solution)/shard_map/ppermute | solution.py:324
